TPU v7x, 32 devices: a whole 2x2x4 slice. The times are simulated.
32 devices in a mesh: ri: 8 (over z, core), ao: 4 (over y, x).
Axes of the slice: x: 2, y: 2, z: 4, core: 2. Of those that a mesh axis runs over, the one named last changes fastest.
Arguments:
- three_center: bfloat16 [128, 512, 512], P('ri', 'ao'), as said below
- slab_tensor: bfloat16 [16, 512, 512], P('ri', 'ao'), as said below
- occ_green: bfloat16 [512, 512], P('ao'), as said below
- virt_green: bfloat16 [512, 512], P('ao'), as said below
- pattern: int32 [32, 32], replicated, may hold values from 0 to 1, as said below
- atom_sizes: int32 [32], replicated, may hold values from 6 to 16, as said below
Outputs:
- polar_slab: float32 [128, 16], P('ri')
Inputs may be any that keep to these rules, and one draw needn't show every extreme that they name: three_center is symmetric in its last two dimensions. slab_tensor is symmetric in its last two dimensions. `occ_green`: symmetric matrix. `virt_green`: symmetric matrix. `pattern`: symmetric 0/1 matrix with ones on the diagonal. `atom_sizes`: some atom block has all 16 functions live.
All inputs are finite; a program needn't handle non-finite values.
Results may differ from a plain program's by a relative error of at most 0.0041.
Values may be sent and summed in bfloat16 or wider, within the bound.
No kernel may reach another device: no remote copies, remote signals or barrier semaphores. Data moves between devices by JAX's collectives and lax.ppermute only.
A program may use at most 128 MiB of HBM per device.

v0:
```python
import jax
import jax.numpy as jnp
from jax import lax
from jax.sharding import PartitionSpec as P

ATOM_BS = 16


def live_functions(atom_sizes):
    atom_count = atom_sizes.shape[0]
    per_slot = jnp.broadcast_to(atom_sizes[:, None], (atom_count, ATOM_BS)).reshape(-1)
    slot_ids = jnp.broadcast_to(
        jnp.arange(ATOM_BS, dtype=jnp.int32)[None, :], (atom_count, ATOM_BS)
    ).reshape(-1)
    return (slot_ids < per_slot).astype(jnp.float32)


def expand_pattern(pattern_rows):
    row_atoms = pattern_rows.shape[0]
    col_atoms = pattern_rows.shape[1]
    grown = jnp.broadcast_to(
        pattern_rows[:, None, :, None], (row_atoms, ATOM_BS, col_atoms, ATOM_BS)
    )
    return grown.reshape(row_atoms * ATOM_BS, col_atoms * ATOM_BS).astype(jnp.float32)


def shards(three_center, slab_tensor, occ_green, virt_green, pattern, atom_sizes):
    own_rows = occ_green.shape[0]
    ao_total = occ_green.shape[1]
    ri_rows = three_center.shape[0]
    ao_index = lax.axis_index("ao")
    live_mask = live_functions(atom_sizes)
    live_rows = lax.dynamic_slice_in_dim(live_mask, ao_index * own_rows, own_rows, 0)
    pattern_rows = lax.dynamic_slice_in_dim(
        pattern, ao_index * (own_rows // ATOM_BS), own_rows // ATOM_BS, 0
    )
    screen = (expand_pattern(pattern_rows) * live_rows[:, None] * live_mask[None, :]).astype(
        jnp.bfloat16
    )
    masked = three_center * screen[None]
    slab_masked = slab_tensor * screen[None]
    occ_full, virt_full = (
        lax.all_gather(occ_green, "ao", axis=0, tiled=True),
        lax.all_gather(virt_green, "ao", axis=0, tiled=True),
    )
    half_product = jnp.einsum(
        "qsl,lm->qsm", slab_masked, occ_full, preferred_element_type=jnp.float32
    ).astype(jnp.bfloat16)
    weighted = jnp.einsum(
        "qsm,ns->qmn",
        lax.all_to_all(half_product, "ao", split_axis=2, concat_axis=1, tiled=True),
        virt_full,
        preferred_element_type=jnp.float32,
    ).astype(jnp.bfloat16)
    flattened = masked.reshape(ri_rows, own_rows * ao_total)
    shard_piece = lax.all_gather(weighted, "ri", axis=0, tiled=True)
    piece_rows = shard_piece.shape[0]
    columns_part = lax.dot_general(
        flattened,
        shard_piece.reshape(piece_rows, own_rows * ao_total),
        (((1,), (1,)), ((), ())),
        preferred_element_type=jnp.float32,
    )
    return lax.psum(columns_part, "ao") / ao_total


def solution(mesh):
    placed = (P("ri", "ao", None), P("ri", "ao", None), P("ao", None), P("ao", None), P(), P())
    return jax.shard_map(
        shards, mesh=mesh, in_specs=placed, out_specs=P("ri", None), check_vma=False
    )
```

profile of v0, /device:TPU:0, one launch (start us, length us, event | category | flops | bytes accessed | tf_op | source)
XLA Modules:
  0.0 92.7 jit_solution(1454622288221513894)
XLA Ops:
  6.5 0.7 fusion.12
  7.3 0.1 reshape.54
  7.3 11.9 %all_gather.9 = bf16[512,512]{1,0:T(8,128)(2,1)S(1)} all-gather(bf16[128,512]{1,0:T(8,128)(2,1)} %param.8), channel_id=1, replica_groups=mesh['ri'=8,'ao'=4] {'ao'}, dimensions={0}, use_global_device_ids=true | all-gather | bytes 655360 | tf_op jit(solution)/shard_map/all_gather | solution.py:43
  19.2 0.7 dynamic-slice_convert_fusion
  19.9 0.0 copy-start.1
  19.9 0.3 broadcast_in_dim.6
  20.2 0.0 copy-start.2
  20.2 1.6 %convert_element_type.35 = f32[128,512]{1,0:T(8,128)S(1)} reshape(f32[8,16,32,16]{3,2,1,0:T(8,128)S(1)} %broadcast_in_dim.6) | data formatting | bytes 524288 | tf_op jit(solution)/shard_map/convert_element_type | solution.py:24
  21.8 0.1 dynamic_slice.7
  21.9 0.1 multiply_convert_fusion
  22.0 0.0 copy-done.1
  22.0 0.3 convolution_convert_fusion.1
  22.3 0.0 copy-start
  22.3 0.9 copy.14
  23.2 3.4 %all-to-all-start = ((bf16[2,128,512]{1,0,2:T(2,128)(2,1)}), bf16[2,128,512]{1,0,2:T(2,128)(2,1)S(1)}, u32[]{:S(2)}, u32[]{:S(2)}) async-start(bf16[2,128,512]{1,0,2:T(2,128)(2,1)} %copy.14), calls=%async_computation | async-start | bytes 524288 | tf_op jit(solution)/shard_map/all_to_all | solution.py:51
  26.6 0.0 all-gather.2.cloned.1.call-start
  26.6 0.0 copy-done.2
  26.6 10.6 %all_gather.10 = bf16[512,512]{1,0:T(8,128)(2,1)S(1)} all-gather(bf16[128,512]{1,0:T(8,128)(2,1)S(1)} %copy-done.2), channel_id=1, replica_groups=mesh['ri'=8,'ao'=4] {'ao'}, dimensions={0}, use_global_device_ids=true | all-gather | bytes 655360 | tf_op jit(solution)/shard_map/all_gather | solution.py:44
  37.3 0.0 all-to-all-done
  37.3 0.2 copy.16
  37.5 1.1 %convolution_convert_fusion = bf16[2,128,512]{2,1,0:T(8,128)(2,1)} fusion(bf16[2,512,128]{2,1,0:T(8,128)(2,1)S(1)} %bitcast.16, bf16[512,512]{1,0:T(8,128)(2,1)S(1)} %all_gather.10), kind=kOutput, calls=%fused_computation.3 | convolution fusion | flops 134348800 | bytes 1048576 | tf_op jit(solution)/shard_map/qsm,ns->qmn/dot_general | solution.py:49
  38.5 0.0 all-gather.2.cloned.1.call-update
  38.6 0.0 copy-done
  38.6 1.5 %broadcast_multiply_fusion = bf16[16,128,512]{2,1,0:T(8,128)(2,1)} fusion(bf16[16,128,512]{2,1,0:T(8,128)(2,1)S(1)} %copy-done, bf16[128,512]{1,0:T(8,128)(2,1)S(1)} %multiply_convert_fusion), kind=kLoop, calls=%fused_computation.6 | loop fusion | flops 1048576 | bytes 4325376 | tf_op jit(solution)/shard_map/mul | solution.py:40
  40.0 28.6 %all-gather.2.cloned.1.call-done = bf16[16,128,512]{2,1,0:T(8,128)(2,1)} async-done(((bf16[2,128,512]{2,1,0:T(8,128)(2,1)}), bf16[16,128,512]{2,1,0:T(8,128)(2,1)}) %all-gather.2.cloned.1.call-update) | async-done | bytes 2097168 | tf_op jit(solution)/shard_map/all_gather | solution.py:56
  68.7 6.6 %fusion.3 = f32[16,16]{1,0:T(8,128)S(1)} fusion(bf16[16,128,512]{2,1,0:T(8,128)(2,1)} %all-gather.2.cloned.1.call-done, bf16[16,128,512]{2,1,0:T(8,128)(2,1)} %broadcast_multiply_fusion), kind=kOutput, calls=%fused_computation.5 | convolution fusion | flops 33554432 | bytes 4195328 | tf_op jit(solution)/shard_map/dot_general | solution.py:58
  75.3 10.0 %psum.7 = f32[16,16]{1,0:T(8,128)S(1)} all-reduce(f32[16,16]{1,0:T(8,128)S(1)} %fusion.3), channel_id=1, replica_groups=mesh['ri'=8,'ao'=4] {'ao'}, use_global_device_ids=true, to_apply=%region_0.0 | all-reduce | flops 256 | bytes 2048 | tf_op jit(solution)/shard_map/psum | solution.py:64
  85.3 0.6 broadcast_multiply_fusion.1
  (1 shorter events, 0.0 us)
Async XLA Ops:
  19.9 2.1 %copy-start.1 = (bf16[2,128,512]{2,1,0:T(8,128)(2,1)S(1)}, bf16[2,128,512]{2,1,0:T(8,128)(2,1)}, u32[]{:S(2)}) copy-start(bf16[2,128,512]{2,1,0:T(8,128)(2,1)} %param.7) | copy-start | bytes 786436
  20.2 6.4 %copy-start.2 = (bf16[128,512]{1,0:T(8,128)(2,1)S(1)}, bf16[128,512]{1,0:T(8,128)(2,1)}, u32[]{:S(2)}) copy-start(bf16[128,512]{1,0:T(8,128)(2,1)} %param.9) | copy-start | bytes 393220
  22.3 16.3 %copy-start = (bf16[16,128,512]{2,1,0:T(8,128)(2,1)S(1)}, bf16[16,128,512]{2,1,0:T(8,128)(2,1)}, u32[]{:S(2)}) copy-start(bf16[16,128,512]{2,1,0:T(8,128)(2,1)} %param.6) | copy-start | bytes 6291460
  23.2 14.1 %all-to-all-start = ((bf16[2,128,512]{1,0,2:T(2,128)(2,1)}), bf16[2,128,512]{1,0,2:T(2,128)(2,1)S(1)}, u32[]{:S(2)}, u32[]{:S(2)}) async-start(bf16[2,128,512]{1,0,2:T(2,128)(2,1)} %copy.14), calls=%async_computation | async-start | bytes 524288 | tf_op jit(solution)/shard_map/all_to_all | solution.py:51
  26.6 42.1 %all-gather.2.cloned.1.call-start = ((), (), s32[]{:S(2)}) async-start(), calls=%async_computation.1 | async-start | bytes 2359296 | tf_op jit(solution)/shard_map/all_gather | solution.py:56
Sparse Core Ops, SparseCore 0:
  38.7 29.9 all-gather.1
where the time goes:
time: 93.1 us; the launch traced here: 92.7 us
  blocking collectives  32.5 us (35%)
  waiting for transfers between devices  28.7 us (31%)
  between operations  13.5 us (15%)
  matrix products  7.99 us (9%)
  other arithmetic  3.57 us (4%)
  starting transfers between devices  3.45 us (4%)
  local copies, waits for them, and re-layouts  3.13 us (3%)
    all_gather x1, waiting for transfers between devices, shards(): shard_piece = lax.all_gather(weighted, 'ri', axis=0, tiled=True)  28.6 us
    all_gather x1, blocking collectives, shards(): lax.all_gather(occ_green, 'ao', axis=0, tiled=True)  11.9 us
    all_gather x1, blocking collectives, shards(): lax.all_gather(virt_green, 'ao', axis=0, tiled=True)  10.6 us
    psum x1, blocking collectives, shards(): return lax.psum(columns_part, 'ao') / ao_total  9.98 us
    dot_general x1, matrix products, shards(): lax.dot_general(flattened, shard_piece.reshape(piece_rows, own_rows * ao_...  6.64 us
    all_to_all x1, starting transfers between devices, shards(): lax.all_to_all(half_product, 'ao', split_axis=2, concat_axis=1, tiled=True)  3.4 us
  transfers between devices with their start and end apart: 2, of which 1 were waited for; matrix products, arithmetic and copies ran while one was open for 2% of the time, Pallas kernels for 0%

commit v1 on v0

v1 whole, which is shorter than its diff:
```python
import jax
import jax.numpy as jnp
from jax import lax
from jax.experimental import pallas as pl
from jax.experimental.pallas import tpu as pltpu
from jax.sharding import PartitionSpec as P

ATOM_BS = 16
TILE = 16


def top_bit(k):
    return k.bit_length() - 1


def which(a, k):
    return lax.shift_right_logical(a, jnp.int32(top_bit(k))) & 1


def tri_masks(block):
    row = lax.broadcasted_iota(jnp.int32, (block, block), 0)
    col = lax.broadcasted_iota(jnp.int32, (block, block), 1)
    return row > col, row == col


def fold_diagonal(first, second, below, on):
    folded = jnp.where(below | on, first, second)
    diagonal = jnp.sum(jnp.where(on, second, 0.0), axis=0, keepdims=True)
    return folded, diagonal


def block_at(ref, index, block):
    return ref[:, pl.ds(pl.multiple_of(index * block, block), block)]


def prep_kernel(sizes_ref, pattern_ref, slab_ref, occ_ref, virt_ref, pay_ref, screen_ref, mask_ref):
    block = occ_ref.shape[0]
    total = occ_ref.shape[1]
    ao = total // block
    atoms = pattern_ref.shape[0]
    f32, bf16 = jnp.float32, jnp.bfloat16
    a = lax.axis_index("ao")
    row_atom = lax.shift_right_logical(
        lax.broadcasted_iota(jnp.int32, (block, atoms), 0), jnp.int32(4)
    ) + a * (block // ATOM_BS)
    pick_row = row_atom == lax.broadcasted_iota(jnp.int32, (block, atoms), 1)
    col_atom = lax.shift_right_logical(
        lax.broadcasted_iota(jnp.int32, (atoms, total), 1), jnp.int32(4)
    )
    pick_col = (col_atom == lax.broadcasted_iota(jnp.int32, (atoms, total), 0)).astype(f32).astype(bf16)
    sizes = sizes_ref[...].astype(f32)
    size_row = jnp.sum(jnp.where(pick_row, jnp.broadcast_to(sizes, (block, atoms)), 0.0), axis=1, keepdims=True)
    size_col = jnp.dot(
        jnp.broadcast_to(sizes, (8, atoms)).astype(bf16), pick_col, preferred_element_type=f32
    )[0:1]
    rows = jnp.dot(
        pick_row.astype(f32).astype(bf16), pattern_ref[...].astype(f32).astype(bf16),
        preferred_element_type=f32,
    ).astype(bf16)
    kept = jnp.dot(rows, pick_col, preferred_element_type=f32)
    slot_row = (lax.broadcasted_iota(jnp.int32, (block, total), 0) & (ATOM_BS - 1)).astype(f32)
    slot_col = (lax.broadcasted_iota(jnp.int32, (block, total), 1) & (ATOM_BS - 1)).astype(f32)
    live = (slot_row < size_row) & (slot_col < size_col)
    mask_ref[...] = jnp.where(live, kept, 0.0).astype(bf16)
    below, on = tri_masks(block)
    half = ao * block + TILE
    for k in range(1, ao):
        screen = block_at(mask_ref, a ^ k, block)
        screen_ref[:, k * block : (k + 1) * block] = screen
        matrix = which(a, k)
        start = (k - 1) * block
        cols = pl.ds(pl.multiple_of((a ^ k) * block, block), block)
        pay_ref[start : start + block, :] = slab_ref[matrix, :, cols] * screen
        pay_ref[half + start : half + start + block, :] = jnp.where(
            matrix == 0, occ_ref[:, cols], virt_ref[:, cols]
        )
    screen = block_at(mask_ref, a, block)
    screen_ref[:, 0:block] = screen
    own = pl.ds(pl.multiple_of(a * block, block), block)
    start = (ao - 1) * block
    pairs = (
        (start, (slab_ref[0, :, own] * screen).astype(f32), (slab_ref[1, :, own] * screen).astype(f32)),
        (half + start, occ_ref[:, own].astype(f32), virt_ref[:, own].astype(f32)),
    )
    for at, first, second in pairs:
        folded, diagonal = fold_diagonal(first, second, below, on)
        pay_ref[at : at + block, :] = folded.astype(bf16)
        pay_ref[at + block : at + block + TILE, :] = jnp.broadcast_to(diagonal, (TILE, block)).astype(bf16)


def unfold(pays, base, a, ao, block, put):
    below, on = tri_masks(block)
    for m in range(ao):
        for j in range(m + 1, ao):
            k = m ^ j
            at = base + (k - 1) * block
            here = pays[m][at : at + block, :]
            there = pays[j][at : at + block, :]
            here_t = here.T
            there_t = there.T
            lower = which(a ^ m, k) == 0
            put(0, m, j, jnp.where(lower, here, there_t))
            put(0, j, m, jnp.where(lower, here_t, there))
            put(1, m, j, jnp.where(lower, there_t, here))
            put(1, j, m, jnp.where(lower, there, here_t))
        at = base + (ao - 1) * block
        folded = pays[m][at : at + block, :].astype(jnp.float32)
        folded_t = folded.T
        diagonal = pays[m][at + block : at + block + TILE, :].astype(jnp.float32)[0:1]
        put(0, m, m, jnp.where(below | on, folded, folded_t).astype(jnp.bfloat16))
        put(
            1, m, m,
            jnp.where(below, folded_t, jnp.where(on, jnp.broadcast_to(diagonal, (block, block)), folded)).astype(
                jnp.bfloat16
            ),
        )


def transform_kernel(ao, block, *refs):
    pays = refs[:ao]
    screen_ref, out_ref, slab_ref, green_ref, left_ref = refs[ao:]
    total = ao * block
    a = lax.axis_index("ao")
    half = total + TILE
    f32, bf16 = jnp.float32, jnp.bfloat16

    def put_slab(matrix, row, col, value):
        slab_ref[matrix, row * block : (row + 1) * block, col * block : (col + 1) * block] = value

    def put_green(matrix, row, col, value):
        at = (total if matrix == 0 else 0) + col * block
        green_ref[row, :, at : at + block] = value

    unfold(pays, half, a, ao, block, put_green)
    unfold(pays, 0, a, ao, block, put_slab)
    both = jnp.concatenate([green_ref[0, :, total:], green_ref[0, :, :total]], axis=0)
    for q in range(2):
        left = jnp.dot(both, slab_ref[q], preferred_element_type=f32).astype(bf16)
        left_ref[q, :, :total] = left[:block]
        left_ref[q, :, total:] = left[block:]
    last = (((1,), (1,)), ((), ()))
    for k in range(1, ao):
        sums = lax.dot_general(left_ref[which(a, k)], green_ref[k], last, preferred_element_type=f32)
        screen = screen_ref[:, k * block : (k + 1) * block].astype(f32)
        out_ref[(k - 1) * block : k * block, :] = (sums * screen).astype(bf16)
    below, on = tri_masks(block)
    weight = jnp.where(on, 0.5, 1.0) * screen_ref[:, 0:block].astype(f32)
    first, second = (
        lax.dot_general(left_ref[q], green_ref[0], last, preferred_element_type=f32) * weight for q in range(2)
    )
    folded, diagonal = fold_diagonal(first, second, below, on)
    at = (ao - 1) * block
    out_ref[at : at + block, :] = folded.astype(bf16)
    out_ref[at + block : at + block + TILE, :] = jnp.broadcast_to(diagonal, (TILE, block)).astype(bf16)


def contract_kernel(count, ao, block, *refs):
    pays = refs[:count]
    tensor_ref, out_ref = refs[count:]
    ri_rows = tensor_ref.shape[0]
    a = lax.axis_index("ao")
    r = lax.axis_index("ri")
    f32, bf16 = jnp.float32, jnp.bfloat16
    groups = block // TILE
    last = (((1,), (1,)), ((), ()))

    def spread(values, rows_of):
        return jnp.concatenate(
            [
                jnp.concatenate([rows_of(v, slice(g * TILE, (g + 1) * TILE)) for v in values], axis=0)
                for g in range(groups)
            ],
            axis=1,
        )

    def tensor_block(k):
        cols = pl.ds(pl.multiple_of((a ^ k) * block, block), block)
        return spread(range(ri_rows), lambda p, rows: tensor_ref[p, rows, cols])

    below, on = tri_masks(block)
    at = (ao - 1) * block
    firsts, seconds = [], []
    for pay in pays:
        folded = pay[at : at + block, :].astype(f32)
        diagonal = pay[at + block : at + block + TILE, :].astype(f32)[0:1]
        firsts.append(jnp.where(below | on, folded, 0.0).astype(bf16))
        seconds.append(
            jnp.where(below, 0.0, jnp.where(on, jnp.broadcast_to(diagonal, (block, block)), folded)).astype(bf16)
        )
    sums = lax.dot_general(
        spread(firsts + seconds, lambda v, rows: v[rows]), tensor_block(0), last, preferred_element_type=f32
    )
    half = count * TILE
    sums = [sums[:half], sums[half:]]
    for k in range(1, ao):
        start = (k - 1) * block
        part = lax.dot_general(
            spread(pays, lambda pay, rows: pay[start + rows.start : start + rows.stop, :]),
            tensor_block(k),
            last,
            preferred_element_type=f32,
        )
        to_first = which(a, k) == 0
        sums[0] = sums[0] + jnp.where(to_first, part, 0.0)
        sums[1] = sums[1] + jnp.where(to_first, 0.0, part)
    width = ri_rows * TILE
    row = lax.broadcasted_iota(jnp.int32, (half, width), 0)
    col = lax.broadcasted_iota(jnp.int32, (half, width), 1)
    same = (row & (TILE - 1)) == (col & (TILE - 1))
    traces = jnp.concatenate(
        [jnp.where(same, s, 0.0).reshape(count, TILE, width).sum(axis=1) for s in sums], axis=0
    )
    pick = (
        lax.shift_right_logical(lax.broadcasted_iota(jnp.int32, (ri_rows, width), 1), jnp.int32(4))
        == lax.broadcasted_iota(jnp.int32, (ri_rows, width), 0)
    ).astype(f32)
    by_source = lax.dot_general(
        pick, traces, last, precision=lax.Precision.HIGHEST, preferred_element_type=f32
    )
    source = lax.broadcasted_iota(jnp.int32, (2 * count, 2 * count), 0)
    target = lax.broadcasted_iota(jnp.int32, (2 * count, 2 * count), 1)
    place = ((jnp.where(source < count, source, source - count) ^ r) * 2 + (source >= count).astype(jnp.int32)) == target
    ordered = jnp.dot(
        by_source, place.astype(f32), precision=lax.Precision.HIGHEST, preferred_element_type=f32
    )
    out_ref[...] = ordered * (1.0 / (ao * block))


def exchange(value, axis, size, k):
    return lax.ppermute(value, axis, [(i, i ^ k) for i in range(size)])


def shards(ri, ao, three_center, slab_tensor, occ_green, virt_green, pattern, atom_sizes):
    block = occ_green.shape[0]
    total = occ_green.shape[1]
    ri_rows = three_center.shape[0]
    atoms = pattern.shape[0]
    half = total + TILE
    bf16 = jnp.bfloat16
    vmem = pl.BlockSpec(memory_space=pltpu.VMEM)
    pay, screen = pl.pallas_call(
        prep_kernel,
        out_shape=(
            jax.ShapeDtypeStruct((2 * half, block), bf16),
            jax.ShapeDtypeStruct((block, total), bf16),
        ),
        in_specs=[vmem] * 5,
        out_specs=(vmem, vmem),
        scratch_shapes=[pltpu.VMEM((block, total), bf16)],
        name="prep",
    )(atom_sizes.reshape(1, atoms), pattern, slab_tensor, occ_green, virt_green)
    pays = [pay] + [exchange(pay, "ao", ao, k) for k in range(1, ao)]
    weighted = pl.pallas_call(
        lambda *refs: transform_kernel(ao, block, *refs),
        out_shape=jax.ShapeDtypeStruct((half, block), bf16),
        in_specs=[vmem] * (ao + 1),
        out_specs=vmem,
        scratch_shapes=[
            pltpu.VMEM((2, total, total), bf16),
            pltpu.VMEM((ao, block, 2 * total), bf16),
            pltpu.VMEM((2, block, 2 * total), bf16),
        ],
        name="transform",
    )(*pays, screen)
    sources = [weighted]
    for k in range(2, ri, 2):
        sources.append(exchange(weighted, "ri", ri, k))
    arrived = []
    for value in sources:
        arrived.append(value)
        arrived.append(exchange(value, "ri", ri, 1))
    part = pl.pallas_call(
        lambda *refs: contract_kernel(ri, ao, block, *refs),
        out_shape=jax.ShapeDtypeStruct((ri_rows, 2 * ri), jnp.float32),
        in_specs=[vmem] * (ri + 1),
        out_specs=vmem,
        name="contract",
    )(*arrived, three_center)
    parts = [part] + [exchange(part, "ao", ao, k) for k in range(1, ao)]
    while len(parts) > 1:
        parts = [parts[i] + parts[i + 1] for i in range(0, len(parts), 2)]
    return parts[0]


def solution(mesh):
    placed = (P("ri", "ao", None), P("ri", "ao", None), P("ao", None), P("ao", None), P(), P())
    ri, ao = mesh.shape["ri"], mesh.shape["ao"]

    def body(*args):
        return shards(ri, ao, *args)

    return jax.shard_map(body, mesh=mesh, in_specs=placed, out_specs=P("ri", None), check_vma=False)
```

time: 93.1 us -> 52.9 us (0.57)
  blocking collectives: 32.5 us -> 0 us
  between operations: 13.5 us -> 0.06 us
  starting transfers between devices: 3.45 us -> 12.9 us
  Pallas kernels: 0 us -> 9.07 us
  matrix products: 7.99 us -> 0 us
  other arithmetic: 3.57 us -> 1.3 us
  local copies, waits for them, and re-layouts: 3.13 us -> 1.8 us
  waiting for transfers between devices: 28.7 us -> 27.6 us
    all_gather x1 -> x0, waiting for transfers between devices: 28.6 us -> none  [shards(): shard_piece = lax.all_gather(weighted, 'ri', axis=0, tiled=True)]
    ppermute x0 -> x13, waiting for transfers between devices: none -> 27.6 us  [exchange(): return lax.ppermute(value, axis, [(i, i ^ k) for i in range(size)])]
    all_gather x2 -> x0, blocking collectives: 22.5 us -> none  [the longest x1 11.9 us: shards(): lax.all_gather(occ_green, 'ao', axis=0, tiled=True)]
    ppermute x0 -> x13, starting transfers between devices: none -> 12.9 us  [exchange(): return lax.ppermute(value, axis, [(i, i ^ k) for i in range(size)])]
    psum x1 -> x0, blocking collectives: 9.98 us -> none  [shards(): return lax.psum(columns_part, 'ao') / ao_total]
    pallas_call x0 -> x3, Pallas kernels: none -> 9.07 us  [the longest x1 3.77 us: shards(): pl.pallas_call(lambda *refs: contract_kernel(ri, ao, block, *refs), out_s...]
    dot_general x3 -> x0, matrix products: 7.99 us -> none  [the longest x1 6.64 us: shards(): lax.dot_general(flattened, shard_piece.reshape(piece_rows, own_rows * ao_...]
    all_to_all x1 -> x0, starting transfers between devices: 3.4 us -> none  [shards(): lax.all_to_all(half_product, 'ao', split_axis=2, concat_axis=1, tiled=True)]
  transfers between devices with their start and end apart: 2 -> 13, of which waited for: 1 -> 10; matrix products, arithmetic and copies ran while one was open for 2% -> 0% of each run, Pallas kernels for 0% -> 0%
where the time goes in v1:
time: 52.9 us; the launch traced here: 52.7 us
  waiting for transfers between devices  27.6 us (52%)
  starting transfers between devices  12.9 us (24%)
  Pallas kernels  9.07 us (17%)
  local copies, waits for them, and re-layouts  1.8 us (3%)
  other arithmetic  1.3 us (2%)
    ppermute x13, waiting for transfers between devices, exchange(): return lax.ppermute(value, axis, [(i, i ^ k) for i in range(size)])  27.6 us
    ppermute x13, starting transfers between devices, exchange(): return lax.ppermute(value, axis, [(i, i ^ k) for i in range(size)])  12.9 us
    pallas_call x1, Pallas kernels, shards(): pl.pallas_call(lambda *refs: contract_kernel(ri, ao, block, *refs), out_s...  3.77 us
    pallas_call x1, Pallas kernels, shards(): pl.pallas_call(lambda *refs: transform_kernel(ao, block, *refs), out_shap...  3.11 us
    pallas_call x1, Pallas kernels, shards(): pl.pallas_call(prep_kernel, out_shape=(jax.ShapeDtypeStruct((2 * half, bl...  2.19 us
    unnamed x20, local copies, waits for them, and re-layouts  1.8 us
    add x1, other arithmetic, shards(): parts = [parts[i] + parts[i + 1] for i in range(0, len(parts), 2)]  1.3 us
  transfers between devices with their start and end apart: 13, of which 10 were waited for; matrix products, arithmetic and copies ran while one was open for 0% of the time, Pallas kernels for 0%

profile of v1, /device:TPU:0, one launch (start us, length us, event | category | flops | bytes accessed | tf_op | source)
XLA Modules:
  0.0 52.7 jit_solution(2197383940498920023)
XLA Ops:
  0.0 2.2 %prep.1 = (bf16[1056,128]{1,0:T(8,128)(2,1)}, bf16[128,512]{1,0:T(8,128)(2,1)}) custom-call(s32[1,32]{1,0:T(1,128)} %bitcast.1, s32[32,32]{1,0:T(8,128)} %pattern_ref.1, bf16[2,128,512]{2,1,0:T(8,128)(2,1)} %slab_ref.1, bf16[128,512]{1,0:T(8,128)(2,1)} %occ_ref.1, bf16[128,512]{1,0:T(8,128)(2,1)} %virt_ref.1), custom_call_target="tpu_custom_call" | custom-call | tf_op jit(solution)/shard_map/prep/pallas_call | solution.py:241
  2.2 3.9 %collective-permute-start.2 = (bf16[1056,128]{1,0:T(8,128)(2,1)}, bf16[1056,128]{1,0:T(8,128)(2,1)S(1)}, u32[]{:S(2)}, u32[]{:S(2)}) collective-permute-start(bf16[1056,128]{1,0:T(8,128)(2,1)} %get-tuple-element.7.refs_0_), channel_id=1, source_target_pairs={{0,3},{1,2},{2,1},{3,0},{4,7},{5,6},{6,5},{7,4},{8,11},{9,10},{10,... | collective-permute-start | bytes 811016 | tf_op jit(solution)/shard_map/ppermute | solution.py:230
  6.1 0.5 collective-permute-start.1
  6.6 0.1 collective-permute-start
  6.7 7.0 %collective-permute-done.2.refs_3_ = bf16[1056,128]{1,0:T(8,128)(2,1)S(1)} collective-permute-done((bf16[1056,128]{1,0:T(8,128)(2,1)}, bf16[1056,128]{1,0:T(8,128)(2,1)S(1)}, u32[]{:S(2)}, u32[]{:S(2)}) %collective-permute-start.2) | collective-permute-done | bytes 270368 | tf_op jit(solution)/shard_map/ppermute | solution.py:230
  13.7 0.0 copy-start
  13.7 4.9 %collective-permute-done.1.refs_2_ = bf16[1056,128]{1,0:T(8,128)(2,1)S(1)} collective-permute-done((bf16[1056,128]{1,0:T(8,128)(2,1)}, bf16[1056,128]{1,0:T(8,128)(2,1)S(1)}, u32[]{:S(2)}, u32[]{:S(2)}) %collective-permute-start.1) | collective-permute-done | bytes 270368 | tf_op jit(solution)/shard_map/ppermute | solution.py:230
  18.6 0.0 copy-start.1
  18.6 0.3 collective-permute-done.refs_1_
  18.9 0.0 copy-start.2
  18.9 0.0 copy-done
  18.9 0.4 copy-done.1
  19.3 0.3 copy-done.2
  19.6 3.1 %transform.1.refs_0_ = bf16[528,128]{1,0:T(8,128)(2,1)} custom-call(bf16[1056,128]{1,0:T(8,128)(2,1)} %get-tuple-element.7.refs_0_, bf16[1056,128]{1,0:T(8,128)(2,1)} %copy-done.2, bf16[1056,128]{1,0:T(8,128)(2,1)} %copy-done.1, bf16[1056,128]{1,0:T(8,128)(2,1)} %copy-done, bf16[128,512]{1,0:T(8,128)(2,1)} %get-tuple-element.8.refs_4_), custom_call_target="tpu_custom_call" | custom-call | tf_op jit(solution)/shard_map/transform/pallas_call | solution.py:253
  22.7 3.6 %collective-permute-start.8 = (bf16[528,128]{1,0:T(8,128)(2,1)}, bf16[528,128]{1,0:T(8,128)(2,1)S(1)}, u32[]{:S(2)}, u32[]{:S(2)}) collective-permute-start(bf16[528,128]{1,0:T(8,128)(2,1)} %transform.1.refs_0_), channel_id=1, source_target_pairs={{0,24},{4,28},{8,16},{12,20},{16,8},{20,12},{24,0},{28,4},{1,25},{... | collective-permute-start | bytes 405512 | tf_op jit(solution)/shard_map/ppermute | solution.py:230
  26.3 0.0 collective-permute-start.6
  26.3 0.8 %collective-permute-start.4 = (bf16[528,128]{1,0:T(8,128)(2,1)}, bf16[528,128]{1,0:T(8,128)(2,1)S(1)}, u32[]{:S(2)}, u32[]{:S(2)}) collective-permute-start(bf16[528,128]{1,0:T(8,128)(2,1)} %transform.1.refs_0_), channel_id=1, source_target_pairs={{0,8},{4,12},{8,0},{12,4},{16,24},{20,28},{24,16},{28,20},{1,9},{5... | collective-permute-start | bytes 405512 | tf_op jit(solution)/shard_map/ppermute | solution.py:230
  27.1 0.0 collective-permute-start.3
  27.1 4.2 %collective-permute-done.8.refs_6_ = bf16[528,128]{1,0:T(8,128)(2,1)S(1)} collective-permute-done((bf16[528,128]{1,0:T(8,128)(2,1)}, bf16[528,128]{1,0:T(8,128)(2,1)S(1)}, u32[]{:S(2)}, u32[]{:S(2)}) %collective-permute-start.8) | collective-permute-done | bytes 135200 | tf_op jit(solution)/shard_map/ppermute | solution.py:230
  31.3 0.0 copy-start.3
  31.3 0.0 collective-permute-start.9
  31.3 6.9 %collective-permute-done.6.refs_4_ = bf16[528,128]{1,0:T(8,128)(2,1)S(1)} collective-permute-done((bf16[528,128]{1,0:T(8,128)(2,1)}, bf16[528,128]{1,0:T(8,128)(2,1)S(1)}, u32[]{:S(2)}, u32[]{:S(2)}) %collective-permute-start.6) | collective-permute-done | bytes 135200 | tf_op jit(solution)/shard_map/ppermute | solution.py:230
  38.1 0.0 copy-start.4
  38.1 0.0 collective-permute-start.7
  38.1 0.0 collective-permute-done.4.refs_2_
  38.2 0.0 copy-start.5
  38.2 0.5 collective-permute-start.5
  38.7 0.0 collective-permute-done.3.refs_1_
  38.7 0.0 copy-start.6
  38.7 0.0 collective-permute-done.9.refs_7_
  38.7 0.0 copy-start.7
  38.7 0.8 %collective-permute-done.7.refs_5_ = bf16[528,128]{1,0:T(8,128)(2,1)S(1)} collective-permute-done((bf16[528,128]{1,0:T(8,128)(2,1)S(1)}, bf16[528,128]{1,0:T(8,128)(2,1)S(1)}, u32[]{:S(2)}, u32[]{:S(2)}) %collective-permute-start.7) | collective-permute-done | bytes 135200 | tf_op jit(solution)/shard_map/ppermute | solution.py:230
  39.5 0.2 collective-permute-done.5.refs_3_
  39.7 0.0 copy-done.3
  39.7 0.0 copy-done.4
  39.7 0.0 copy-done.5
  39.7 0.0 copy-done.6
  39.7 0.0 copy-done.7
  39.7 0.4 copy-done.8
  40.2 0.6 %copy-done.9 = bf16[528,128]{1,0:T(8,128)(2,1)} copy-done((bf16[528,128]{1,0:T(8,128)(2,1)}, bf16[528,128]{1,0:T(8,128)(2,1)S(1)}, u32[]{:S(2)}) %copy-start.9) | copy-done | bytes 135192
  40.8 3.8 %contract.1 = f32[16,16]{1,0:T(8,128)} custom-call(bf16[528,128]{1,0:T(8,128)(2,1)} %transform.1.refs_0_, bf16[528,128]{1,0:T(8,128)(2,1)} %copy-done.6, bf16[528,128]{1,0:T(8,128)(2,1)} %copy-done.5, bf16[528,128]{1,0:T(8,128)(2,1)} %copy-done.9, bf16[528,128]{1,0:T(8,128)(2,1)} %copy-done.4, bf16[528,128]{1,0:T(8,128)(2,1)} %copy-done.8, ...), custom_call_target="tpu_custom_call" | custom-call | tf_op jit(solution)/shard_map/contract/pallas_call | solution.py:272
  44.6 1.0 %collective-permute-start.12 = (f32[16,16]{1,0:T(8,128)}, f32[16,16]{1,0:T(8,128)S(1)}, u32[]{:S(2)}, u32[]{:S(2)}) collective-permute-start(f32[16,16]{1,0:T(8,128)} %contract.1), channel_id=1, source_target_pairs={{0,3},{1,2},{2,1},{3,0},{4,7},{5,6},{6,5},{7,4},{8,11},{9,10},{10,... | collective-permute-start | bytes 3080 | tf_op jit(solution)/shard_map/ppermute | solution.py:230
  45.6 1.9 %collective-permute-start.11 = (f32[16,16]{1,0:T(8,128)}, f32[16,16]{1,0:T(8,128)S(1)}, u32[]{:S(2)}, u32[]{:S(2)}) collective-permute-start(f32[16,16]{1,0:T(8,128)} %contract.1), channel_id=1, source_target_pairs={{0,2},{1,3},{2,0},{3,1},{4,6},{5,7},{6,4},{7,5},{8,10},{9,11},{10,... | collective-permute-start | bytes 3080 | tf_op jit(solution)/shard_map/ppermute | solution.py:230
  47.5 0.5 %collective-permute-start.10 = (f32[16,16]{1,0:T(8,128)}, f32[16,16]{1,0:T(8,128)S(1)}, u32[]{:S(2)}, u32[]{:S(2)}) collective-permute-start(f32[16,16]{1,0:T(8,128)} %contract.1), channel_id=1, source_target_pairs={{0,1},{1,0},{2,3},{3,2},{4,5},{5,4},{6,7},{7,6},{8,9},{9,8},{10,11... | collective-permute-start | bytes 3080 | tf_op jit(solution)/shard_map/ppermute | solution.py:230
  48.1 1.3 %collective-permute-done.12 = f32[16,16]{1,0:T(8,128)S(1)} collective-permute-done((f32[16,16]{1,0:T(8,128)}, f32[16,16]{1,0:T(8,128)S(1)}, u32[]{:S(2)}, u32[]{:S(2)}) %collective-permute-start.12) | collective-permute-done | bytes 1056 | tf_op jit(solution)/shard_map/ppermute | solution.py:230
  49.3 0.1 collective-permute-done.11
  49.5 1.9 %collective-permute-done.10 = f32[16,16]{1,0:T(8,128)S(1)} collective-permute-done((f32[16,16]{1,0:T(8,128)}, f32[16,16]{1,0:T(8,128)S(1)}, u32[]{:S(2)}, u32[]{:S(2)}) %collective-permute-start.10) | collective-permute-done | bytes 1056 | tf_op jit(solution)/shard_map/ppermute | solution.py:230
  51.4 1.3 %add_add_fusion = f32[16,16]{1,0:T(8,128)} fusion(f32[16,16]{1,0:T(8,128)S(1)} %collective-permute-done.11, f32[16,16]{1,0:T(8,128)S(1)} %collective-permute-done.12, f32[16,16]{1,0:T(8,128)} %contract.1, f32[16,16]{1,0:T(8,128)S(1)} %collective-permute-done.10), kind=kLoop, calls=%fused_computation | loop fusion | flops 768 | bytes 5120 | tf_op jit(solution)/shard_map/add | solution.py:281
  (2 shorter events, 0.0 us)
Async XLA Ops:
  2.2 11.5 %collective-permute-start.2 = (bf16[1056,128]{1,0:T(8,128)(2,1)}, bf16[1056,128]{1,0:T(8,128)(2,1)S(1)}, u32[]{:S(2)}, u32[]{:S(2)}) collective-permute-start(bf16[1056,128]{1,0:T(8,128)(2,1)} %get-tuple-element.7.refs_0_), channel_id=1, source_target_pairs={{0,3},{1,2},{2,1},{3,0},{4,7},{5,6},{6,5},{7,4},{8,11},{9,10},{10,... | collective-permute-start | bytes 811016 | tf_op jit(solution)/shard_map/ppermute | solution.py:230
  6.1 12.5 %collective-permute-start.1 = (bf16[1056,128]{1,0:T(8,128)(2,1)}, bf16[1056,128]{1,0:T(8,128)(2,1)S(1)}, u32[]{:S(2)}, u32[]{:S(2)}) collective-permute-start(bf16[1056,128]{1,0:T(8,128)(2,1)} %get-tuple-element.7.refs_0_), channel_id=1, source_target_pairs={{0,2},{1,3},{2,0},{3,1},{4,6},{5,7},{6,4},{7,5},{8,10},{9,11},{10,... | collective-permute-start | bytes 811016 | tf_op jit(solution)/shard_map/ppermute | solution.py:230
  6.6 12.3 %collective-permute-start = (bf16[1056,128]{1,0:T(8,128)(2,1)}, bf16[1056,128]{1,0:T(8,128)(2,1)S(1)}, u32[]{:S(2)}, u32[]{:S(2)}) collective-permute-start(bf16[1056,128]{1,0:T(8,128)(2,1)} %get-tuple-element.7.refs_0_), channel_id=1, source_target_pairs={{0,1},{1,0},{2,3},{3,2},{4,5},{5,4},{6,7},{7,6},{8,9},{9,8},{10,11... | collective-permute-start | bytes 811016 | tf_op jit(solution)/shard_map/ppermute | solution.py:230
  13.7 5.2 %copy-start = (bf16[1056,128]{1,0:T(8,128)(2,1)}, bf16[1056,128]{1,0:T(8,128)(2,1)S(1)}, u32[]{:S(2)}) copy-start(bf16[1056,128]{1,0:T(8,128)(2,1)S(1)} %collective-permute-done.2.refs_3_) | copy-start | bytes 811012
  18.6 0.7 %copy-start.1 = (bf16[1056,128]{1,0:T(8,128)(2,1)}, bf16[1056,128]{1,0:T(8,128)(2,1)S(1)}, u32[]{:S(2)}) copy-start(bf16[1056,128]{1,0:T(8,128)(2,1)S(1)} %collective-permute-done.1.refs_2_) | copy-start | bytes 811012
  18.9 0.7 %copy-start.2 = (bf16[1056,128]{1,0:T(8,128)(2,1)}, bf16[1056,128]{1,0:T(8,128)(2,1)S(1)}, u32[]{:S(2)}) copy-start(bf16[1056,128]{1,0:T(8,128)(2,1)S(1)} %collective-permute-done.refs_1_) | copy-start | bytes 811012
  22.7 8.6 %collective-permute-start.8 = (bf16[528,128]{1,0:T(8,128)(2,1)}, bf16[528,128]{1,0:T(8,128)(2,1)S(1)}, u32[]{:S(2)}, u32[]{:S(2)}) collective-permute-start(bf16[528,128]{1,0:T(8,128)(2,1)} %transform.1.refs_0_), channel_id=1, source_target_pairs={{0,24},{4,28},{8,16},{12,20},{16,8},{20,12},{24,0},{28,4},{1,25},{... | collective-permute-start | bytes 405512 | tf_op jit(solution)/shard_map/ppermute | solution.py:230
  26.3 11.8 %collective-permute-start.6 = (bf16[528,128]{1,0:T(8,128)(2,1)}, bf16[528,128]{1,0:T(8,128)(2,1)S(1)}, u32[]{:S(2)}, u32[]{:S(2)}) collective-permute-start(bf16[528,128]{1,0:T(8,128)(2,1)} %transform.1.refs_0_), channel_id=1, source_target_pairs={{0,16},{4,20},{8,24},{12,28},{16,0},{20,4},{24,8},{28,12},{1,17},{... | collective-permute-start | bytes 405512 | tf_op jit(solution)/shard_map/ppermute | solution.py:230
  26.3 11.8 %collective-permute-start.4 = (bf16[528,128]{1,0:T(8,128)(2,1)}, bf16[528,128]{1,0:T(8,128)(2,1)S(1)}, u32[]{:S(2)}, u32[]{:S(2)}) collective-permute-start(bf16[528,128]{1,0:T(8,128)(2,1)} %transform.1.refs_0_), channel_id=1, source_target_pairs={{0,8},{4,12},{8,0},{12,4},{16,24},{20,28},{24,16},{28,20},{1,9},{5... | collective-permute-start | bytes 405512 | tf_op jit(solution)/shard_map/ppermute | solution.py:230
  27.1 11.6 %collective-permute-start.3 = (bf16[528,128]{1,0:T(8,128)(2,1)}, bf16[528,128]{1,0:T(8,128)(2,1)S(1)}, u32[]{:S(2)}, u32[]{:S(2)}) collective-permute-start(bf16[528,128]{1,0:T(8,128)(2,1)} %transform.1.refs_0_), channel_id=1, source_target_pairs={{0,4},{4,0},{8,12},{12,8},{16,20},{20,16},{24,28},{28,24},{1,5},{5... | collective-permute-start | bytes 405512 | tf_op jit(solution)/shard_map/ppermute | solution.py:230
  31.3 8.4 %copy-start.3 = (bf16[528,128]{1,0:T(8,128)(2,1)}, bf16[528,128]{1,0:T(8,128)(2,1)S(1)}, u32[]{:S(2)}) copy-start(bf16[528,128]{1,0:T(8,128)(2,1)S(1)} %collective-permute-done.8.refs_6_) | copy-start | bytes 405508
  31.3 7.4 %collective-permute-start.9 = (bf16[528,128]{1,0:T(8,128)(2,1)S(1)}, bf16[528,128]{1,0:T(8,128)(2,1)S(1)}, u32[]{:S(2)}, u32[]{:S(2)}) collective-permute-start(bf16[528,128]{1,0:T(8,128)(2,1)S(1)} %collective-permute-done.8.refs_6_), channel_id=1, source_target_pairs={{0,4},{4,0},{8,12},{12,8},{16,20},{20,16},{24,28},{28,24},{1,5},{5... | collective-permute-start | bytes 405512 | tf_op jit(solution)/shard_map/ppermute | solution.py:230
  38.1 1.6 %copy-start.4 = (bf16[528,128]{1,0:T(8,128)(2,1)}, bf16[528,128]{1,0:T(8,128)(2,1)S(1)}, u32[]{:S(2)}) copy-start(bf16[528,128]{1,0:T(8,128)(2,1)S(1)} %collective-permute-done.6.refs_4_) | copy-start | bytes 405508
  38.1 1.4 %collective-permute-start.7 = (bf16[528,128]{1,0:T(8,128)(2,1)S(1)}, bf16[528,128]{1,0:T(8,128)(2,1)S(1)}, u32[]{:S(2)}, u32[]{:S(2)}) collective-permute-start(bf16[528,128]{1,0:T(8,128)(2,1)S(1)} %collective-permute-done.6.refs_4_), channel_id=1, source_target_pairs={{0,4},{4,0},{8,12},{12,8},{16,20},{20,16},{24,28},{28,24},{1,5},{5... | collective-permute-start | bytes 405512 | tf_op jit(solution)/shard_map/ppermute | solution.py:230
  38.2 1.5 %copy-start.5 = (bf16[528,128]{1,0:T(8,128)(2,1)}, bf16[528,128]{1,0:T(8,128)(2,1)S(1)}, u32[]{:S(2)}) copy-start(bf16[528,128]{1,0:T(8,128)(2,1)S(1)} %collective-permute-done.4.refs_2_) | copy-start | bytes 405508
  38.2 1.5 %collective-permute-start.5 = (bf16[528,128]{1,0:T(8,128)(2,1)S(1)}, bf16[528,128]{1,0:T(8,128)(2,1)S(1)}, u32[]{:S(2)}, u32[]{:S(2)}) collective-permute-start(bf16[528,128]{1,0:T(8,128)(2,1)S(1)} %collective-permute-done.4.refs_2_), channel_id=1, source_target_pairs={{0,4},{4,0},{8,12},{12,8},{16,20},{20,16},{24,28},{28,24},{1,5},{5... | collective-permute-start | bytes 405512 | tf_op jit(solution)/shard_map/ppermute | solution.py:230
  38.7 1.0 %copy-start.6 = (bf16[528,128]{1,0:T(8,128)(2,1)}, bf16[528,128]{1,0:T(8,128)(2,1)S(1)}, u32[]{:S(2)}) copy-start(bf16[528,128]{1,0:T(8,128)(2,1)S(1)} %collective-permute-done.3.refs_1_) | copy-start | bytes 405508
  38.7 1.0 %copy-start.7 = (bf16[528,128]{1,0:T(8,128)(2,1)}, bf16[528,128]{1,0:T(8,128)(2,1)S(1)}, u32[]{:S(2)}) copy-start(bf16[528,128]{1,0:T(8,128)(2,1)S(1)} %collective-permute-done.9.refs_7_) | copy-start | bytes 405508
  39.5 0.7 %copy-start.8 = (bf16[528,128]{1,0:T(8,128)(2,1)}, bf16[528,128]{1,0:T(8,128)(2,1)S(1)}, u32[]{:S(2)}) copy-start(bf16[528,128]{1,0:T(8,128)(2,1)S(1)} %collective-permute-done.7.refs_5_) | copy-start | bytes 405508
  40.2 0.6 %copy-start.9 = (bf16[528,128]{1,0:T(8,128)(2,1)}, bf16[528,128]{1,0:T(8,128)(2,1)S(1)}, u32[]{:S(2)}) copy-start(bf16[528,128]{1,0:T(8,128)(2,1)S(1)} %collective-permute-done.5.refs_3_) | copy-start | bytes 405508
  44.6 4.8 %collective-permute-start.12 = (f32[16,16]{1,0:T(8,128)}, f32[16,16]{1,0:T(8,128)S(1)}, u32[]{:S(2)}, u32[]{:S(2)}) collective-permute-start(f32[16,16]{1,0:T(8,128)} %contract.1), channel_id=1, source_target_pairs={{0,3},{1,2},{2,1},{3,0},{4,7},{5,6},{6,5},{7,4},{8,11},{9,10},{10,... | collective-permute-start | bytes 3080 | tf_op jit(solution)/shard_map/ppermute | solution.py:230
  45.6 3.9 %collective-permute-start.11 = (f32[16,16]{1,0:T(8,128)}, f32[16,16]{1,0:T(8,128)S(1)}, u32[]{:S(2)}, u32[]{:S(2)}) collective-permute-start(f32[16,16]{1,0:T(8,128)} %contract.1), channel_id=1, source_target_pairs={{0,2},{1,3},{2,0},{3,1},{4,6},{5,7},{6,4},{7,5},{8,10},{9,11},{10,... | collective-permute-start | bytes 3080 | tf_op jit(solution)/shard_map/ppermute | solution.py:230
  47.5 3.9 %collective-permute-start.10 = (f32[16,16]{1,0:T(8,128)}, f32[16,16]{1,0:T(8,128)S(1)}, u32[]{:S(2)}, u32[]{:S(2)}) collective-permute-start(f32[16,16]{1,0:T(8,128)} %contract.1), channel_id=1, source_target_pairs={{0,1},{1,0},{2,3},{3,2},{4,5},{5,4},{6,7},{7,6},{8,9},{9,8},{10,11... | collective-permute-start | bytes 3080 | tf_op jit(solution)/shard_map/ppermute | solution.py:230

commit v2 on v1

--- a/solution.py
+++ b/solution.py
@@ -1,3 +1,5 @@
+import math
+
 import jax
 import jax.numpy as jnp
 from jax import lax
@@ -33,7 +35,12 @@
     return ref[:, pl.ds(pl.multiple_of(index * block, block), block)]
 
 
-def prep_kernel(sizes_ref, pattern_ref, slab_ref, occ_ref, virt_ref, pay_ref, screen_ref, mask_ref):
+def prep_kernel(*refs):
+    hbm, (pay_ref, screen_ref), copied, mask_ref, sems = refs[:5], refs[5:7], refs[7:12], refs[12], refs[13]
+    copies = [pltpu.make_async_copy(src, dst, sems.at[i]) for i, (src, dst) in enumerate(zip(hbm, copied))]
+    for copy in copies:
+        copy.start()
+    sizes_ref, pattern_ref, slab_ref, occ_ref, virt_ref = copied
     block = occ_ref.shape[0]
     total = occ_ref.shape[1]
     ao = total // block
@@ -48,6 +55,8 @@
         lax.broadcasted_iota(jnp.int32, (atoms, total), 1), jnp.int32(4)
     )
     pick_col = (col_atom == lax.broadcasted_iota(jnp.int32, (atoms, total), 0)).astype(f32).astype(bf16)
+    copies[0].wait()
+    copies[1].wait()
     sizes = sizes_ref[...].astype(f32)
     size_row = jnp.sum(jnp.where(pick_row, jnp.broadcast_to(sizes, (block, atoms)), 0.0), axis=1, keepdims=True)
     size_col = jnp.dot(
@@ -64,6 +73,8 @@
     mask_ref[...] = jnp.where(live, kept, 0.0).astype(bf16)
     below, on = tri_masks(block)
     half = ao * block + TILE
+    for copy in copies[2:]:
+        copy.wait()
     for k in range(1, ao):
         screen = block_at(mask_ref, a ^ k, block)
         screen_ref[:, k * block : (k + 1) * block] = screen
@@ -118,7 +129,7 @@
 
 def transform_kernel(ao, block, *refs):
     pays = refs[:ao]
-    screen_ref, out_ref, slab_ref, green_ref, left_ref = refs[ao:]
+    screen_ref, _, out_ref, slab_ref, green_ref, left_ref = refs[ao:]
     total = ao * block
     a = lax.axis_index("ao")
     half = total + TILE
@@ -154,10 +165,25 @@
     out_ref[at + block : at + block + TILE, :] = jnp.broadcast_to(diagonal, (TILE, block)).astype(bf16)
 
 
+def stage_kernel(tensor_hbm, _, out_ref, tensor_ref, sem):
+    ri_rows, block, _ = tensor_ref.shape
+    a = lax.axis_index("ao")
+    copy = pltpu.make_async_copy(tensor_hbm, tensor_ref, sem)
+    copy.start()
+    copy.wait()
+    for k in range(out_ref.shape[0]):
+        cols = pl.ds(pl.multiple_of((a ^ k) * block, block), block)
+        for g in range(block // TILE):
+            for p in range(ri_rows):
+                out_ref[k, p * TILE : (p + 1) * TILE, g * block : (g + 1) * block] = tensor_ref[
+                    p, g * TILE : (g + 1) * TILE, cols
+                ]
+
+
 def contract_kernel(count, ao, block, *refs):
     pays = refs[:count]
     tensor_ref, out_ref = refs[count:]
-    ri_rows = tensor_ref.shape[0]
+    ri_rows = tensor_ref.shape[1] // TILE
     a = lax.axis_index("ao")
     r = lax.axis_index("ri")
     f32, bf16 = jnp.float32, jnp.bfloat16
@@ -172,10 +198,6 @@
             ],
             axis=1,
         )
-
-    def tensor_block(k):
-        cols = pl.ds(pl.multiple_of((a ^ k) * block, block), block)
-        return spread(range(ri_rows), lambda p, rows: tensor_ref[p, rows, cols])
 
     below, on = tri_masks(block)
     at = (ao - 1) * block
@@ -188,7 +210,7 @@
             jnp.where(below, 0.0, jnp.where(on, jnp.broadcast_to(diagonal, (block, block)), folded)).astype(bf16)
         )
     sums = lax.dot_general(
-        spread(firsts + seconds, lambda v, rows: v[rows]), tensor_block(0), last, preferred_element_type=f32
+        spread(firsts + seconds, lambda v, rows: v[rows]), tensor_ref[0], last, preferred_element_type=f32
     )
     half = count * TILE
     sums = [sums[:half], sums[half:]]
@@ -196,7 +218,7 @@
         start = (k - 1) * block
         part = lax.dot_general(
             spread(pays, lambda pay, rows: pay[start + rows.start : start + rows.stop, :]),
-            tensor_block(k),
+            tensor_ref[k],
             last,
             preferred_element_type=f32,
         )
@@ -226,6 +248,11 @@
     out_ref[...] = ordered * (1.0 / (ao * block))
 
 
+def room(*arrays):
+    total = sum(2 * math.prod(shape) for shape in arrays)
+    return pltpu.CompilerParams(vmem_limit_bytes=min(2 * total + (4 << 20), 60 << 20))
+
+
 def exchange(value, axis, size, k):
     return lax.ppermute(value, axis, [(i, i ^ k) for i in range(size)])
 
@@ -238,30 +265,48 @@
     half = total + TILE
     bf16 = jnp.bfloat16
     vmem = pl.BlockSpec(memory_space=pltpu.VMEM)
+    inputs = tuple(
+        pltpu.with_memory_space_constraint(x, pltpu.HBM)
+        for x in (atom_sizes.reshape(1, atoms), pattern, slab_tensor, occ_green, virt_green)
+    )
     pay, screen = pl.pallas_call(
         prep_kernel,
         out_shape=(
             jax.ShapeDtypeStruct((2 * half, block), bf16),
             jax.ShapeDtypeStruct((block, total), bf16),
         ),
-        in_specs=[vmem] * 5,
+        in_specs=[pl.BlockSpec(memory_space=pltpu.HBM)] * 5,
         out_specs=(vmem, vmem),
-        scratch_shapes=[pltpu.VMEM((block, total), bf16)],
+        scratch_shapes=[pltpu.VMEM(x.shape, x.dtype) for x in inputs]
+        + [pltpu.VMEM((block, total), bf16), pltpu.SemaphoreType.DMA((5,))],
+        compiler_params=room((4 * half, block), (3 * block, total), (2 * block, 2 * total)),
         name="prep",
-    )(atom_sizes.reshape(1, atoms), pattern, slab_tensor, occ_green, virt_green)
+    )(*inputs)
     pays = [pay] + [exchange(pay, "ao", ao, k) for k in range(1, ao)]
+    groups = block // TILE
+    staged = pl.pallas_call(
+        stage_kernel,
+        out_shape=jax.ShapeDtypeStruct((ao, ri_rows * TILE, groups * block), bf16),
+        in_specs=[pl.BlockSpec(memory_space=pltpu.HBM)] * 2,
+        out_specs=vmem,
+        scratch_shapes=[pltpu.VMEM(three_center.shape, bf16), pltpu.SemaphoreType.DMA],
+        compiler_params=room((2 * ri_rows, block, total)),
+        cost_estimate=pl.CostEstimate(flops=0, transcendentals=0, bytes_accessed=8 * ri_rows * block * total),
+        name="stage",
+    )(pltpu.with_memory_space_constraint(three_center, pltpu.HBM), pay)
     weighted = pl.pallas_call(
         lambda *refs: transform_kernel(ao, block, *refs),
         out_shape=jax.ShapeDtypeStruct((half, block), bf16),
-        in_specs=[vmem] * (ao + 1),
+        in_specs=[vmem] * (ao + 1) + [pl.BlockSpec(memory_space=pl.ANY)],
         out_specs=vmem,
         scratch_shapes=[
             pltpu.VMEM((2, total, total), bf16),
             pltpu.VMEM((ao, block, 2 * total), bf16),
             pltpu.VMEM((2, block, 2 * total), bf16),
         ],
+        compiler_params=room((2 * half * ao, block), (2, total, total), (ao, block, 2 * total), (4, block, total)),
         name="transform",
-    )(*pays, screen)
+    )(*pays, screen, staged)
     sources = [weighted]
     for k in range(2, ri, 2):
         sources.append(exchange(weighted, "ri", ri, k))
@@ -274,8 +319,9 @@
         out_shape=jax.ShapeDtypeStruct((ri_rows, 2 * ri), jnp.float32),
         in_specs=[vmem] * (ri + 1),
         out_specs=vmem,
+        compiler_params=room((half * ri, block), (2 * ri_rows, block, total)),
         name="contract",
-    )(*arrived, three_center)
+    )(*arrived, staged)
     parts = [part] + [exchange(part, "ao", ao, k) for k in range(1, ao)]
     while len(parts) > 1:
         parts = [parts[i] + parts[i + 1] for i in range(0, len(parts), 2)]

time: 52.9 us -> 44.3 us (0.84)
  Pallas kernels: 9.07 us -> 5.76 us
  waiting for transfers between devices: 27.6 us -> 24.6 us
  local copies, waits for them, and re-layouts: 1.8 us -> 0 us
  other arithmetic: 1.3 us -> 0.6 us
    ppermute x13, waiting for transfers between devices: 27.6 us -> 24.6 us  [exchange(): return lax.ppermute(value, axis, [(i, i ^ k) for i in range(size)])]
    pallas_call x1, Pallas kernels: 3.77 us -> 1.1 us  [shards(): pl.pallas_call(lambda *refs: contract_kernel(ri, ao, block, *refs), out_s...]
    pallas_call x0 -> x1, Pallas kernels: none -> 2.17 us  [shards(): pl.pallas_call(stage_kernel, out_shape=jax.ShapeDtypeStruct((ao, ri_rows...]
    pallas_call x1, Pallas kernels: 3.11 us -> 1.26 us  [shards(): pl.pallas_call(lambda *refs: transform_kernel(ao, block, *refs), out_shap...]
    unnamed x20 -> x0, local copies, waits for them, and re-layouts: 1.8 us -> none
    pallas_call x1, Pallas kernels: 2.19 us -> 1.23 us  [shards(): pl.pallas_call(prep_kernel, out_shape=(jax.ShapeDtypeStruct((2 * half, bl...]
    add x1, other arithmetic: 1.3 us -> 0.6 us  [shards(): parts = [parts[i] + parts[i + 1] for i in range(0, len(parts), 2)]]
  transfers between devices with their start and end apart: 13 -> 13, of which waited for: 10 -> 10; matrix products, arithmetic and copies ran while one was open for 0% -> 0% of each run, Pallas kernels for 0% -> 5%
where the time goes in v2:
time: 44.3 us; the launch traced here: 44.1 us
  waiting for transfers between devices  24.6 us (56%)
  starting transfers between devices  13.1 us (30%)
  Pallas kernels  5.76 us (13%)
  other arithmetic  0.6 us (1%)
    ppermute x13, waiting for transfers between devices, exchange(): return lax.ppermute(value, axis, [(i, i ^ k) for i in range(size)])  24.6 us
    ppermute x13, starting transfers between devices, exchange(): return lax.ppermute(value, axis, [(i, i ^ k) for i in range(size)])  13.1 us
    pallas_call x1, Pallas kernels, shards(): pl.pallas_call(stage_kernel, out_shape=jax.ShapeDtypeStruct((ao, ri_rows...  2.17 us
    pallas_call x1, Pallas kernels, shards(): pl.pallas_call(lambda *refs: transform_kernel(ao, block, *refs), out_shap...  1.26 us
    pallas_call x1, Pallas kernels, shards(): pl.pallas_call(prep_kernel, out_shape=(jax.ShapeDtypeStruct((2 * half, bl...  1.23 us
    pallas_call x1, Pallas kernels, shards(): pl.pallas_call(lambda *refs: contract_kernel(ri, ao, block, *refs), out_s...  1.1 us
  transfers between devices with their start and end apart: 13, of which 10 were waited for; matrix products, arithmetic and copies ran while one was open for 0% of the time, Pallas kernels for 5%

profile of v2, /device:TPU:0, one launch (start us, length us, event | category | flops | bytes accessed | tf_op | source)
XLA Modules:
  0.0 44.1 jit_solution(6749205402844260604)
XLA Ops:
  0.0 1.2 %prep.1 = (bf16[1056,128]{1,0:T(8,128)(2,1)S(1)}, bf16[128,512]{1,0:T(8,128)(2,1)S(1)}) custom-call(s32[1,32]{1,0:T(1,128)} %bitcast.1, s32[32,32]{1,0:T(8,128)} %refs_1_.1, bf16[2,128,512]{2,1,0:T(8,128)(2,1)} %refs_2_.1, bf16[128,512]{1,0:T(8,128)(2,1)} %refs_3_.1, bf16[128,512]{1,0:T(8,128)(2,1)} %refs_4_.1), custom_call_target="tpu_custom_call" | custom-call | tf_op jit(solution)/shard_map/prep/pallas_call | solution.py:272
  1.2 4.0 %collective-permute-start.2 = (bf16[1056,128]{1,0:T(8,128)(2,1)S(1)}, bf16[1056,128]{1,0:T(8,128)(2,1)S(1)}, u32[]{:S(2)}, u32[]{:S(2)}) collective-permute-start(bf16[1056,128]{1,0:T(8,128)(2,1)S(1)} %get-tuple-element.7._.refs_0_), channel_id=1, source_target_pairs={{0,3},{1,2},{2,1},{3,0},{4,7},{5,6},{6,5},{7,4},{8,11},{9,10},{10,... | collective-permute-start | bytes 811016 | tf_op jit(solution)/shard_map/ppermute | solution.py:257
  5.2 0.5 %collective-permute-start.1 = (bf16[1056,128]{1,0:T(8,128)(2,1)S(1)}, bf16[1056,128]{1,0:T(8,128)(2,1)S(1)}, u32[]{:S(2)}, u32[]{:S(2)}) collective-permute-start(bf16[1056,128]{1,0:T(8,128)(2,1)S(1)} %get-tuple-element.7._.refs_0_), channel_id=1, source_target_pairs={{0,2},{1,3},{2,0},{3,1},{4,6},{5,7},{6,4},{7,5},{8,10},{9,11},{10,... | collective-permute-start | bytes 811016 | tf_op jit(solution)/shard_map/ppermute | solution.py:257
  5.7 0.1 collective-permute-start
  5.9 2.2 %stage.1.refs_5_.refs_8_ = bf16[4,256,1024]{2,1,0:T(8,128)(2,1)S(1)} custom-call(bf16[16,128,512]{2,1,0:T(8,128)(2,1)} %tensor_hbm.1, bf16[1056,128]{1,0:T(8,128)(2,1)S(1)} %get-tuple-element.7._.refs_0_), custom_call_target="tpu_custom_call" | custom-call | bytes 8388608 | tf_op jit(solution)/shard_map/stage/pallas_call | solution.py:287
  8.1 4.6 %collective-permute-done.2.refs_3_ = bf16[1056,128]{1,0:T(8,128)(2,1)S(1)} collective-permute-done((bf16[1056,128]{1,0:T(8,128)(2,1)S(1)}, bf16[1056,128]{1,0:T(8,128)(2,1)S(1)}, u32[]{:S(2)}, u32[]{:S(2)}) %collective-permute-start.2) | collective-permute-done | bytes 270368 | tf_op jit(solution)/shard_map/ppermute | solution.py:257
  12.6 4.9 %collective-permute-done.1.refs_2_ = bf16[1056,128]{1,0:T(8,128)(2,1)S(1)} collective-permute-done((bf16[1056,128]{1,0:T(8,128)(2,1)S(1)}, bf16[1056,128]{1,0:T(8,128)(2,1)S(1)}, u32[]{:S(2)}, u32[]{:S(2)}) %collective-permute-start.1) | collective-permute-done | bytes 270368 | tf_op jit(solution)/shard_map/ppermute | solution.py:257
  17.5 0.3 collective-permute-done.refs_1_
  17.8 1.3 %transform.1.refs_0_ = bf16[528,128]{1,0:T(8,128)(2,1)S(1)} custom-call(bf16[1056,128]{1,0:T(8,128)(2,1)S(1)} %get-tuple-element.7._.refs_0_, bf16[1056,128]{1,0:T(8,128)(2,1)S(1)} %collective-permute-done.refs_1_, bf16[1056,128]{1,0:T(8,128)(2,1)S(1)} %collective-permute-done.1.refs_2_, bf16[1056,128]{1,0:T(8,128)(2,1)S(1)} %collective-permute-done.2.refs_3_, ...), custom_call_target="tpu_custom_call" | custom-call | tf_op jit(solution)/shard_map/transform/pallas_call | solution.py:297
  19.1 3.7 %collective-permute-start.8 = (bf16[528,128]{1,0:T(8,128)(2,1)S(1)}, bf16[528,128]{1,0:T(8,128)(2,1)S(1)}, u32[]{:S(2)}, u32[]{:S(2)}) collective-permute-start(bf16[528,128]{1,0:T(8,128)(2,1)S(1)} %transform.1.refs_0_), channel_id=1, source_target_pairs={{0,24},{4,28},{8,16},{12,20},{16,8},{20,12},{24,0},{28,4},{1,25},{... | collective-permute-start | bytes 405512 | tf_op jit(solution)/shard_map/ppermute | solution.py:257
  22.7 0.0 collective-permute-start.6
  22.7 0.8 %collective-permute-start.4 = (bf16[528,128]{1,0:T(8,128)(2,1)S(1)}, bf16[528,128]{1,0:T(8,128)(2,1)S(1)}, u32[]{:S(2)}, u32[]{:S(2)}) collective-permute-start(bf16[528,128]{1,0:T(8,128)(2,1)S(1)} %transform.1.refs_0_), channel_id=1, source_target_pairs={{0,8},{4,12},{8,0},{12,4},{16,24},{20,28},{24,16},{28,20},{1,9},{5... | collective-permute-start | bytes 405512 | tf_op jit(solution)/shard_map/ppermute | solution.py:257
  23.5 0.0 collective-permute-start.3
  23.5 3.9 %collective-permute-done.8.refs_6_ = bf16[528,128]{1,0:T(8,128)(2,1)S(1)} collective-permute-done((bf16[528,128]{1,0:T(8,128)(2,1)S(1)}, bf16[528,128]{1,0:T(8,128)(2,1)S(1)}, u32[]{:S(2)}, u32[]{:S(2)}) %collective-permute-start.8) | collective-permute-done | bytes 135200 | tf_op jit(solution)/shard_map/ppermute | solution.py:257
  27.5 0.0 collective-permute-start.9
  27.5 6.8 %collective-permute-done.6.refs_4_ = bf16[528,128]{1,0:T(8,128)(2,1)S(1)} collective-permute-done((bf16[528,128]{1,0:T(8,128)(2,1)S(1)}, bf16[528,128]{1,0:T(8,128)(2,1)S(1)}, u32[]{:S(2)}, u32[]{:S(2)}) %collective-permute-start.6) | collective-permute-done | bytes 135200 | tf_op jit(solution)/shard_map/ppermute | solution.py:257
  34.2 0.0 collective-permute-start.7
  34.2 0.0 collective-permute-done.4.refs_2_
  34.2 0.5 %collective-permute-start.5 = (bf16[528,128]{1,0:T(8,128)(2,1)S(1)}, bf16[528,128]{1,0:T(8,128)(2,1)S(1)}, u32[]{:S(2)}, u32[]{:S(2)}) collective-permute-start(bf16[528,128]{1,0:T(8,128)(2,1)S(1)} %collective-permute-done.4.refs_2_), channel_id=1, source_target_pairs={{0,4},{4,0},{8,12},{12,8},{16,20},{20,16},{24,28},{28,24},{1,5},{5... | collective-permute-start | bytes 405512 | tf_op jit(solution)/shard_map/ppermute | solution.py:257
  34.8 0.0 collective-permute-done.3.refs_1_
  34.8 0.0 collective-permute-done.9.refs_7_
  34.8 0.8 %collective-permute-done.7.refs_5_ = bf16[528,128]{1,0:T(8,128)(2,1)S(1)} collective-permute-done((bf16[528,128]{1,0:T(8,128)(2,1)S(1)}, bf16[528,128]{1,0:T(8,128)(2,1)S(1)}, u32[]{:S(2)}, u32[]{:S(2)}) %collective-permute-start.7) | collective-permute-done | bytes 135200 | tf_op jit(solution)/shard_map/ppermute | solution.py:257
  35.6 0.2 collective-permute-done.5.refs_3_
  35.8 1.1 %contract.1 = f32[16,16]{1,0:T(8,128)S(1)} custom-call(bf16[528,128]{1,0:T(8,128)(2,1)S(1)} %transform.1.refs_0_, bf16[528,128]{1,0:T(8,128)(2,1)S(1)} %collective-permute-done.3.refs_1_, bf16[528,128]{1,0:T(8,128)(2,1)S(1)} %collective-permute-done.4.refs_2_, bf16[528,128]{1,0:T(8,128)(2,1)S(1)} %collective-permute-done.5.refs_3_, ...), custom_call_target="tpu_custom_call" | custom-call | tf_op jit(solution)/shard_map/contract/pallas_call | solution.py:317
  36.9 1.1 %collective-permute-start.12 = (f32[16,16]{1,0:T(8,128)S(1)}, f32[16,16]{1,0:T(8,128)S(1)}, u32[]{:S(2)}, u32[]{:S(2)}) collective-permute-start(f32[16,16]{1,0:T(8,128)S(1)} %contract.1), channel_id=1, source_target_pairs={{0,3},{1,2},{2,1},{3,0},{4,7},{5,6},{6,5},{7,4},{8,11},{9,10},{10,... | collective-permute-start | bytes 3080 | tf_op jit(solution)/shard_map/ppermute | solution.py:257
  38.0 1.9 %collective-permute-start.11 = (f32[16,16]{1,0:T(8,128)S(1)}, f32[16,16]{1,0:T(8,128)S(1)}, u32[]{:S(2)}, u32[]{:S(2)}) collective-permute-start(f32[16,16]{1,0:T(8,128)S(1)} %contract.1), channel_id=1, source_target_pairs={{0,2},{1,3},{2,0},{3,1},{4,6},{5,7},{6,4},{7,5},{8,10},{9,11},{10,... | collective-permute-start | bytes 3080 | tf_op jit(solution)/shard_map/ppermute | solution.py:257
  39.9 0.5 %collective-permute-start.10 = (f32[16,16]{1,0:T(8,128)S(1)}, f32[16,16]{1,0:T(8,128)S(1)}, u32[]{:S(2)}, u32[]{:S(2)}) collective-permute-start(f32[16,16]{1,0:T(8,128)S(1)} %contract.1), channel_id=1, source_target_pairs={{0,1},{1,0},{2,3},{3,2},{4,5},{5,4},{6,7},{7,6},{8,9},{9,8},{10,11... | collective-permute-start | bytes 3080 | tf_op jit(solution)/shard_map/ppermute | solution.py:257
  40.4 1.1 %collective-permute-done.12 = f32[16,16]{1,0:T(8,128)S(1)} collective-permute-done((f32[16,16]{1,0:T(8,128)S(1)}, f32[16,16]{1,0:T(8,128)S(1)}, u32[]{:S(2)}, u32[]{:S(2)}) %collective-permute-start.12) | collective-permute-done | bytes 1056 | tf_op jit(solution)/shard_map/ppermute | solution.py:257
  41.5 0.2 collective-permute-done.11
  41.6 1.9 %collective-permute-done.10 = f32[16,16]{1,0:T(8,128)S(1)} collective-permute-done((f32[16,16]{1,0:T(8,128)S(1)}, f32[16,16]{1,0:T(8,128)S(1)}, u32[]{:S(2)}, u32[]{:S(2)}) %collective-permute-start.10) | collective-permute-done | bytes 1056 | tf_op jit(solution)/shard_map/ppermute | solution.py:257
  43.5 0.6 %add_add_fusion = f32[16,16]{1,0:T(8,128)} fusion(f32[16,16]{1,0:T(8,128)S(1)} %collective-permute-done.11, f32[16,16]{1,0:T(8,128)S(1)} %collective-permute-done.12, f32[16,16]{1,0:T(8,128)S(1)} %contract.1, f32[16,16]{1,0:T(8,128)S(1)} %collective-permute-done.10), kind=kLoop, calls=%fused_computation | loop fusion | flops 768 | bytes 5120 | tf_op jit(solution)/shard_map/add | solution.py:327
Async XLA Ops:
  1.2 11.4 %collective-permute-start.2 = (bf16[1056,128]{1,0:T(8,128)(2,1)S(1)}, bf16[1056,128]{1,0:T(8,128)(2,1)S(1)}, u32[]{:S(2)}, u32[]{:S(2)}) collective-permute-start(bf16[1056,128]{1,0:T(8,128)(2,1)S(1)} %get-tuple-element.7._.refs_0_), channel_id=1, source_target_pairs={{0,3},{1,2},{2,1},{3,0},{4,7},{5,6},{6,5},{7,4},{8,11},{9,10},{10,... | collective-permute-start | bytes 811016 | tf_op jit(solution)/shard_map/ppermute | solution.py:257
  5.2 12.3 %collective-permute-start.1 = (bf16[1056,128]{1,0:T(8,128)(2,1)S(1)}, bf16[1056,128]{1,0:T(8,128)(2,1)S(1)}, u32[]{:S(2)}, u32[]{:S(2)}) collective-permute-start(bf16[1056,128]{1,0:T(8,128)(2,1)S(1)} %get-tuple-element.7._.refs_0_), channel_id=1, source_target_pairs={{0,2},{1,3},{2,0},{3,1},{4,6},{5,7},{6,4},{7,5},{8,10},{9,11},{10,... | collective-permute-start | bytes 811016 | tf_op jit(solution)/shard_map/ppermute | solution.py:257
  5.7 12.1 %collective-permute-start = (bf16[1056,128]{1,0:T(8,128)(2,1)S(1)}, bf16[1056,128]{1,0:T(8,128)(2,1)S(1)}, u32[]{:S(2)}, u32[]{:S(2)}) collective-permute-start(bf16[1056,128]{1,0:T(8,128)(2,1)S(1)} %get-tuple-element.7._.refs_0_), channel_id=1, source_target_pairs={{0,1},{1,0},{2,3},{3,2},{4,5},{5,4},{6,7},{7,6},{8,9},{9,8},{10,11... | collective-permute-start | bytes 811016 | tf_op jit(solution)/shard_map/ppermute | solution.py:257
  19.1 8.4 %collective-permute-start.8 = (bf16[528,128]{1,0:T(8,128)(2,1)S(1)}, bf16[528,128]{1,0:T(8,128)(2,1)S(1)}, u32[]{:S(2)}, u32[]{:S(2)}) collective-permute-start(bf16[528,128]{1,0:T(8,128)(2,1)S(1)} %transform.1.refs_0_), channel_id=1, source_target_pairs={{0,24},{4,28},{8,16},{12,20},{16,8},{20,12},{24,0},{28,4},{1,25},{... | collective-permute-start | bytes 405512 | tf_op jit(solution)/shard_map/ppermute | solution.py:257
  22.7 11.5 %collective-permute-start.6 = (bf16[528,128]{1,0:T(8,128)(2,1)S(1)}, bf16[528,128]{1,0:T(8,128)(2,1)S(1)}, u32[]{:S(2)}, u32[]{:S(2)}) collective-permute-start(bf16[528,128]{1,0:T(8,128)(2,1)S(1)} %transform.1.refs_0_), channel_id=1, source_target_pairs={{0,16},{4,20},{8,24},{12,28},{16,0},{20,4},{24,8},{28,12},{1,17},{... | collective-permute-start | bytes 405512 | tf_op jit(solution)/shard_map/ppermute | solution.py:257
  22.7 11.5 %collective-permute-start.4 = (bf16[528,128]{1,0:T(8,128)(2,1)S(1)}, bf16[528,128]{1,0:T(8,128)(2,1)S(1)}, u32[]{:S(2)}, u32[]{:S(2)}) collective-permute-start(bf16[528,128]{1,0:T(8,128)(2,1)S(1)} %transform.1.refs_0_), channel_id=1, source_target_pairs={{0,8},{4,12},{8,0},{12,4},{16,24},{20,28},{24,16},{28,20},{1,9},{5... | collective-permute-start | bytes 405512 | tf_op jit(solution)/shard_map/ppermute | solution.py:257
  23.5 11.2 %collective-permute-start.3 = (bf16[528,128]{1,0:T(8,128)(2,1)S(1)}, bf16[528,128]{1,0:T(8,128)(2,1)S(1)}, u32[]{:S(2)}, u32[]{:S(2)}) collective-permute-start(bf16[528,128]{1,0:T(8,128)(2,1)S(1)} %transform.1.refs_0_), channel_id=1, source_target_pairs={{0,4},{4,0},{8,12},{12,8},{16,20},{20,16},{24,28},{28,24},{1,5},{5... | collective-permute-start | bytes 405512 | tf_op jit(solution)/shard_map/ppermute | solution.py:257
  27.5 7.3 %collective-permute-start.9 = (bf16[528,128]{1,0:T(8,128)(2,1)S(1)}, bf16[528,128]{1,0:T(8,128)(2,1)S(1)}, u32[]{:S(2)}, u32[]{:S(2)}) collective-permute-start(bf16[528,128]{1,0:T(8,128)(2,1)S(1)} %collective-permute-done.8.refs_6_), channel_id=1, source_target_pairs={{0,4},{4,0},{8,12},{12,8},{16,20},{20,16},{24,28},{28,24},{1,5},{5... | collective-permute-start | bytes 405512 | tf_op jit(solution)/shard_map/ppermute | solution.py:257
  34.2 1.4 %collective-permute-start.7 = (bf16[528,128]{1,0:T(8,128)(2,1)S(1)}, bf16[528,128]{1,0:T(8,128)(2,1)S(1)}, u32[]{:S(2)}, u32[]{:S(2)}) collective-permute-start(bf16[528,128]{1,0:T(8,128)(2,1)S(1)} %collective-permute-done.6.refs_4_), channel_id=1, source_target_pairs={{0,4},{4,0},{8,12},{12,8},{16,20},{20,16},{24,28},{28,24},{1,5},{5... | collective-permute-start | bytes 405512 | tf_op jit(solution)/shard_map/ppermute | solution.py:257
  34.2 1.5 %collective-permute-start.5 = (bf16[528,128]{1,0:T(8,128)(2,1)S(1)}, bf16[528,128]{1,0:T(8,128)(2,1)S(1)}, u32[]{:S(2)}, u32[]{:S(2)}) collective-permute-start(bf16[528,128]{1,0:T(8,128)(2,1)S(1)} %collective-permute-done.4.refs_2_), channel_id=1, source_target_pairs={{0,4},{4,0},{8,12},{12,8},{16,20},{20,16},{24,28},{28,24},{1,5},{5... | collective-permute-start | bytes 405512 | tf_op jit(solution)/shard_map/ppermute | solution.py:257
  36.9 4.6 %collective-permute-start.12 = (f32[16,16]{1,0:T(8,128)S(1)}, f32[16,16]{1,0:T(8,128)S(1)}, u32[]{:S(2)}, u32[]{:S(2)}) collective-permute-start(f32[16,16]{1,0:T(8,128)S(1)} %contract.1), channel_id=1, source_target_pairs={{0,3},{1,2},{2,1},{3,0},{4,7},{5,6},{6,5},{7,4},{8,11},{9,10},{10,... | collective-permute-start | bytes 3080 | tf_op jit(solution)/shard_map/ppermute | solution.py:257
  38.0 3.7 %collective-permute-start.11 = (f32[16,16]{1,0:T(8,128)S(1)}, f32[16,16]{1,0:T(8,128)S(1)}, u32[]{:S(2)}, u32[]{:S(2)}) collective-permute-start(f32[16,16]{1,0:T(8,128)S(1)} %contract.1), channel_id=1, source_target_pairs={{0,2},{1,3},{2,0},{3,1},{4,6},{5,7},{6,4},{7,5},{8,10},{9,11},{10,... | collective-permute-start | bytes 3080 | tf_op jit(solution)/shard_map/ppermute | solution.py:257
  39.9 3.7 %collective-permute-start.10 = (f32[16,16]{1,0:T(8,128)S(1)}, f32[16,16]{1,0:T(8,128)S(1)}, u32[]{:S(2)}, u32[]{:S(2)}) collective-permute-start(f32[16,16]{1,0:T(8,128)S(1)} %contract.1), channel_id=1, source_target_pairs={{0,1},{1,0},{2,3},{3,2},{4,5},{5,4},{6,7},{7,6},{8,9},{9,8},{10,11... | collective-permute-start | bytes 3080 | tf_op jit(solution)/shard_map/ppermute | solution.py:257

commit v3 on v2

--- a/solution.py
+++ b/solution.py
@@ -36,7 +36,8 @@
 
 
 def prep_kernel(*refs):
-    hbm, (pay_ref, screen_ref), copied, mask_ref, sems = refs[:5], refs[5:7], refs[7:12], refs[12], refs[13]
+    hbm, copied, mask_ref, sems = refs[:5], refs[9:14], refs[14], refs[15]
+    pay_ref, green_ref, part_ref, screen_ref = refs[5:9]
     copies = [pltpu.make_async_copy(src, dst, sems.at[i]) for i, (src, dst) in enumerate(zip(hbm, copied))]
     for copy in copies:
         copy.start()
@@ -72,7 +73,6 @@
     live = (slot_row < size_row) & (slot_col < size_col)
     mask_ref[...] = jnp.where(live, kept, 0.0).astype(bf16)
     below, on = tri_masks(block)
-    half = ao * block + TILE
     for copy in copies[2:]:
         copy.wait()
     for k in range(1, ao):
@@ -82,7 +82,7 @@
         start = (k - 1) * block
         cols = pl.ds(pl.multiple_of((a ^ k) * block, block), block)
         pay_ref[start : start + block, :] = slab_ref[matrix, :, cols] * screen
-        pay_ref[half + start : half + start + block, :] = jnp.where(
+        green_ref[start : start + block, :] = jnp.where(
             matrix == 0, occ_ref[:, cols], virt_ref[:, cols]
         )
     screen = block_at(mask_ref, a, block)
@@ -90,23 +90,45 @@
     own = pl.ds(pl.multiple_of(a * block, block), block)
     start = (ao - 1) * block
     pairs = (
-        (start, (slab_ref[0, :, own] * screen).astype(f32), (slab_ref[1, :, own] * screen).astype(f32)),
-        (half + start, occ_ref[:, own].astype(f32), virt_ref[:, own].astype(f32)),
-    )
-    for at, first, second in pairs:
+        (pay_ref, (slab_ref[0, :, own] * screen).astype(f32), (slab_ref[1, :, own] * screen).astype(f32)),
+        (green_ref, occ_ref[:, own].astype(f32), virt_ref[:, own].astype(f32)),
+    )
+    for ref, first, second in pairs:
         folded, diagonal = fold_diagonal(first, second, below, on)
-        pay_ref[at : at + block, :] = folded.astype(bf16)
-        pay_ref[at + block : at + block + TILE, :] = jnp.broadcast_to(diagonal, (TILE, block)).astype(bf16)
-
-
-def unfold(pays, base, a, ao, block, put):
+        ref[start : start + block, :] = folded.astype(bf16)
+        ref[start + block :, :] = jnp.broadcast_to(diagonal, (TILE, block)).astype(bf16)
+    core = lax.axis_index("ri") & 1
+    rows = block // 2
+    for k in range(ao):
+        part_ref[k * rows : (k + 1) * rows, :] = green_ref[
+            pl.ds(pl.multiple_of(k * block + core * rows, TILE), rows), :
+        ]
+    part_ref[ao * rows :, :] = green_ref[ao * block :, :]
+
+
+def whole_reader(ref, block):
+    return lambda k: ref[k * block : (k + 1) * block, :] if k >= 0 else ref[ref.shape[0] - TILE :, :]
+
+
+def halves_reader(mine, other, core, block):
+    rows = block // 2
+
+    def read(k):
+        if k < 0:
+            return mine[mine.shape[0] - TILE :, :]
+        here, there = mine[k * rows : (k + 1) * rows, :], other[k * rows : (k + 1) * rows, :]
+        return jnp.concatenate([jnp.where(core == 0, here, there), jnp.where(core == 0, there, here)], axis=0)
+
+    return read
+
+
+def unfold(reads, a, ao, block, put):
     below, on = tri_masks(block)
     for m in range(ao):
         for j in range(m + 1, ao):
             k = m ^ j
-            at = base + (k - 1) * block
-            here = pays[m][at : at + block, :]
-            there = pays[j][at : at + block, :]
+            here = reads[m](k - 1)
+            there = reads[j](k - 1)
             here_t = here.T
             there_t = there.T
             lower = which(a ^ m, k) == 0
@@ -114,10 +136,9 @@
             put(0, j, m, jnp.where(lower, here_t, there))
             put(1, m, j, jnp.where(lower, there_t, here))
             put(1, j, m, jnp.where(lower, there, here_t))
-        at = base + (ao - 1) * block
-        folded = pays[m][at : at + block, :].astype(jnp.float32)
+        folded = reads[m](ao - 1).astype(jnp.float32)
         folded_t = folded.T
-        diagonal = pays[m][at + block : at + block + TILE, :].astype(jnp.float32)[0:1]
+        diagonal = reads[m](-1).astype(jnp.float32)[0:1]
         put(0, m, m, jnp.where(below | on, folded, folded_t).astype(jnp.bfloat16))
         put(
             1, m, m,
@@ -128,12 +149,13 @@
 
 
 def transform_kernel(ao, block, *refs):
-    pays = refs[:ao]
-    screen_ref, _, out_ref, slab_ref, green_ref, left_ref = refs[ao:]
+    pays, own, mine, other = refs[:ao], refs[ao], refs[ao + 1 : 2 * ao], refs[2 * ao : 3 * ao - 1]
+    screen_ref, _, out_ref, slab_ref, green_ref, left_ref = refs[3 * ao - 1 :]
     total = ao * block
     a = lax.axis_index("ao")
-    half = total + TILE
+    core = lax.axis_index("ri") & 1
     f32, bf16 = jnp.float32, jnp.bfloat16
+    greens = [whole_reader(own, block)] + [halves_reader(x, y, core, block) for x, y in zip(mine, other)]
 
     def put_slab(matrix, row, col, value):
         slab_ref[matrix, row * block : (row + 1) * block, col * block : (col + 1) * block] = value
@@ -142,8 +164,8 @@
         at = (total if matrix == 0 else 0) + col * block
         green_ref[row, :, at : at + block] = value
 
-    unfold(pays, half, a, ao, block, put_green)
-    unfold(pays, 0, a, ao, block, put_slab)
+    unfold(greens, a, ao, block, put_green)
+    unfold([whole_reader(x, block) for x in pays], a, ao, block, put_slab)
     both = jnp.concatenate([green_ref[0, :, total:], green_ref[0, :, :total]], axis=0)
     for q in range(2):
         left = jnp.dot(both, slab_ref[q], preferred_element_type=f32).astype(bf16)
@@ -269,19 +291,22 @@
         pltpu.with_memory_space_constraint(x, pltpu.HBM)
         for x in (atom_sizes.reshape(1, atoms), pattern, slab_tensor, occ_green, virt_green)
     )
-    pay, screen = pl.pallas_call(
+    pay, green, green_part, screen = pl.pallas_call(
         prep_kernel,
         out_shape=(
-            jax.ShapeDtypeStruct((2 * half, block), bf16),
+            jax.ShapeDtypeStruct((half, block), bf16),
+            jax.ShapeDtypeStruct((half, block), bf16),
+            jax.ShapeDtypeStruct((total // 2 + TILE, block), bf16),
             jax.ShapeDtypeStruct((block, total), bf16),
         ),
         in_specs=[pl.BlockSpec(memory_space=pltpu.HBM)] * 5,
-        out_specs=(vmem, vmem),
+        out_specs=(vmem,) * 4,
         scratch_shapes=[pltpu.VMEM(x.shape, x.dtype) for x in inputs]
         + [pltpu.VMEM((block, total), bf16), pltpu.SemaphoreType.DMA((5,))],
         compiler_params=room((4 * half, block), (3 * block, total), (2 * block, 2 * total)),
         name="prep",
     )(*inputs)
+    green_mine = [exchange(green_part, "ao", ao, k) for k in range(1, ao)]
     pays = [pay] + [exchange(pay, "ao", ao, k) for k in range(1, ao)]
     groups = block // TILE
     staged = pl.pallas_call(
@@ -294,10 +319,12 @@
         cost_estimate=pl.CostEstimate(flops=0, transcendentals=0, bytes_accessed=8 * ri_rows * block * total),
         name="stage",
     )(pltpu.with_memory_space_constraint(three_center, pltpu.HBM), pay)
+    green_mine, staged = lax.optimization_barrier((green_mine, staged))
+    green_other = [exchange(value, "ri", ri, 1) for value in green_mine]
     weighted = pl.pallas_call(
         lambda *refs: transform_kernel(ao, block, *refs),
         out_shape=jax.ShapeDtypeStruct((half, block), bf16),
-        in_specs=[vmem] * (ao + 1) + [pl.BlockSpec(memory_space=pl.ANY)],
+        in_specs=[vmem] * (3 * ao) + [pl.BlockSpec(memory_space=pl.ANY)],
         out_specs=vmem,
         scratch_shapes=[
             pltpu.VMEM((2, total, total), bf16),
@@ -306,7 +333,7 @@
         ],
         compiler_params=room((2 * half * ao, block), (2, total, total), (ao, block, 2 * total), (4, block, total)),
         name="transform",
-    )(*pays, screen, staged)
+    )(*pays, green, *green_mine, *green_other, screen, staged)
     sources = [weighted]
     for k in range(2, ri, 2):
         sources.append(exchange(weighted, "ri", ri, k))

time: 44.3 us -> 41.9 us (0.946)
  waiting for transfers between devices: 24.6 us -> 17.3 us
  starting transfers between devices: 13.1 us -> 18 us
    ppermute x13 -> x19, waiting for transfers between devices: 24.6 us -> 17.3 us  [exchange(): return lax.ppermute(value, axis, [(i, i ^ k) for i in range(size)])]
    ppermute x13 -> x19, starting transfers between devices: 13.1 us -> 18 us  [exchange(): return lax.ppermute(value, axis, [(i, i ^ k) for i in range(size)])]
  transfers between devices with their start and end apart: 13 -> 19, of which waited for: 10 -> 10; matrix products, arithmetic and copies ran while one was open for 0% -> 0% of each run, Pallas kernels for 5% -> 5%
where the time goes in v3:
time: 41.9 us; the launch traced here: 41.8 us
  starting transfers between devices  18 us (43%)
  waiting for transfers between devices  17.3 us (41%)
  Pallas kernels  5.81 us (14%)
  other arithmetic  0.6 us (1%)
    ppermute x19, starting transfers between devices, exchange(): return lax.ppermute(value, axis, [(i, i ^ k) for i in range(size)])  18 us
    ppermute x19, waiting for transfers between devices, exchange(): return lax.ppermute(value, axis, [(i, i ^ k) for i in range(size)])  17.3 us
    pallas_call x1, Pallas kernels, shards(): pl.pallas_call(stage_kernel, out_shape=jax.ShapeDtypeStruct((ao, ri_rows...  2.17 us
    pallas_call x1, Pallas kernels, shards(): pl.pallas_call(lambda *refs: transform_kernel(ao, block, *refs), out_shap...  1.29 us
    pallas_call x1, Pallas kernels, shards(): pl.pallas_call(prep_kernel, out_shape=(jax.ShapeDtypeStruct((half, block)...  1.26 us
    pallas_call x1, Pallas kernels, shards(): pl.pallas_call(lambda *refs: contract_kernel(ri, ao, block, *refs), out_s...  1.1 us
  transfers between devices with their start and end apart: 19, of which 10 were waited for; matrix products, arithmetic and copies ran while one was open for 0% of the time, Pallas kernels for 5%

profile of v3, /device:TPU:0, one launch (start us, length us, event | category | flops | bytes accessed | tf_op | source)
XLA Modules:
  0.0 41.8 jit_solution(1241585547231999959)
XLA Ops:
  0.0 1.3 %prep.1 = (bf16[528,128]{1,0:T(8,128)(2,1)S(1)}, bf16[528,128]{1,0:T(8,128)(2,1)S(1)}, bf16[272,128]{1,0:T(8,128)(2,1)S(1)}, bf16[128,512]{1,0:T(8,128)(2,1)S(1)}) custom-call(s32[1,32]{1,0:T(1,128)} %bitcast.1, s32[32,32]{1,0:T(8,128)} %refs_1_.1, bf16[2,128,512]{2,1,0:T(8,128)(2,1)} %refs_2_.1, bf16[128,512]{1,0:T(8,128)(2,1)} %refs_3_.1, ...), custom_call_target="tpu_custom_call" | custom-call | tf_op jit(solution)/shard_map/prep/pallas_call | solution.py:294
  1.3 4.0 %collective-permute-start.5 = (bf16[272,128]{1,0:T(8,128)(2,1)S(1)}, bf16[272,128]{1,0:T(8,128)(2,1)S(1)}, u32[]{:S(2)}, u32[]{:S(2)}) collective-permute-start(bf16[272,128]{1,0:T(8,128)(2,1)S(1)} %get-tuple-element.15), channel_id=1, source_target_pairs={{0,3},{1,2},{2,1},{3,0},{4,7},{5,6},{6,5},{7,4},{8,11},{9,10},{10,... | collective-permute-start | bytes 208904 | tf_op jit(solution)/shard_map/ppermute | solution.py:279
  5.3 0.1 collective-permute-start.2
  5.3 1.9 %collective-permute-start.4 = (bf16[272,128]{1,0:T(8,128)(2,1)S(1)}, bf16[272,128]{1,0:T(8,128)(2,1)S(1)}, u32[]{:S(2)}, u32[]{:S(2)}) collective-permute-start(bf16[272,128]{1,0:T(8,128)(2,1)S(1)} %get-tuple-element.15), channel_id=1, source_target_pairs={{0,2},{1,3},{2,0},{3,1},{4,6},{5,7},{6,4},{7,5},{8,10},{9,11},{10,... | collective-permute-start | bytes 208904 | tf_op jit(solution)/shard_map/ppermute | solution.py:279
  7.3 1.5 %collective-permute-start.3 = (bf16[272,128]{1,0:T(8,128)(2,1)S(1)}, bf16[272,128]{1,0:T(8,128)(2,1)S(1)}, u32[]{:S(2)}, u32[]{:S(2)}) collective-permute-start(bf16[272,128]{1,0:T(8,128)(2,1)S(1)} %get-tuple-element.15), channel_id=1, source_target_pairs={{0,1},{1,0},{2,3},{3,2},{4,5},{5,4},{6,7},{7,6},{8,9},{9,8},{10,11... | collective-permute-start | bytes 208904 | tf_op jit(solution)/shard_map/ppermute | solution.py:279
  8.7 0.5 %collective-permute-start.1 = (bf16[528,128]{1,0:T(8,128)(2,1)S(1)}, bf16[528,128]{1,0:T(8,128)(2,1)S(1)}, u32[]{:S(2)}, u32[]{:S(2)}) collective-permute-start(bf16[528,128]{1,0:T(8,128)(2,1)S(1)} %get-tuple-element.13._.refs_0_), channel_id=1, source_target_pairs={{0,2},{1,3},{2,0},{3,1},{4,6},{5,7},{6,4},{7,5},{8,10},{9,11},{10,... | collective-permute-start | bytes 405512 | tf_op jit(solution)/shard_map/ppermute | solution.py:279
  9.2 0.0 collective-permute-done.5.refs_7_
  9.3 1.0 %collective-permute-start = (bf16[528,128]{1,0:T(8,128)(2,1)S(1)}, bf16[528,128]{1,0:T(8,128)(2,1)S(1)}, u32[]{:S(2)}, u32[]{:S(2)}) collective-permute-start(bf16[528,128]{1,0:T(8,128)(2,1)S(1)} %get-tuple-element.13._.refs_0_), channel_id=1, source_target_pairs={{0,1},{1,0},{2,3},{3,2},{4,5},{5,4},{6,7},{7,6},{8,9},{9,8},{10,11... | collective-permute-start | bytes 405512 | tf_op jit(solution)/shard_map/ppermute | solution.py:279
  10.3 2.2 %stage.1.refs_12_.refs_8_ = bf16[4,256,1024]{2,1,0:T(8,128)(2,1)S(1)} custom-call(bf16[16,128,512]{2,1,0:T(8,128)(2,1)} %tensor_hbm.1, bf16[528,128]{1,0:T(8,128)(2,1)S(1)} %get-tuple-element.13._.refs_0_), custom_call_target="tpu_custom_call" | custom-call | bytes 8388608 | tf_op jit(solution)/shard_map/stage/pallas_call | solution.py:312
  12.4 0.0 collective-permute-done.4.refs_6_
  12.5 0.7 %collective-permute-done.3.refs_5_ = bf16[272,128]{1,0:T(8,128)(2,1)S(1)} collective-permute-done((bf16[272,128]{1,0:T(8,128)(2,1)S(1)}, bf16[272,128]{1,0:T(8,128)(2,1)S(1)}, u32[]{:S(2)}, u32[]{:S(2)}) %collective-permute-start.3) | collective-permute-done | bytes 69664 | tf_op jit(solution)/shard_map/ppermute | solution.py:279
  13.2 0.0 collective-permute-start.6
  13.2 0.5 %collective-permute-start.7 = (bf16[272,128]{1,0:T(8,128)(2,1)S(1)}, bf16[272,128]{1,0:T(8,128)(2,1)S(1)}, u32[]{:S(2)}, u32[]{:S(2)}) collective-permute-start(bf16[272,128]{1,0:T(8,128)(2,1)S(1)} %collective-permute-done.4.refs_6_), channel_id=1, source_target_pairs={{0,4},{4,0},{8,12},{12,8},{16,20},{20,16},{24,28},{28,24},{1,5},{5... | collective-permute-start | bytes 208904 | tf_op jit(solution)/shard_map/ppermute | solution.py:279
  13.7 0.0 collective-permute-done.2.refs_3_
  13.7 0.0 collective-permute-start.8
  13.7 1.1 %collective-permute-done.1.refs_2_ = bf16[528,128]{1,0:T(8,128)(2,1)S(1)} collective-permute-done((bf16[528,128]{1,0:T(8,128)(2,1)S(1)}, bf16[528,128]{1,0:T(8,128)(2,1)S(1)}, u32[]{:S(2)}, u32[]{:S(2)}) %collective-permute-start.1) | collective-permute-done | bytes 135200 | tf_op jit(solution)/shard_map/ppermute | solution.py:279
  14.8 0.6 %collective-permute-done.refs_1_ = bf16[528,128]{1,0:T(8,128)(2,1)S(1)} collective-permute-done((bf16[528,128]{1,0:T(8,128)(2,1)S(1)}, bf16[528,128]{1,0:T(8,128)(2,1)S(1)}, u32[]{:S(2)}, u32[]{:S(2)}) %collective-permute-start) | collective-permute-done | bytes 135200 | tf_op jit(solution)/shard_map/ppermute | solution.py:279
  15.4 0.0 collective-permute-done.6.refs_8_
  15.4 0.0 collective-permute-done.7.refs_9_
  15.4 0.0 collective-permute-done.8.refs_10_
  15.4 1.3 %transform.1.refs_0_ = bf16[528,128]{1,0:T(8,128)(2,1)S(1)} custom-call(bf16[528,128]{1,0:T(8,128)(2,1)S(1)} %get-tuple-element.13._.refs_0_, bf16[528,128]{1,0:T(8,128)(2,1)S(1)} %collective-permute-done.refs_1_, bf16[528,128]{1,0:T(8,128)(2,1)S(1)} %collective-permute-done.1.refs_2_, bf16[528,128]{1,0:T(8,128)(2,1)S(1)} %collective-permute-done.2.refs_3_, ...), custom_call_target="tpu_custom_call" | custom-call | tf_op jit(solution)/shard_map/transform/pallas_call | solution.py:324
  16.7 3.7 %collective-permute-start.14 = (bf16[528,128]{1,0:T(8,128)(2,1)S(1)}, bf16[528,128]{1,0:T(8,128)(2,1)S(1)}, u32[]{:S(2)}, u32[]{:S(2)}) collective-permute-start(bf16[528,128]{1,0:T(8,128)(2,1)S(1)} %transform.1.refs_0_), channel_id=1, source_target_pairs={{0,24},{4,28},{8,16},{12,20},{16,8},{20,12},{24,0},{28,4},{1,25},{... | collective-permute-start | bytes 405512 | tf_op jit(solution)/shard_map/ppermute | solution.py:279
  20.4 0.0 collective-permute-start.12
  20.4 0.8 %collective-permute-start.10 = (bf16[528,128]{1,0:T(8,128)(2,1)S(1)}, bf16[528,128]{1,0:T(8,128)(2,1)S(1)}, u32[]{:S(2)}, u32[]{:S(2)}) collective-permute-start(bf16[528,128]{1,0:T(8,128)(2,1)S(1)} %transform.1.refs_0_), channel_id=1, source_target_pairs={{0,8},{4,12},{8,0},{12,4},{16,24},{20,28},{24,16},{28,20},{1,9},{5... | collective-permute-start | bytes 405512 | tf_op jit(solution)/shard_map/ppermute | solution.py:279
  21.2 0.0 collective-permute-start.9
  21.2 3.9 %collective-permute-done.14.refs_6_ = bf16[528,128]{1,0:T(8,128)(2,1)S(1)} collective-permute-done((bf16[528,128]{1,0:T(8,128)(2,1)S(1)}, bf16[528,128]{1,0:T(8,128)(2,1)S(1)}, u32[]{:S(2)}, u32[]{:S(2)}) %collective-permute-start.14) | collective-permute-done | bytes 135200 | tf_op jit(solution)/shard_map/ppermute | solution.py:279
  25.1 0.0 collective-permute-start.15
  25.1 6.6 %collective-permute-done.12.refs_4_ = bf16[528,128]{1,0:T(8,128)(2,1)S(1)} collective-permute-done((bf16[528,128]{1,0:T(8,128)(2,1)S(1)}, bf16[528,128]{1,0:T(8,128)(2,1)S(1)}, u32[]{:S(2)}, u32[]{:S(2)}) %collective-permute-start.12) | collective-permute-done | bytes 135200 | tf_op jit(solution)/shard_map/ppermute | solution.py:279
  31.7 0.0 collective-permute-start.13
  31.7 0.0 collective-permute-done.10.refs_2_
  31.7 0.5 %collective-permute-start.11 = (bf16[528,128]{1,0:T(8,128)(2,1)S(1)}, bf16[528,128]{1,0:T(8,128)(2,1)S(1)}, u32[]{:S(2)}, u32[]{:S(2)}) collective-permute-start(bf16[528,128]{1,0:T(8,128)(2,1)S(1)} %collective-permute-done.10.refs_2_), channel_id=1, source_target_pairs={{0,4},{4,0},{8,12},{12,8},{16,20},{20,16},{24,28},{28,24},{1,5},{5... | collective-permute-start | bytes 405512 | tf_op jit(solution)/shard_map/ppermute | solution.py:279
  32.2 0.0 collective-permute-done.9.refs_1_
  32.2 0.0 collective-permute-done.15.refs_7_
  32.2 0.8 %collective-permute-done.13.refs_5_ = bf16[528,128]{1,0:T(8,128)(2,1)S(1)} collective-permute-done((bf16[528,128]{1,0:T(8,128)(2,1)S(1)}, bf16[528,128]{1,0:T(8,128)(2,1)S(1)}, u32[]{:S(2)}, u32[]{:S(2)}) %collective-permute-start.13) | collective-permute-done | bytes 135200 | tf_op jit(solution)/shard_map/ppermute | solution.py:279
  33.1 0.2 collective-permute-done.11.refs_3_
  33.3 1.1 %contract.1 = f32[16,16]{1,0:T(8,128)S(1)} custom-call(bf16[528,128]{1,0:T(8,128)(2,1)S(1)} %transform.1.refs_0_, bf16[528,128]{1,0:T(8,128)(2,1)S(1)} %collective-permute-done.9.refs_1_, bf16[528,128]{1,0:T(8,128)(2,1)S(1)} %collective-permute-done.10.refs_2_, bf16[528,128]{1,0:T(8,128)(2,1)S(1)} %collective-permute-done.11.refs_3_, ...), custom_call_target="tpu_custom_call" | custom-call | tf_op jit(solution)/shard_map/contract/pallas_call | solution.py:344
  34.4 2.3 %collective-permute-start.18 = (f32[16,16]{1,0:T(8,128)S(1)}, f32[16,16]{1,0:T(8,128)S(1)}, u32[]{:S(2)}, u32[]{:S(2)}) collective-permute-start(f32[16,16]{1,0:T(8,128)S(1)} %contract.1), channel_id=1, source_target_pairs={{0,3},{1,2},{2,1},{3,0},{4,7},{5,6},{6,5},{7,4},{8,11},{9,10},{10,... | collective-permute-start | bytes 3080 | tf_op jit(solution)/shard_map/ppermute | solution.py:279
  36.6 0.9 %collective-permute-start.17 = (f32[16,16]{1,0:T(8,128)S(1)}, f32[16,16]{1,0:T(8,128)S(1)}, u32[]{:S(2)}, u32[]{:S(2)}) collective-permute-start(f32[16,16]{1,0:T(8,128)S(1)} %contract.1), channel_id=1, source_target_pairs={{0,2},{1,3},{2,0},{3,1},{4,6},{5,7},{6,4},{7,5},{8,10},{9,11},{10,... | collective-permute-start | bytes 3080 | tf_op jit(solution)/shard_map/ppermute | solution.py:279
  37.5 0.3 collective-permute-start.16
  37.9 1.1 %collective-permute-done.18 = f32[16,16]{1,0:T(8,128)S(1)} collective-permute-done((f32[16,16]{1,0:T(8,128)S(1)}, f32[16,16]{1,0:T(8,128)S(1)}, u32[]{:S(2)}, u32[]{:S(2)}) %collective-permute-start.18) | collective-permute-done | bytes 1056 | tf_op jit(solution)/shard_map/ppermute | solution.py:279
  38.9 1.3 %collective-permute-done.17 = f32[16,16]{1,0:T(8,128)S(1)} collective-permute-done((f32[16,16]{1,0:T(8,128)S(1)}, f32[16,16]{1,0:T(8,128)S(1)}, u32[]{:S(2)}, u32[]{:S(2)}) %collective-permute-start.17) | collective-permute-done | bytes 1056 | tf_op jit(solution)/shard_map/ppermute | solution.py:279
  40.3 0.9 %collective-permute-done.16 = f32[16,16]{1,0:T(8,128)S(1)} collective-permute-done((f32[16,16]{1,0:T(8,128)S(1)}, f32[16,16]{1,0:T(8,128)S(1)}, u32[]{:S(2)}, u32[]{:S(2)}) %collective-permute-start.16) | collective-permute-done | bytes 1056 | tf_op jit(solution)/shard_map/ppermute | solution.py:279
  41.2 0.6 %add_add_fusion = f32[16,16]{1,0:T(8,128)} fusion(f32[16,16]{1,0:T(8,128)S(1)} %collective-permute-done.17, f32[16,16]{1,0:T(8,128)S(1)} %collective-permute-done.18, f32[16,16]{1,0:T(8,128)S(1)} %contract.1, f32[16,16]{1,0:T(8,128)S(1)} %collective-permute-done.16), kind=kLoop, calls=%fused_computation | loop fusion | flops 768 | bytes 5120 | tf_op jit(solution)/shard_map/add | solution.py:354
Async XLA Ops:
  1.3 8.0 %collective-permute-start.5 = (bf16[272,128]{1,0:T(8,128)(2,1)S(1)}, bf16[272,128]{1,0:T(8,128)(2,1)S(1)}, u32[]{:S(2)}, u32[]{:S(2)}) collective-permute-start(bf16[272,128]{1,0:T(8,128)(2,1)S(1)} %get-tuple-element.15), channel_id=1, source_target_pairs={{0,3},{1,2},{2,1},{3,0},{4,7},{5,6},{6,5},{7,4},{8,11},{9,10},{10,... | collective-permute-start | bytes 208904 | tf_op jit(solution)/shard_map/ppermute | solution.py:279
  5.3 8.5 %collective-permute-start.2 = (bf16[528,128]{1,0:T(8,128)(2,1)S(1)}, bf16[528,128]{1,0:T(8,128)(2,1)S(1)}, u32[]{:S(2)}, u32[]{:S(2)}) collective-permute-start(bf16[528,128]{1,0:T(8,128)(2,1)S(1)} %get-tuple-element.13._.refs_0_), channel_id=1, source_target_pairs={{0,3},{1,2},{2,1},{3,0},{4,7},{5,6},{6,5},{7,4},{8,11},{9,10},{10,... | collective-permute-start | bytes 405512 | tf_op jit(solution)/shard_map/ppermute | solution.py:279
  5.3 7.2 %collective-permute-start.4 = (bf16[272,128]{1,0:T(8,128)(2,1)S(1)}, bf16[272,128]{1,0:T(8,128)(2,1)S(1)}, u32[]{:S(2)}, u32[]{:S(2)}) collective-permute-start(bf16[272,128]{1,0:T(8,128)(2,1)S(1)} %get-tuple-element.15), channel_id=1, source_target_pairs={{0,2},{1,3},{2,0},{3,1},{4,6},{5,7},{6,4},{7,5},{8,10},{9,11},{10,... | collective-permute-start | bytes 208904 | tf_op jit(solution)/shard_map/ppermute | solution.py:279
  7.3 6.0 %collective-permute-start.3 = (bf16[272,128]{1,0:T(8,128)(2,1)S(1)}, bf16[272,128]{1,0:T(8,128)(2,1)S(1)}, u32[]{:S(2)}, u32[]{:S(2)}) collective-permute-start(bf16[272,128]{1,0:T(8,128)(2,1)S(1)} %get-tuple-element.15), channel_id=1, source_target_pairs={{0,1},{1,0},{2,3},{3,2},{4,5},{5,4},{6,7},{7,6},{8,9},{9,8},{10,11... | collective-permute-start | bytes 208904 | tf_op jit(solution)/shard_map/ppermute | solution.py:279
  8.7 6.1 %collective-permute-start.1 = (bf16[528,128]{1,0:T(8,128)(2,1)S(1)}, bf16[528,128]{1,0:T(8,128)(2,1)S(1)}, u32[]{:S(2)}, u32[]{:S(2)}) collective-permute-start(bf16[528,128]{1,0:T(8,128)(2,1)S(1)} %get-tuple-element.13._.refs_0_), channel_id=1, source_target_pairs={{0,2},{1,3},{2,0},{3,1},{4,6},{5,7},{6,4},{7,5},{8,10},{9,11},{10,... | collective-permute-start | bytes 405512 | tf_op jit(solution)/shard_map/ppermute | solution.py:279
  9.3 6.1 %collective-permute-start = (bf16[528,128]{1,0:T(8,128)(2,1)S(1)}, bf16[528,128]{1,0:T(8,128)(2,1)S(1)}, u32[]{:S(2)}, u32[]{:S(2)}) collective-permute-start(bf16[528,128]{1,0:T(8,128)(2,1)S(1)} %get-tuple-element.13._.refs_0_), channel_id=1, source_target_pairs={{0,1},{1,0},{2,3},{3,2},{4,5},{5,4},{6,7},{7,6},{8,9},{9,8},{10,11... | collective-permute-start | bytes 405512 | tf_op jit(solution)/shard_map/ppermute | solution.py:279
  13.2 2.2 %collective-permute-start.6 = (bf16[272,128]{1,0:T(8,128)(2,1)S(1)}, bf16[272,128]{1,0:T(8,128)(2,1)S(1)}, u32[]{:S(2)}, u32[]{:S(2)}) collective-permute-start(bf16[272,128]{1,0:T(8,128)(2,1)S(1)} %collective-permute-done.3.refs_5_), channel_id=1, source_target_pairs={{0,4},{4,0},{8,12},{12,8},{16,20},{20,16},{24,28},{28,24},{1,5},{5... | collective-permute-start | bytes 208904 | tf_op jit(solution)/shard_map/ppermute | solution.py:279
  13.2 2.2 %collective-permute-start.7 = (bf16[272,128]{1,0:T(8,128)(2,1)S(1)}, bf16[272,128]{1,0:T(8,128)(2,1)S(1)}, u32[]{:S(2)}, u32[]{:S(2)}) collective-permute-start(bf16[272,128]{1,0:T(8,128)(2,1)S(1)} %collective-permute-done.4.refs_6_), channel_id=1, source_target_pairs={{0,4},{4,0},{8,12},{12,8},{16,20},{20,16},{24,28},{28,24},{1,5},{5... | collective-permute-start | bytes 208904 | tf_op jit(solution)/shard_map/ppermute | solution.py:279
  13.7 1.7 %collective-permute-start.8 = (bf16[272,128]{1,0:T(8,128)(2,1)S(1)}, bf16[272,128]{1,0:T(8,128)(2,1)S(1)}, u32[]{:S(2)}, u32[]{:S(2)}) collective-permute-start(bf16[272,128]{1,0:T(8,128)(2,1)S(1)} %collective-permute-done.5.refs_7_), channel_id=1, source_target_pairs={{0,4},{4,0},{8,12},{12,8},{16,20},{20,16},{24,28},{28,24},{1,5},{5... | collective-permute-start | bytes 208904 | tf_op jit(solution)/shard_map/ppermute | solution.py:279
  16.7 8.4 %collective-permute-start.14 = (bf16[528,128]{1,0:T(8,128)(2,1)S(1)}, bf16[528,128]{1,0:T(8,128)(2,1)S(1)}, u32[]{:S(2)}, u32[]{:S(2)}) collective-permute-start(bf16[528,128]{1,0:T(8,128)(2,1)S(1)} %transform.1.refs_0_), channel_id=1, source_target_pairs={{0,24},{4,28},{8,16},{12,20},{16,8},{20,12},{24,0},{28,4},{1,25},{... | collective-permute-start | bytes 405512 | tf_op jit(solution)/shard_map/ppermute | solution.py:279
  20.4 11.3 %collective-permute-start.12 = (bf16[528,128]{1,0:T(8,128)(2,1)S(1)}, bf16[528,128]{1,0:T(8,128)(2,1)S(1)}, u32[]{:S(2)}, u32[]{:S(2)}) collective-permute-start(bf16[528,128]{1,0:T(8,128)(2,1)S(1)} %transform.1.refs_0_), channel_id=1, source_target_pairs={{0,16},{4,20},{8,24},{12,28},{16,0},{20,4},{24,8},{28,12},{1,17},{... | collective-permute-start | bytes 405512 | tf_op jit(solution)/shard_map/ppermute | solution.py:279
  20.4 11.3 %collective-permute-start.10 = (bf16[528,128]{1,0:T(8,128)(2,1)S(1)}, bf16[528,128]{1,0:T(8,128)(2,1)S(1)}, u32[]{:S(2)}, u32[]{:S(2)}) collective-permute-start(bf16[528,128]{1,0:T(8,128)(2,1)S(1)} %transform.1.refs_0_), channel_id=1, source_target_pairs={{0,8},{4,12},{8,0},{12,4},{16,24},{20,28},{24,16},{28,20},{1,9},{5... | collective-permute-start | bytes 405512 | tf_op jit(solution)/shard_map/ppermute | solution.py:279
  21.2 11.1 %collective-permute-start.9 = (bf16[528,128]{1,0:T(8,128)(2,1)S(1)}, bf16[528,128]{1,0:T(8,128)(2,1)S(1)}, u32[]{:S(2)}, u32[]{:S(2)}) collective-permute-start(bf16[528,128]{1,0:T(8,128)(2,1)S(1)} %transform.1.refs_0_), channel_id=1, source_target_pairs={{0,4},{4,0},{8,12},{12,8},{16,20},{20,16},{24,28},{28,24},{1,5},{5... | collective-permute-start | bytes 405512 | tf_op jit(solution)/shard_map/ppermute | solution.py:279
  25.1 7.1 %collective-permute-start.15 = (bf16[528,128]{1,0:T(8,128)(2,1)S(1)}, bf16[528,128]{1,0:T(8,128)(2,1)S(1)}, u32[]{:S(2)}, u32[]{:S(2)}) collective-permute-start(bf16[528,128]{1,0:T(8,128)(2,1)S(1)} %collective-permute-done.14.refs_6_), channel_id=1, source_target_pairs={{0,4},{4,0},{8,12},{12,8},{16,20},{20,16},{24,28},{28,24},{1,5},{5... | collective-permute-start | bytes 405512 | tf_op jit(solution)/shard_map/ppermute | solution.py:279
  31.7 1.4 %collective-permute-start.13 = (bf16[528,128]{1,0:T(8,128)(2,1)S(1)}, bf16[528,128]{1,0:T(8,128)(2,1)S(1)}, u32[]{:S(2)}, u32[]{:S(2)}) collective-permute-start(bf16[528,128]{1,0:T(8,128)(2,1)S(1)} %collective-permute-done.12.refs_4_), channel_id=1, source_target_pairs={{0,4},{4,0},{8,12},{12,8},{16,20},{20,16},{24,28},{28,24},{1,5},{5... | collective-permute-start | bytes 405512 | tf_op jit(solution)/shard_map/ppermute | solution.py:279
  31.7 1.5 %collective-permute-start.11 = (bf16[528,128]{1,0:T(8,128)(2,1)S(1)}, bf16[528,128]{1,0:T(8,128)(2,1)S(1)}, u32[]{:S(2)}, u32[]{:S(2)}) collective-permute-start(bf16[528,128]{1,0:T(8,128)(2,1)S(1)} %collective-permute-done.10.refs_2_), channel_id=1, source_target_pairs={{0,4},{4,0},{8,12},{12,8},{16,20},{20,16},{24,28},{28,24},{1,5},{5... | collective-permute-start | bytes 405512 | tf_op jit(solution)/shard_map/ppermute | solution.py:279
  34.4 4.6 %collective-permute-start.18 = (f32[16,16]{1,0:T(8,128)S(1)}, f32[16,16]{1,0:T(8,128)S(1)}, u32[]{:S(2)}, u32[]{:S(2)}) collective-permute-start(f32[16,16]{1,0:T(8,128)S(1)} %contract.1), channel_id=1, source_target_pairs={{0,3},{1,2},{2,1},{3,0},{4,7},{5,6},{6,5},{7,4},{8,11},{9,10},{10,... | collective-permute-start | bytes 3080 | tf_op jit(solution)/shard_map/ppermute | solution.py:279
  36.6 3.7 %collective-permute-start.17 = (f32[16,16]{1,0:T(8,128)S(1)}, f32[16,16]{1,0:T(8,128)S(1)}, u32[]{:S(2)}, u32[]{:S(2)}) collective-permute-start(f32[16,16]{1,0:T(8,128)S(1)} %contract.1), channel_id=1, source_target_pairs={{0,2},{1,3},{2,0},{3,1},{4,6},{5,7},{6,4},{7,5},{8,10},{9,11},{10,... | collective-permute-start | bytes 3080 | tf_op jit(solution)/shard_map/ppermute | solution.py:279
  37.5 3.7 %collective-permute-start.16 = (f32[16,16]{1,0:T(8,128)S(1)}, f32[16,16]{1,0:T(8,128)S(1)}, u32[]{:S(2)}, u32[]{:S(2)}) collective-permute-start(f32[16,16]{1,0:T(8,128)S(1)} %contract.1), channel_id=1, source_target_pairs={{0,1},{1,0},{2,3},{3,2},{4,5},{5,4},{6,7},{7,6},{8,9},{9,8},{10,11... | collective-permute-start | bytes 3080 | tf_op jit(solution)/shard_map/ppermute | solution.py:279

commit v4 on v2

--- a/solution.py
+++ b/solution.py
@@ -7,12 +7,17 @@
 from jax.experimental.pallas import tpu as pltpu
 from jax.sharding import PartitionSpec as P
 
+
 ATOM_BS = 16
 TILE = 16
 
 
 def top_bit(k):
     return k.bit_length() - 1
+
+
+def shared(k, ao):
+    return ao == 4 and k == 3
 
 
 def which(a, k):
@@ -36,7 +41,8 @@
 
 
 def prep_kernel(*refs):
-    hbm, (pay_ref, screen_ref), copied, mask_ref, sems = refs[:5], refs[5:7], refs[7:12], refs[12], refs[13]
+    hbm, outs, copied, mask_ref, sems = refs[:5], refs[5:-7], refs[-7:-2], refs[-2], refs[-1]
+    own_ref, screen_ref, pay_refs = outs[0], outs[1], outs[2:]
     copies = [pltpu.make_async_copy(src, dst, sems.at[i]) for i, (src, dst) in enumerate(zip(hbm, copied))]
     for copy in copies:
         copy.start()
@@ -72,41 +78,80 @@
     live = (slot_row < size_row) & (slot_col < size_col)
     mask_ref[...] = jnp.where(live, kept, 0.0).astype(bf16)
     below, on = tri_masks(block)
-    half = ao * block + TILE
     for copy in copies[2:]:
         copy.wait()
+    slab_blocks, green_blocks = [], []
+    for k in range(ao):
+        screen = block_at(mask_ref, a ^ k, block)
+        span = slice(k * block, (k + 1) * block)
+        screen_ref[:, span] = screen
+        cols = pl.ds(pl.multiple_of((a ^ k) * block, block), block)
+        slabs = [slab_ref[q, :, cols] * screen for q in range(2)]
+        greens = [occ_ref[:, cols], virt_ref[:, cols]]
+        own_ref[0, :, span], own_ref[1, :, span] = slabs
+        own_ref[2, :, span], own_ref[3, :, span] = greens
+        if k == 0:
+            folded = [fold_diagonal(x.astype(f32), y.astype(f32), below, on) for x, y in (slabs, greens)]
+        else:
+            first = which(a, k) == 0
+            slab_blocks.append(jnp.where(first, *slabs))
+            green_blocks.append(jnp.where(first, *greens))
+    tails = []
+    for (block_part, diagonal), blocks in zip(folded, (slab_blocks, green_blocks)):
+        blocks.append(block_part.astype(bf16))
+        tails.append(jnp.broadcast_to(diagonal, (TILE, block)).astype(bf16))
+
+    def put(ref, at, parts, tail):
+        for part in parts + [tail]:
+            ref[at : at + part.shape[0], :] = part
+            at += part.shape[0]
+        return at
+
+    even = (lax.axis_index("ri") & 1) == 0
+    rows = block // 2
     for k in range(1, ao):
-        screen = block_at(mask_ref, a ^ k, block)
-        screen_ref[:, k * block : (k + 1) * block] = screen
-        matrix = which(a, k)
-        start = (k - 1) * block
-        cols = pl.ds(pl.multiple_of((a ^ k) * block, block), block)
-        pay_ref[start : start + block, :] = slab_ref[matrix, :, cols] * screen
-        pay_ref[half + start : half + start + block, :] = jnp.where(
-            matrix == 0, occ_ref[:, cols], virt_ref[:, cols]
-        )
-    screen = block_at(mask_ref, a, block)
-    screen_ref[:, 0:block] = screen
-    own = pl.ds(pl.multiple_of(a * block, block), block)
-    start = (ao - 1) * block
-    pairs = (
-        (start, (slab_ref[0, :, own] * screen).astype(f32), (slab_ref[1, :, own] * screen).astype(f32)),
-        (half + start, occ_ref[:, own].astype(f32), virt_ref[:, own].astype(f32)),
-    )
-    for at, first, second in pairs:
-        folded, diagonal = fold_diagonal(first, second, below, on)
-        pay_ref[at : at + block, :] = folded.astype(bf16)
-        pay_ref[at + block : at + block + TILE, :] = jnp.broadcast_to(diagonal, (TILE, block)).astype(bf16)
-
-
-def unfold(pays, base, a, ao, block, put):
+        at = put(pay_refs[k - 1], 0, slab_blocks[: k - 1] + slab_blocks[k:], tails[0])
+        parts = green_blocks[: k - 1] + green_blocks[k:]
+        if shared(k, ao):
+            parts = [jnp.where(even, x[:rows], x[rows:]) for x in parts]
+        put(pay_refs[k - 1], at, parts, tails[1])
+
+
+def reader(ref, base, m, ao, block):
+    def read(k):
+        if k < 0:
+            return ref[base + (ao - 1) * block : base + (ao - 1) * block + TILE, :]
+        at = base + ((ao - 2) if k == 0 else k - 1 - (k > m)) * block
+        return ref[at : at + block, :]
+
+    return read
+
+
+def halves_reader(mine, other, even, base, m, ao, block):
+    here, there = (reader(x, base, m, ao, block // 2) for x in (mine, other))
+
+    def read(k):
+        if k < 0:
+            return here(k)
+        x, y = here(k), there(k)
+        return jnp.concatenate([jnp.where(even, x, y), jnp.where(even, y, x)], axis=0)
+
+    return read
+
+
+def unfold(reads, own, a, ao, block, put):
     below, on = tri_masks(block)
-    for m in range(ao):
+    for q in range(2):
+        for k in range(ao):
+            value = own(q, k)
+            put(q, 0, k, value)
+            if k:
+                put(q, k, 0, value.T)
+    for m in range(1, ao):
         for j in range(m + 1, ao):
             k = m ^ j
-            at = base + (k - 1) * block
-            here = pays[m][at : at + block, :]
-            there = pays[j][at : at + block, :]
+            here = reads[m](k)
+            there = reads[j](k)
             here_t = here.T
             there_t = there.T
             lower = which(a ^ m, k) == 0
@@ -114,10 +159,9 @@
             put(0, j, m, jnp.where(lower, here_t, there))
             put(1, m, j, jnp.where(lower, there_t, here))
             put(1, j, m, jnp.where(lower, there, here_t))
-        at = base + (ao - 1) * block
-        folded = pays[m][at : at + block, :].astype(jnp.float32)
+        folded = reads[m](0).astype(jnp.float32)
         folded_t = folded.T
-        diagonal = pays[m][at + block : at + block + TILE, :].astype(jnp.float32)[0:1]
+        diagonal = reads[m](-1).astype(jnp.float32)[0:1]
         put(0, m, m, jnp.where(below | on, folded, folded_t).astype(jnp.bfloat16))
         put(
             1, m, m,
@@ -128,12 +172,21 @@
 
 
 def transform_kernel(ao, block, *refs):
-    pays = refs[:ao]
-    screen_ref, _, out_ref, slab_ref, green_ref, left_ref = refs[ao:]
+    own_ref, screen_ref, _, out_ref, slab_ref, green_ref, left_ref = refs[-7:]
+    pays = refs[:-7]
     total = ao * block
     a = lax.axis_index("ao")
-    half = total + TILE
     f32, bf16 = jnp.float32, jnp.bfloat16
+    size = (ao - 1) * block + TILE
+    pays, others = pays[: ao - 1], list(pays[ao - 1 :])
+    even = (lax.axis_index("ri") & 1) == 0
+    slabs, greens = [None], [None]
+    for m, x in enumerate(pays, 1):
+        slabs.append(reader(x, 0, m, ao, block))
+        if shared(m, ao):
+            greens.append(halves_reader(x, others.pop(0), even, size, m, ao, block))
+        else:
+            greens.append(reader(x, size, m, ao, block))
 
     def put_slab(matrix, row, col, value):
         slab_ref[matrix, row * block : (row + 1) * block, col * block : (col + 1) * block] = value
@@ -142,8 +195,11 @@
         at = (total if matrix == 0 else 0) + col * block
         green_ref[row, :, at : at + block] = value
 
-    unfold(pays, half, a, ao, block, put_green)
-    unfold(pays, 0, a, ao, block, put_slab)
+    def own(first):
+        return lambda q, k: own_ref[first + q, :, k * block : (k + 1) * block]
+
+    unfold(greens, own(2), a, ao, block, put_green)
+    unfold(slabs, own(0), a, ao, block, put_slab)
     both = jnp.concatenate([green_ref[0, :, total:], green_ref[0, :, :total]], axis=0)
     for q in range(2):
         left = jnp.dot(both, slab_ref[q], preferred_element_type=f32).astype(bf16)
@@ -269,20 +325,24 @@
         pltpu.with_memory_space_constraint(x, pltpu.HBM)
         for x in (atom_sizes.reshape(1, atoms), pattern, slab_tensor, occ_green, virt_green)
     )
-    pay, screen = pl.pallas_call(
+    size = (ao - 1) * block + TILE
+    sizes = [size + (size - (ao - 1) * block // 2 if shared(k, ao) else size) for k in range(1, ao)]
+    prepared = pl.pallas_call(
         prep_kernel,
-        out_shape=(
-            jax.ShapeDtypeStruct((2 * half, block), bf16),
-            jax.ShapeDtypeStruct((block, total), bf16),
-        ),
+        out_shape=[jax.ShapeDtypeStruct((4, block, total), bf16), jax.ShapeDtypeStruct((block, total), bf16)]
+        + [jax.ShapeDtypeStruct((rows, block), bf16) for rows in sizes],
         in_specs=[pl.BlockSpec(memory_space=pltpu.HBM)] * 5,
-        out_specs=(vmem, vmem),
+        out_specs=[vmem] * (2 + len(sizes)),
         scratch_shapes=[pltpu.VMEM(x.shape, x.dtype) for x in inputs]
         + [pltpu.VMEM((block, total), bf16), pltpu.SemaphoreType.DMA((5,))],
-        compiler_params=room((4 * half, block), (3 * block, total), (2 * block, 2 * total)),
+        compiler_params=room((sum(sizes), block), (5 * block, total), (2 * block, 2 * total)),
         name="prep",
     )(*inputs)
-    pays = [pay] + [exchange(pay, "ao", ao, k) for k in range(1, ao)]
+    own, screen, *pays = prepared
+    arrived = []
+    for k, pay in enumerate(pays, 1):
+        arrived.append(exchange(pay, "ao", ao, k))
+    pays = arrived + [exchange(x, "ri", ri, 1) for k, x in enumerate(arrived, 1) if shared(k, ao)]
     groups = block // TILE
     staged = pl.pallas_call(
         stage_kernel,
@@ -293,20 +353,20 @@
         compiler_params=room((2 * ri_rows, block, total)),
         cost_estimate=pl.CostEstimate(flops=0, transcendentals=0, bytes_accessed=8 * ri_rows * block * total),
         name="stage",
-    )(pltpu.with_memory_space_constraint(three_center, pltpu.HBM), pay)
+    )(pltpu.with_memory_space_constraint(three_center, pltpu.HBM), screen)
     weighted = pl.pallas_call(
         lambda *refs: transform_kernel(ao, block, *refs),
         out_shape=jax.ShapeDtypeStruct((half, block), bf16),
-        in_specs=[vmem] * (ao + 1) + [pl.BlockSpec(memory_space=pl.ANY)],
+        in_specs=[vmem] * (len(pays) + 2) + [pl.BlockSpec(memory_space=pl.ANY)],
         out_specs=vmem,
         scratch_shapes=[
             pltpu.VMEM((2, total, total), bf16),
             pltpu.VMEM((ao, block, 2 * total), bf16),
             pltpu.VMEM((2, block, 2 * total), bf16),
         ],
-        compiler_params=room((2 * half * ao, block), (2, total, total), (ao, block, 2 * total), (4, block, total)),
+        compiler_params=room((sum(sizes), block), (4 * block, total), (2, total, total), (ao, block, 2 * total), (4, block, total)),
         name="transform",
-    )(*pays, screen, staged)
+    )(*pays, own, screen, staged)
     sources = [weighted]
     for k in range(2, ri, 2):
         sources.append(exchange(weighted, "ri", ri, k))

time: 44.3 us -> 40.1 us (0.905)
  waiting for transfers between devices: 24.6 us -> 20.3 us
    ppermute x13 -> x14, waiting for transfers between devices: 24.6 us -> 20.3 us  [exchange(): return lax.ppermute(value, axis, [(i, i ^ k) for i in range(size)])]
    ppermute x13 -> x14, starting transfers between devices: 13.1 us -> 13.1 us  [exchange(): return lax.ppermute(value, axis, [(i, i ^ k) for i in range(size)])]
  transfers between devices with their start and end apart: 13 -> 14, of which waited for: 10 -> 9; matrix products, arithmetic and copies ran while one was open for 0% -> 0% of each run, Pallas kernels for 5% -> 5%
where the time goes in v4:
time: 40.1 us; the launch traced here: 39.9 us
  waiting for transfers between devices  20.3 us (51%)
  starting transfers between devices  13.1 us (33%)
  Pallas kernels  5.82 us (15%)
  other arithmetic  0.6 us (1%)
    ppermute x14, waiting for transfers between devices, exchange(): return lax.ppermute(value, axis, [(i, i ^ k) for i in range(size)])  20.3 us
    ppermute x14, starting transfers between devices, exchange(): return lax.ppermute(value, axis, [(i, i ^ k) for i in range(size)])  13.1 us
    pallas_call x1, Pallas kernels, shards(): pl.pallas_call(stage_kernel, out_shape=jax.ShapeDtypeStruct((ao, ri_rows...  2.17 us
    pallas_call x1, Pallas kernels, shards(): pl.pallas_call(prep_kernel, out_shape=[jax.ShapeDtypeStruct((4, block, to...  1.34 us
    pallas_call x1, Pallas kernels, shards(): pl.pallas_call(lambda *refs: transform_kernel(ao, block, *refs), out_shap...  1.21 us
    pallas_call x1, Pallas kernels, shards(): pl.pallas_call(lambda *refs: contract_kernel(ri, ao, block, *refs), out_s...  1.1 us
  transfers between devices with their start and end apart: 14, of which 9 were waited for; matrix products, arithmetic and copies ran while one was open for 0% of the time, Pallas kernels for 5%

profile of v4, /device:TPU:0, one launch (start us, length us, event | category | flops | bytes accessed | tf_op | source)
XLA Modules:
  0.0 39.9 jit_solution(10367709786890938092)
XLA Ops:
  0.0 1.3 %prep.1 = (bf16[4,128,512]{2,1,0:T(8,128)(2,1)S(1)}, bf16[128,512]{1,0:T(8,128)(2,1)S(1)}, bf16[800,128]{1,0:T(8,128)(2,1)S(1)}, bf16[800,128]{1,0:T(8,128)(2,1)S(1)}, bf16[608,128]{1,0:T(8,128)(2,1)S(1)}) custom-call(s32[1,32]{1,0:T(1,128)} %bitcast.1, s32[32,32]{1,0:T(8,128)} %refs_1_.1, bf16[2,128,512]{2,1,0:T(8,128)(2,1)} %refs_2_.1, ...), custom_call_target="tpu_custom_call" | custom-call | tf_op jit(solution)/shard_map/prep/pallas_call | solution.py:330
  1.3 4.0 %collective-permute-start.2 = (bf16[608,128]{1,0:T(8,128)(2,1)S(1)}, bf16[608,128]{1,0:T(8,128)(2,1)S(1)}, u32[]{:S(2)}, u32[]{:S(2)}) collective-permute-start(bf16[608,128]{1,0:T(8,128)(2,1)S(1)} %get-tuple-element.12), channel_id=1, source_target_pairs={{0,3},{1,2},{2,1},{3,0},{4,7},{5,6},{6,5},{7,4},{8,11},{9,10},{10,... | collective-permute-start | bytes 466952 | tf_op jit(solution)/shard_map/ppermute | solution.py:313
  5.3 0.5 %collective-permute-start = (bf16[800,128]{1,0:T(8,128)(2,1)S(1)}, bf16[800,128]{1,0:T(8,128)(2,1)S(1)}, u32[]{:S(2)}, u32[]{:S(2)}) collective-permute-start(bf16[800,128]{1,0:T(8,128)(2,1)S(1)} %get-tuple-element.10), channel_id=1, source_target_pairs={{0,1},{1,0},{2,3},{3,2},{4,5},{5,4},{6,7},{7,6},{8,9},{9,8},{10,11... | collective-permute-start | bytes 614408 | tf_op jit(solution)/shard_map/ppermute | solution.py:313
  5.9 0.1 collective-permute-start.1
  6.0 4.2 %collective-permute-done.2.refs_2_ = bf16[608,128]{1,0:T(8,128)(2,1)S(1)} collective-permute-done((bf16[608,128]{1,0:T(8,128)(2,1)S(1)}, bf16[608,128]{1,0:T(8,128)(2,1)S(1)}, u32[]{:S(2)}, u32[]{:S(2)}) %collective-permute-start.2) | collective-permute-done | bytes 155680 | tf_op jit(solution)/shard_map/ppermute | solution.py:313
  10.2 0.0 collective-permute-start.3
  10.2 2.2 %stage.1.refs_6_.refs_8_ = bf16[4,256,1024]{2,1,0:T(8,128)(2,1)S(1)} custom-call(bf16[16,128,512]{2,1,0:T(8,128)(2,1)} %tensor_hbm.1, bf16[128,512]{1,0:T(8,128)(2,1)S(1)} %get-tuple-element.14._.refs_5_), custom_call_target="tpu_custom_call" | custom-call | bytes 8388608 | tf_op jit(solution)/shard_map/stage/pallas_call | solution.py:347
  12.4 1.6 %collective-permute-done.refs_0_ = bf16[800,128]{1,0:T(8,128)(2,1)S(1)} collective-permute-done((bf16[800,128]{1,0:T(8,128)(2,1)S(1)}, bf16[800,128]{1,0:T(8,128)(2,1)S(1)}, u32[]{:S(2)}, u32[]{:S(2)}) %collective-permute-start) | collective-permute-done | bytes 204832 | tf_op jit(solution)/shard_map/ppermute | solution.py:313
  14.0 0.0 collective-permute-done.1.refs_1_
  14.0 0.0 collective-permute-done.3.refs_3_
  14.0 1.2 %transform.1.refs_0_ = bf16[528,128]{1,0:T(8,128)(2,1)S(1)} custom-call(bf16[800,128]{1,0:T(8,128)(2,1)S(1)} %collective-permute-done.refs_0_, bf16[800,128]{1,0:T(8,128)(2,1)S(1)} %collective-permute-done.1.refs_1_, bf16[608,128]{1,0:T(8,128)(2,1)S(1)} %collective-permute-done.2.refs_2_, bf16[608,128]{1,0:T(8,128)(2,1)S(1)} %collective-permute-done.3.refs_3_, ...), custom_call_target="tpu_custom_call" | custom-call | tf_op jit(solution)/shard_map/transform/pallas_call | solution.py:357
  15.3 3.7 %collective-permute-start.9 = (bf16[528,128]{1,0:T(8,128)(2,1)S(1)}, bf16[528,128]{1,0:T(8,128)(2,1)S(1)}, u32[]{:S(2)}, u32[]{:S(2)}) collective-permute-start(bf16[528,128]{1,0:T(8,128)(2,1)S(1)} %transform.1.refs_0_), channel_id=1, source_target_pairs={{0,24},{4,28},{8,16},{12,20},{16,8},{20,12},{24,0},{28,4},{1,25},{... | collective-permute-start | bytes 405512 | tf_op jit(solution)/shard_map/ppermute | solution.py:313
  18.9 0.0 collective-permute-start.7
  18.9 0.8 %collective-permute-start.5 = (bf16[528,128]{1,0:T(8,128)(2,1)S(1)}, bf16[528,128]{1,0:T(8,128)(2,1)S(1)}, u32[]{:S(2)}, u32[]{:S(2)}) collective-permute-start(bf16[528,128]{1,0:T(8,128)(2,1)S(1)} %transform.1.refs_0_), channel_id=1, source_target_pairs={{0,8},{4,12},{8,0},{12,4},{16,24},{20,28},{24,16},{28,20},{1,9},{5... | collective-permute-start | bytes 405512 | tf_op jit(solution)/shard_map/ppermute | solution.py:313
  19.7 0.0 collective-permute-start.4
  19.7 3.9 %collective-permute-done.9.refs_6_ = bf16[528,128]{1,0:T(8,128)(2,1)S(1)} collective-permute-done((bf16[528,128]{1,0:T(8,128)(2,1)S(1)}, bf16[528,128]{1,0:T(8,128)(2,1)S(1)}, u32[]{:S(2)}, u32[]{:S(2)}) %collective-permute-start.9) | collective-permute-done | bytes 135200 | tf_op jit(solution)/shard_map/ppermute | solution.py:313
  23.6 0.0 collective-permute-start.10
  23.6 6.4 %collective-permute-done.7.refs_4_ = bf16[528,128]{1,0:T(8,128)(2,1)S(1)} collective-permute-done((bf16[528,128]{1,0:T(8,128)(2,1)S(1)}, bf16[528,128]{1,0:T(8,128)(2,1)S(1)}, u32[]{:S(2)}, u32[]{:S(2)}) %collective-permute-start.7) | collective-permute-done | bytes 135200 | tf_op jit(solution)/shard_map/ppermute | solution.py:313
  30.0 0.0 collective-permute-start.8
  30.0 0.0 collective-permute-done.5.refs_2_
  30.0 0.5 %collective-permute-start.6 = (bf16[528,128]{1,0:T(8,128)(2,1)S(1)}, bf16[528,128]{1,0:T(8,128)(2,1)S(1)}, u32[]{:S(2)}, u32[]{:S(2)}) collective-permute-start(bf16[528,128]{1,0:T(8,128)(2,1)S(1)} %collective-permute-done.5.refs_2_), channel_id=1, source_target_pairs={{0,4},{4,0},{8,12},{12,8},{16,20},{20,16},{24,28},{28,24},{1,5},{5... | collective-permute-start | bytes 405512 | tf_op jit(solution)/shard_map/ppermute | solution.py:313
  30.5 0.0 collective-permute-done.4.refs_1_
  30.5 0.0 collective-permute-done.10.refs_7_
  30.5 0.8 %collective-permute-done.8.refs_5_ = bf16[528,128]{1,0:T(8,128)(2,1)S(1)} collective-permute-done((bf16[528,128]{1,0:T(8,128)(2,1)S(1)}, bf16[528,128]{1,0:T(8,128)(2,1)S(1)}, u32[]{:S(2)}, u32[]{:S(2)}) %collective-permute-start.8) | collective-permute-done | bytes 135200 | tf_op jit(solution)/shard_map/ppermute | solution.py:313
  31.4 0.2 collective-permute-done.6.refs_3_
  31.6 1.1 %contract.1 = f32[16,16]{1,0:T(8,128)S(1)} custom-call(bf16[528,128]{1,0:T(8,128)(2,1)S(1)} %transform.1.refs_0_, bf16[528,128]{1,0:T(8,128)(2,1)S(1)} %collective-permute-done.4.refs_1_, bf16[528,128]{1,0:T(8,128)(2,1)S(1)} %collective-permute-done.5.refs_2_, bf16[528,128]{1,0:T(8,128)(2,1)S(1)} %collective-permute-done.6.refs_3_, ...), custom_call_target="tpu_custom_call" | custom-call | tf_op jit(solution)/shard_map/contract/pallas_call | solution.py:377
  32.7 2.9 %collective-permute-start.13 = (f32[16,16]{1,0:T(8,128)S(1)}, f32[16,16]{1,0:T(8,128)S(1)}, u32[]{:S(2)}, u32[]{:S(2)}) collective-permute-start(f32[16,16]{1,0:T(8,128)S(1)} %contract.1), channel_id=1, source_target_pairs={{0,3},{1,2},{2,1},{3,0},{4,7},{5,6},{6,5},{7,4},{8,11},{9,10},{10,... | collective-permute-start | bytes 3080 | tf_op jit(solution)/shard_map/ppermute | solution.py:313
  35.6 0.1 collective-permute-start.12
  35.6 0.5 %collective-permute-start.11 = (f32[16,16]{1,0:T(8,128)S(1)}, f32[16,16]{1,0:T(8,128)S(1)}, u32[]{:S(2)}, u32[]{:S(2)}) collective-permute-start(f32[16,16]{1,0:T(8,128)S(1)} %contract.1), channel_id=1, source_target_pairs={{0,1},{1,0},{2,3},{3,2},{4,5},{5,4},{6,7},{7,6},{8,9},{9,8},{10,11... | collective-permute-start | bytes 3080 | tf_op jit(solution)/shard_map/ppermute | solution.py:313
  36.2 1.1 %collective-permute-done.13 = f32[16,16]{1,0:T(8,128)S(1)} collective-permute-done((f32[16,16]{1,0:T(8,128)S(1)}, f32[16,16]{1,0:T(8,128)S(1)}, u32[]{:S(2)}, u32[]{:S(2)}) %collective-permute-start.13) | collective-permute-done | bytes 1056 | tf_op jit(solution)/shard_map/ppermute | solution.py:313
  37.2 2.0 %collective-permute-done.12 = f32[16,16]{1,0:T(8,128)S(1)} collective-permute-done((f32[16,16]{1,0:T(8,128)S(1)}, f32[16,16]{1,0:T(8,128)S(1)}, u32[]{:S(2)}, u32[]{:S(2)}) %collective-permute-start.12) | collective-permute-done | bytes 1056 | tf_op jit(solution)/shard_map/ppermute | solution.py:313
  39.2 0.1 collective-permute-done.11
  39.3 0.6 %add_add_fusion = f32[16,16]{1,0:T(8,128)} fusion(f32[16,16]{1,0:T(8,128)S(1)} %collective-permute-done.12, f32[16,16]{1,0:T(8,128)S(1)} %collective-permute-done.13, f32[16,16]{1,0:T(8,128)S(1)} %contract.1, f32[16,16]{1,0:T(8,128)S(1)} %collective-permute-done.11), kind=kLoop, calls=%fused_computation | loop fusion | flops 768 | bytes 5120 | tf_op jit(solution)/shard_map/add | solution.py:387
Async XLA Ops:
  1.3 8.9 %collective-permute-start.2 = (bf16[608,128]{1,0:T(8,128)(2,1)S(1)}, bf16[608,128]{1,0:T(8,128)(2,1)S(1)}, u32[]{:S(2)}, u32[]{:S(2)}) collective-permute-start(bf16[608,128]{1,0:T(8,128)(2,1)S(1)} %get-tuple-element.12), channel_id=1, source_target_pairs={{0,3},{1,2},{2,1},{3,0},{4,7},{5,6},{6,5},{7,4},{8,11},{9,10},{10,... | collective-permute-start | bytes 466952 | tf_op jit(solution)/shard_map/ppermute | solution.py:313
  5.3 8.7 %collective-permute-start = (bf16[800,128]{1,0:T(8,128)(2,1)S(1)}, bf16[800,128]{1,0:T(8,128)(2,1)S(1)}, u32[]{:S(2)}, u32[]{:S(2)}) collective-permute-start(bf16[800,128]{1,0:T(8,128)(2,1)S(1)} %get-tuple-element.10), channel_id=1, source_target_pairs={{0,1},{1,0},{2,3},{3,2},{4,5},{5,4},{6,7},{7,6},{8,9},{9,8},{10,11... | collective-permute-start | bytes 614408 | tf_op jit(solution)/shard_map/ppermute | solution.py:313
  5.9 8.2 %collective-permute-start.1 = (bf16[800,128]{1,0:T(8,128)(2,1)S(1)}, bf16[800,128]{1,0:T(8,128)(2,1)S(1)}, u32[]{:S(2)}, u32[]{:S(2)}) collective-permute-start(bf16[800,128]{1,0:T(8,128)(2,1)S(1)} %get-tuple-element.11), channel_id=1, source_target_pairs={{0,2},{1,3},{2,0},{3,1},{4,6},{5,7},{6,4},{7,5},{8,10},{9,11},{10,... | collective-permute-start | bytes 614408 | tf_op jit(solution)/shard_map/ppermute | solution.py:313
  10.2 3.8 %collective-permute-start.3 = (bf16[608,128]{1,0:T(8,128)(2,1)S(1)}, bf16[608,128]{1,0:T(8,128)(2,1)S(1)}, u32[]{:S(2)}, u32[]{:S(2)}) collective-permute-start(bf16[608,128]{1,0:T(8,128)(2,1)S(1)} %collective-permute-done.2.refs_2_), channel_id=1, source_target_pairs={{0,4},{4,0},{8,12},{12,8},{16,20},{20,16},{24,28},{28,24},{1,5},{5... | collective-permute-start | bytes 466952 | tf_op jit(solution)/shard_map/ppermute | solution.py:313
  15.3 8.4 %collective-permute-start.9 = (bf16[528,128]{1,0:T(8,128)(2,1)S(1)}, bf16[528,128]{1,0:T(8,128)(2,1)S(1)}, u32[]{:S(2)}, u32[]{:S(2)}) collective-permute-start(bf16[528,128]{1,0:T(8,128)(2,1)S(1)} %transform.1.refs_0_), channel_id=1, source_target_pairs={{0,24},{4,28},{8,16},{12,20},{16,8},{20,12},{24,0},{28,4},{1,25},{... | collective-permute-start | bytes 405512 | tf_op jit(solution)/shard_map/ppermute | solution.py:313
  18.9 11.1 %collective-permute-start.7 = (bf16[528,128]{1,0:T(8,128)(2,1)S(1)}, bf16[528,128]{1,0:T(8,128)(2,1)S(1)}, u32[]{:S(2)}, u32[]{:S(2)}) collective-permute-start(bf16[528,128]{1,0:T(8,128)(2,1)S(1)} %transform.1.refs_0_), channel_id=1, source_target_pairs={{0,16},{4,20},{8,24},{12,28},{16,0},{20,4},{24,8},{28,12},{1,17},{... | collective-permute-start | bytes 405512 | tf_op jit(solution)/shard_map/ppermute | solution.py:313
  18.9 11.1 %collective-permute-start.5 = (bf16[528,128]{1,0:T(8,128)(2,1)S(1)}, bf16[528,128]{1,0:T(8,128)(2,1)S(1)}, u32[]{:S(2)}, u32[]{:S(2)}) collective-permute-start(bf16[528,128]{1,0:T(8,128)(2,1)S(1)} %transform.1.refs_0_), channel_id=1, source_target_pairs={{0,8},{4,12},{8,0},{12,4},{16,24},{20,28},{24,16},{28,20},{1,9},{5... | collective-permute-start | bytes 405512 | tf_op jit(solution)/shard_map/ppermute | solution.py:313
  19.7 10.8 %collective-permute-start.4 = (bf16[528,128]{1,0:T(8,128)(2,1)S(1)}, bf16[528,128]{1,0:T(8,128)(2,1)S(1)}, u32[]{:S(2)}, u32[]{:S(2)}) collective-permute-start(bf16[528,128]{1,0:T(8,128)(2,1)S(1)} %transform.1.refs_0_), channel_id=1, source_target_pairs={{0,4},{4,0},{8,12},{12,8},{16,20},{20,16},{24,28},{28,24},{1,5},{5... | collective-permute-start | bytes 405512 | tf_op jit(solution)/shard_map/ppermute | solution.py:313
  23.6 6.9 %collective-permute-start.10 = (bf16[528,128]{1,0:T(8,128)(2,1)S(1)}, bf16[528,128]{1,0:T(8,128)(2,1)S(1)}, u32[]{:S(2)}, u32[]{:S(2)}) collective-permute-start(bf16[528,128]{1,0:T(8,128)(2,1)S(1)} %collective-permute-done.9.refs_6_), channel_id=1, source_target_pairs={{0,4},{4,0},{8,12},{12,8},{16,20},{20,16},{24,28},{28,24},{1,5},{5... | collective-permute-start | bytes 405512 | tf_op jit(solution)/shard_map/ppermute | solution.py:313
  30.0 1.4 %collective-permute-start.8 = (bf16[528,128]{1,0:T(8,128)(2,1)S(1)}, bf16[528,128]{1,0:T(8,128)(2,1)S(1)}, u32[]{:S(2)}, u32[]{:S(2)}) collective-permute-start(bf16[528,128]{1,0:T(8,128)(2,1)S(1)} %collective-permute-done.7.refs_4_), channel_id=1, source_target_pairs={{0,4},{4,0},{8,12},{12,8},{16,20},{20,16},{24,28},{28,24},{1,5},{5... | collective-permute-start | bytes 405512 | tf_op jit(solution)/shard_map/ppermute | solution.py:313
  30.0 1.5 %collective-permute-start.6 = (bf16[528,128]{1,0:T(8,128)(2,1)S(1)}, bf16[528,128]{1,0:T(8,128)(2,1)S(1)}, u32[]{:S(2)}, u32[]{:S(2)}) collective-permute-start(bf16[528,128]{1,0:T(8,128)(2,1)S(1)} %collective-permute-done.5.refs_2_), channel_id=1, source_target_pairs={{0,4},{4,0},{8,12},{12,8},{16,20},{20,16},{24,28},{28,24},{1,5},{5... | collective-permute-start | bytes 405512 | tf_op jit(solution)/shard_map/ppermute | solution.py:313
  32.7 4.6 %collective-permute-start.13 = (f32[16,16]{1,0:T(8,128)S(1)}, f32[16,16]{1,0:T(8,128)S(1)}, u32[]{:S(2)}, u32[]{:S(2)}) collective-permute-start(f32[16,16]{1,0:T(8,128)S(1)} %contract.1), channel_id=1, source_target_pairs={{0,3},{1,2},{2,1},{3,0},{4,7},{5,6},{6,5},{7,4},{8,11},{9,10},{10,... | collective-permute-start | bytes 3080 | tf_op jit(solution)/shard_map/ppermute | solution.py:313
  35.6 3.7 %collective-permute-start.12 = (f32[16,16]{1,0:T(8,128)S(1)}, f32[16,16]{1,0:T(8,128)S(1)}, u32[]{:S(2)}, u32[]{:S(2)}) collective-permute-start(f32[16,16]{1,0:T(8,128)S(1)} %contract.1), channel_id=1, source_target_pairs={{0,2},{1,3},{2,0},{3,1},{4,6},{5,7},{6,4},{7,5},{8,10},{9,11},{10,... | collective-permute-start | bytes 3080 | tf_op jit(solution)/shard_map/ppermute | solution.py:313
  35.6 3.7 %collective-permute-start.11 = (f32[16,16]{1,0:T(8,128)S(1)}, f32[16,16]{1,0:T(8,128)S(1)}, u32[]{:S(2)}, u32[]{:S(2)}) collective-permute-start(f32[16,16]{1,0:T(8,128)S(1)} %contract.1), channel_id=1, source_target_pairs={{0,1},{1,0},{2,3},{3,2},{4,5},{5,4},{6,7},{7,6},{8,9},{9,8},{10,11... | collective-permute-start | bytes 3080 | tf_op jit(solution)/shard_map/ppermute | solution.py:313

commit v5 on v4

--- a/solution.py
+++ b/solution.py
@@ -10,6 +10,7 @@
 
 ATOM_BS = 16
 TILE = 16
+TAIL = 8
 
 
 def top_bit(k):
@@ -40,10 +41,19 @@
     return ref[:, pl.ds(pl.multiple_of(index * block, block), block)]
 
 
+def pieces(shape):
+    half = shape[-2] // 2
+    halves = [pl.ds(0, half), pl.ds(half, half)]
+    return halves if len(shape) == 2 else [(i, x) for i in range(shape[0]) for x in halves]
+
+
 def prep_kernel(*refs):
     hbm, outs, copied, mask_ref, sems = refs[:5], refs[5:-7], refs[-7:-2], refs[-2], refs[-1]
     own_ref, screen_ref, pay_refs = outs[0], outs[1], outs[2:]
-    copies = [pltpu.make_async_copy(src, dst, sems.at[i]) for i, (src, dst) in enumerate(zip(hbm, copied))]
+    copies = []
+    for i, (src, dst) in enumerate(zip(hbm, copied)):
+        parts = [(src, dst)] if i < 2 else [(src.at[x], dst.at[x]) for x in pieces(src.shape)]
+        copies += [pltpu.make_async_copy(x, y, sems.at[len(copies) + n]) for n, (x, y) in enumerate(parts)]
     for copy in copies:
         copy.start()
     sizes_ref, pattern_ref, slab_ref, occ_ref, virt_ref = copied
@@ -96,31 +106,25 @@
             first = which(a, k) == 0
             slab_blocks.append(jnp.where(first, *slabs))
             green_blocks.append(jnp.where(first, *greens))
-    tails = []
-    for (block_part, diagonal), blocks in zip(folded, (slab_blocks, green_blocks)):
-        blocks.append(block_part.astype(bf16))
-        tails.append(jnp.broadcast_to(diagonal, (TILE, block)).astype(bf16))
-
-    def put(ref, at, parts, tail):
-        for part in parts + [tail]:
-            ref[at : at + part.shape[0], :] = part
-            at += part.shape[0]
-        return at
+    slab_blocks.append(folded[0][0].astype(bf16))
+    green_blocks.append(folded[1][0].astype(bf16))
+    upper = lax.broadcasted_iota(jnp.int32, (2 * TAIL, block), 0) < TAIL
+    tail = jnp.where(upper, folded[0][1], folded[1][1]).astype(bf16)
 
     even = (lax.axis_index("ri") & 1) == 0
     rows = block // 2
     for k in range(1, ao):
-        at = put(pay_refs[k - 1], 0, slab_blocks[: k - 1] + slab_blocks[k:], tails[0])
         parts = green_blocks[: k - 1] + green_blocks[k:]
         if shared(k, ao):
             parts = [jnp.where(even, x[:rows], x[rows:]) for x in parts]
-        put(pay_refs[k - 1], at, parts, tails[1])
+        at = 0
+        for part in slab_blocks[: k - 1] + slab_blocks[k:] + parts + [tail]:
+            pay_refs[k - 1][at : at + part.shape[0], :] = part
+            at += part.shape[0]
 
 
 def reader(ref, base, m, ao, block):
     def read(k):
-        if k < 0:
-            return ref[base + (ao - 1) * block : base + (ao - 1) * block + TILE, :]
         at = base + ((ao - 2) if k == 0 else k - 1 - (k > m)) * block
         return ref[at : at + block, :]
 
@@ -131,15 +135,13 @@
     here, there = (reader(x, base, m, ao, block // 2) for x in (mine, other))
 
     def read(k):
-        if k < 0:
-            return here(k)
         x, y = here(k), there(k)
         return jnp.concatenate([jnp.where(even, x, y), jnp.where(even, y, x)], axis=0)
 
     return read
 
 
-def unfold(reads, own, a, ao, block, put):
+def unfold(reads, diagonals, own, a, ao, block, put):
     below, on = tri_masks(block)
     for q in range(2):
         for k in range(ao):
@@ -148,20 +150,14 @@
             if k:
                 put(q, k, 0, value.T)
     for m in range(1, ao):
-        for j in range(m + 1, ao):
-            k = m ^ j
-            here = reads[m](k)
-            there = reads[j](k)
-            here_t = here.T
-            there_t = there.T
-            lower = which(a ^ m, k) == 0
-            put(0, m, j, jnp.where(lower, here, there_t))
-            put(0, j, m, jnp.where(lower, here_t, there))
-            put(1, m, j, jnp.where(lower, there_t, here))
-            put(1, j, m, jnp.where(lower, there, here_t))
+        for k in range(1, ao):
+            if k != m:
+                value = reads[m](k)
+                put(which(a ^ m, k), m, m ^ k, value)
+                put(which(a ^ m, k), m ^ k, m, value.T)
         folded = reads[m](0).astype(jnp.float32)
         folded_t = folded.T
-        diagonal = reads[m](-1).astype(jnp.float32)[0:1]
+        diagonal = diagonals[m]
         put(0, m, m, jnp.where(below | on, folded, folded_t).astype(jnp.bfloat16))
         put(
             1, m, m,
@@ -177,11 +173,14 @@
     total = ao * block
     a = lax.axis_index("ao")
     f32, bf16 = jnp.float32, jnp.bfloat16
-    size = (ao - 1) * block + TILE
+    size = (ao - 1) * block
     pays, others = pays[: ao - 1], list(pays[ao - 1 :])
     even = (lax.axis_index("ri") & 1) == 0
-    slabs, greens = [None], [None]
+    slabs, greens, diagonals = [None], [None], ([None], [None])
     for m, x in enumerate(pays, 1):
+        tail = x[x.shape[0] - 2 * TAIL :, :].astype(f32)
+        for rows, at in zip(diagonals, (0, TAIL)):
+            rows.append(tail[at : at + 1])
         slabs.append(reader(x, 0, m, ao, block))
         if shared(m, ao):
             greens.append(halves_reader(x, others.pop(0), even, size, m, ao, block))
@@ -192,36 +191,46 @@
         slab_ref[matrix, row * block : (row + 1) * block, col * block : (col + 1) * block] = value
 
     def put_green(matrix, row, col, value):
-        at = (total if matrix == 0 else 0) + col * block
-        green_ref[row, :, at : at + block] = value
+        at = pl.multiple_of((1 - matrix) * total + col * block, block)
+        green_ref[row, :, pl.ds(at, block)] = value
 
     def own(first):
         return lambda q, k: own_ref[first + q, :, k * block : (k + 1) * block]
 
-    unfold(greens, own(2), a, ao, block, put_green)
-    unfold(slabs, own(0), a, ao, block, put_slab)
+    unfold(greens, diagonals[1], own(2), a, ao, block, put_green)
+    unfold(slabs, diagonals[0], own(0), a, ao, block, put_slab)
     both = jnp.concatenate([green_ref[0, :, total:], green_ref[0, :, :total]], axis=0)
     for q in range(2):
         left = jnp.dot(both, slab_ref[q], preferred_element_type=f32).astype(bf16)
         left_ref[q, :, :total] = left[:block]
         left_ref[q, :, total:] = left[block:]
     last = (((1,), (1,)), ((), ()))
-    for k in range(1, ao):
-        sums = lax.dot_general(left_ref[which(a, k)], green_ref[k], last, preferred_element_type=f32)
+    below, on = tri_masks(block)
+
+    def put_block(k, sums):
         screen = screen_ref[:, k * block : (k + 1) * block].astype(f32)
         out_ref[(k - 1) * block : k * block, :] = (sums * screen).astype(bf16)
-    below, on = tri_masks(block)
+
+    lefts = jnp.concatenate([left_ref[0], left_ref[1]], axis=0)
+    rights = green_ref[0 : min(2, ao)].reshape(min(2, ao) * block, 2 * total)
+    sums = lax.dot_general(lefts, rights, last, preferred_element_type=f32)
     weight = jnp.where(on, 0.5, 1.0) * screen_ref[:, 0:block].astype(f32)
-    first, second = (
-        lax.dot_general(left_ref[q], green_ref[0], last, preferred_element_type=f32) * weight for q in range(2)
-    )
-    folded, diagonal = fold_diagonal(first, second, below, on)
+    folded, diagonal = fold_diagonal(sums[:block, :block] * weight, sums[block:, :block] * weight, below, on)
+    if ao > 1:
+        put_block(1, jnp.where(which(a, 1) == 0, sums[:block, block:], sums[block:, block:]))
+    start = 2
+    while start < ao:
+        rights = green_ref[start : 2 * start].reshape(start * block, 2 * total)
+        sums = lax.dot_general(left_ref[which(a, start)], rights, last, preferred_element_type=f32)
+        for k in range(start, 2 * start):
+            put_block(k, sums[:, (k - start) * block : (k - start + 1) * block])
+        start *= 2
     at = (ao - 1) * block
     out_ref[at : at + block, :] = folded.astype(bf16)
-    out_ref[at + block : at + block + TILE, :] = jnp.broadcast_to(diagonal, (TILE, block)).astype(bf16)
-
-
-def stage_kernel(tensor_hbm, _, out_ref, tensor_ref, sem):
+    out_ref[at + block :, :] = jnp.broadcast_to(diagonal, (TAIL, block)).astype(bf16)
+
+
+def stage_kernel(tensor_hbm, _, out_ref, tensor_ref, rows_ref, sem):
     ri_rows, block, _ = tensor_ref.shape
     a = lax.axis_index("ao")
     copy = pltpu.make_async_copy(tensor_hbm, tensor_ref, sem)
@@ -231,20 +240,19 @@
         cols = pl.ds(pl.multiple_of((a ^ k) * block, block), block)
         for g in range(block // TILE):
             for p in range(ri_rows):
-                out_ref[k, p * TILE : (p + 1) * TILE, g * block : (g + 1) * block] = tensor_ref[
-                    p, g * TILE : (g + 1) * TILE, cols
-                ]
+                rows_ref[p * TILE : (p + 1) * TILE, :] = tensor_ref[p, g * TILE : (g + 1) * TILE, cols]
+            out_ref[k, g * block : (g + 1) * block, :] = rows_ref[...].T
 
 
 def contract_kernel(count, ao, block, *refs):
     pays = refs[:count]
     tensor_ref, out_ref = refs[count:]
-    ri_rows = tensor_ref.shape[1] // TILE
+    ri_rows = tensor_ref.shape[2] // TILE
     a = lax.axis_index("ao")
     r = lax.axis_index("ri")
     f32, bf16 = jnp.float32, jnp.bfloat16
     groups = block // TILE
-    last = (((1,), (1,)), ((), ()))
+    last, plain = (((1,), (1,)), ((), ())), (((1,), (0,)), ((), ()))
 
     def spread(values, rows_of):
         return jnp.concatenate(
@@ -260,34 +268,37 @@
     firsts, seconds = [], []
     for pay in pays:
         folded = pay[at : at + block, :].astype(f32)
-        diagonal = pay[at + block : at + block + TILE, :].astype(f32)[0:1]
+        diagonal = pay[at + block : at + block + TAIL, :].astype(f32)[0:1]
         firsts.append(jnp.where(below | on, folded, 0.0).astype(bf16))
         seconds.append(
             jnp.where(below, 0.0, jnp.where(on, jnp.broadcast_to(diagonal, (block, block)), folded)).astype(bf16)
         )
     sums = lax.dot_general(
-        spread(firsts + seconds, lambda v, rows: v[rows]), tensor_ref[0], last, preferred_element_type=f32
+        spread(firsts + seconds, lambda v, rows: v[rows]), tensor_ref[0], plain, preferred_element_type=f32
     )
-    half = count * TILE
-    sums = [sums[:half], sums[half:]]
-    for k in range(1, ao):
-        start = (k - 1) * block
-        part = lax.dot_general(
-            spread(pays, lambda pay, rows: pay[start + rows.start : start + rows.stop, :]),
-            tensor_ref[k],
-            last,
-            preferred_element_type=f32,
-        )
-        to_first = which(a, k) == 0
-        sums[0] = sums[0] + jnp.where(to_first, part, 0.0)
-        sums[1] = sums[1] + jnp.where(to_first, 0.0, part)
-    width = ri_rows * TILE
+    half, width = count * TILE, ri_rows * TILE
     row = lax.broadcasted_iota(jnp.int32, (half, width), 0)
     col = lax.broadcasted_iota(jnp.int32, (half, width), 1)
     same = (row & (TILE - 1)) == (col & (TILE - 1))
-    traces = jnp.concatenate(
-        [jnp.where(same, s, 0.0).reshape(count, TILE, width).sum(axis=1) for s in sums], axis=0
-    )
+
+    def trace(values):
+        return jnp.where(same, values, 0.0).reshape(count, TILE, width).sum(axis=1)
+
+    traces = [trace(sums[:half]), trace(sums[half:])]
+    for k in range(1, ao):
+        start = (k - 1) * block
+        part = trace(
+            lax.dot_general(
+                spread(pays, lambda pay, rows: pay[start + rows.start : start + rows.stop, :]),
+                tensor_ref[k],
+                plain,
+                preferred_element_type=f32,
+            )
+        )
+        to_first = which(a, k) == 0
+        traces[0] = traces[0] + jnp.where(to_first, part, 0.0)
+        traces[1] = traces[1] + jnp.where(to_first, 0.0, part)
+    traces = jnp.concatenate(traces, axis=0)
     pick = (
         lax.shift_right_logical(lax.broadcasted_iota(jnp.int32, (ri_rows, width), 1), jnp.int32(4))
         == lax.broadcasted_iota(jnp.int32, (ri_rows, width), 0)
@@ -318,15 +329,15 @@
     total = occ_green.shape[1]
     ri_rows = three_center.shape[0]
     atoms = pattern.shape[0]
-    half = total + TILE
+    half = total + TAIL
     bf16 = jnp.bfloat16
     vmem = pl.BlockSpec(memory_space=pltpu.VMEM)
     inputs = tuple(
         pltpu.with_memory_space_constraint(x, pltpu.HBM)
         for x in (atom_sizes.reshape(1, atoms), pattern, slab_tensor, occ_green, virt_green)
     )
-    size = (ao - 1) * block + TILE
-    sizes = [size + (size - (ao - 1) * block // 2 if shared(k, ao) else size) for k in range(1, ao)]
+    size = (ao - 1) * block
+    sizes = [size + (size // 2 if shared(k, ao) else size) + 2 * TAIL for k in range(1, ao)]
     prepared = pl.pallas_call(
         prep_kernel,
         out_shape=[jax.ShapeDtypeStruct((4, block, total), bf16), jax.ShapeDtypeStruct((block, total), bf16)]
@@ -334,7 +345,7 @@
         in_specs=[pl.BlockSpec(memory_space=pltpu.HBM)] * 5,
         out_specs=[vmem] * (2 + len(sizes)),
         scratch_shapes=[pltpu.VMEM(x.shape, x.dtype) for x in inputs]
-        + [pltpu.VMEM((block, total), bf16), pltpu.SemaphoreType.DMA((5,))],
+        + [pltpu.VMEM((block, total), bf16), pltpu.SemaphoreType.DMA((2 + sum(len(pieces(x.shape)) for x in inputs[2:]),))],
         compiler_params=room((sum(sizes), block), (5 * block, total), (2 * block, 2 * total)),
         name="prep",
     )(*inputs)
@@ -346,10 +357,14 @@
     groups = block // TILE
     staged = pl.pallas_call(
         stage_kernel,
-        out_shape=jax.ShapeDtypeStruct((ao, ri_rows * TILE, groups * block), bf16),
+        out_shape=jax.ShapeDtypeStruct((ao, groups * block, ri_rows * TILE), bf16),
         in_specs=[pl.BlockSpec(memory_space=pltpu.HBM)] * 2,
         out_specs=vmem,
-        scratch_shapes=[pltpu.VMEM(three_center.shape, bf16), pltpu.SemaphoreType.DMA],
+        scratch_shapes=[
+            pltpu.VMEM(three_center.shape, bf16),
+            pltpu.VMEM((ri_rows * TILE, block), bf16),
+            pltpu.SemaphoreType.DMA,
+        ],
         compiler_params=room((2 * ri_rows, block, total)),
         cost_estimate=pl.CostEstimate(flops=0, transcendentals=0, bytes_accessed=8 * ri_rows * block * total),
         name="stage",

time: 40.1 us -> 39.4 us (0.983)
    ppermute x14, waiting for transfers between devices: 20.3 us -> 19.9 us  [exchange(): return lax.ppermute(value, axis, [(i, i ^ k) for i in range(size)])]
  transfers between devices with their start and end apart: 14 -> 14, of which waited for: 9 -> 9; matrix products, arithmetic and copies ran while one was open for 0% -> 0% of each run, Pallas kernels for 5% -> 6%
where the time goes in v5:
time: 39.4 us; the launch traced here: 39.2 us
  waiting for transfers between devices  19.9 us (51%)
  starting transfers between devices  13.1 us (33%)
  Pallas kernels  5.55 us (14%)
  other arithmetic  0.6 us (2%)
    ppermute x14, waiting for transfers between devices, exchange(): return lax.ppermute(value, axis, [(i, i ^ k) for i in range(size)])  19.9 us
    ppermute x14, starting transfers between devices, exchange(): return lax.ppermute(value, axis, [(i, i ^ k) for i in range(size)])  13.1 us
    pallas_call x1, Pallas kernels, shards(): pl.pallas_call(stage_kernel, out_shape=jax.ShapeDtypeStruct((ao, groups *...  2.25 us
    pallas_call x1, Pallas kernels, shards(): pl.pallas_call(prep_kernel, out_shape=[jax.ShapeDtypeStruct((4, block, to...  1.39 us
    pallas_call x1, Pallas kernels, shards(): pl.pallas_call(lambda *refs: transform_kernel(ao, block, *refs), out_shap...  1.06 us
    pallas_call x1, Pallas kernels, shards(): pl.pallas_call(lambda *refs: contract_kernel(ri, ao, block, *refs), out_s...  0.85 us
  transfers between devices with their start and end apart: 14, of which 9 were waited for; matrix products, arithmetic and copies ran while one was open for 0% of the time, Pallas kernels for 6%

profile of v5, /device:TPU:0, one launch (start us, length us, event | category | flops | bytes accessed | tf_op | source)
XLA Modules:
  0.0 39.2 jit_solution(9880171426006639017)
XLA Ops:
  0.0 1.4 %prep.1 = (bf16[4,128,512]{2,1,0:T(8,128)(2,1)S(1)}, bf16[128,512]{1,0:T(8,128)(2,1)S(1)}, bf16[784,128]{1,0:T(8,128)(2,1)S(1)}, bf16[784,128]{1,0:T(8,128)(2,1)S(1)}, bf16[592,128]{1,0:T(8,128)(2,1)S(1)}) custom-call(s32[1,32]{1,0:T(1,128)} %bitcast.1, s32[32,32]{1,0:T(8,128)} %refs_1_.1, bf16[2,128,512]{2,1,0:T(8,128)(2,1)} %refs_2_.1, ...), custom_call_target="tpu_custom_call" | custom-call | tf_op jit(solution)/shard_map/prep/pallas_call | solution.py:341
  1.4 4.0 %collective-permute-start.2 = (bf16[592,128]{1,0:T(8,128)(2,1)S(1)}, bf16[592,128]{1,0:T(8,128)(2,1)S(1)}, u32[]{:S(2)}, u32[]{:S(2)}) collective-permute-start(bf16[592,128]{1,0:T(8,128)(2,1)S(1)} %get-tuple-element.12), channel_id=1, source_target_pairs={{0,3},{1,2},{2,1},{3,0},{4,7},{5,6},{6,5},{7,4},{8,11},{9,10},{10,... | collective-permute-start | bytes 454664 | tf_op jit(solution)/shard_map/ppermute | solution.py:324
  5.4 0.5 %collective-permute-start = (bf16[784,128]{1,0:T(8,128)(2,1)S(1)}, bf16[784,128]{1,0:T(8,128)(2,1)S(1)}, u32[]{:S(2)}, u32[]{:S(2)}) collective-permute-start(bf16[784,128]{1,0:T(8,128)(2,1)S(1)} %get-tuple-element.10), channel_id=1, source_target_pairs={{0,1},{1,0},{2,3},{3,2},{4,5},{5,4},{6,7},{7,6},{8,9},{9,8},{10,11... | collective-permute-start | bytes 602120 | tf_op jit(solution)/shard_map/ppermute | solution.py:324
  5.9 0.1 collective-permute-start.1
  6.0 4.1 %collective-permute-done.2.refs_2_ = bf16[592,128]{1,0:T(8,128)(2,1)S(1)} collective-permute-done((bf16[592,128]{1,0:T(8,128)(2,1)S(1)}, bf16[592,128]{1,0:T(8,128)(2,1)S(1)}, u32[]{:S(2)}, u32[]{:S(2)}) %collective-permute-start.2) | collective-permute-done | bytes 151584 | tf_op jit(solution)/shard_map/ppermute | solution.py:324
  10.2 0.0 collective-permute-start.3
  10.2 2.2 %stage.1.refs_6_.refs_8_ = bf16[4,1024,256]{2,1,0:T(8,128)(2,1)S(1)} custom-call(bf16[16,128,512]{2,1,0:T(8,128)(2,1)} %tensor_hbm.1, bf16[128,512]{1,0:T(8,128)(2,1)S(1)} %get-tuple-element.14._.refs_5_), custom_call_target="tpu_custom_call" | custom-call | bytes 8388608 | tf_op jit(solution)/shard_map/stage/pallas_call | solution.py:358
  12.4 1.5 %collective-permute-done.refs_0_ = bf16[784,128]{1,0:T(8,128)(2,1)S(1)} collective-permute-done((bf16[784,128]{1,0:T(8,128)(2,1)S(1)}, bf16[784,128]{1,0:T(8,128)(2,1)S(1)}, u32[]{:S(2)}, u32[]{:S(2)}) %collective-permute-start) | collective-permute-done | bytes 200736 | tf_op jit(solution)/shard_map/ppermute | solution.py:324
  13.9 0.0 collective-permute-done.1.refs_1_
  13.9 0.0 collective-permute-done.3.refs_3_
  13.9 1.1 %transform.1.refs_0_ = bf16[520,128]{1,0:T(8,128)(2,1)S(1)} custom-call(bf16[784,128]{1,0:T(8,128)(2,1)S(1)} %collective-permute-done.refs_0_, bf16[784,128]{1,0:T(8,128)(2,1)S(1)} %collective-permute-done.1.refs_1_, bf16[592,128]{1,0:T(8,128)(2,1)S(1)} %collective-permute-done.2.refs_2_, bf16[592,128]{1,0:T(8,128)(2,1)S(1)} %collective-permute-done.3.refs_3_, ...), custom_call_target="tpu_custom_call" | custom-call | tf_op jit(solution)/shard_map/transform/pallas_call | solution.py:372
  15.0 3.6 %collective-permute-start.9 = (bf16[520,128]{1,0:T(8,128)(2,1)S(1)}, bf16[520,128]{1,0:T(8,128)(2,1)S(1)}, u32[]{:S(2)}, u32[]{:S(2)}) collective-permute-start(bf16[520,128]{1,0:T(8,128)(2,1)S(1)} %transform.1.refs_0_), channel_id=1, source_target_pairs={{0,24},{4,28},{8,16},{12,20},{16,8},{20,12},{24,0},{28,4},{1,25},{... | collective-permute-start | bytes 399368 | tf_op jit(solution)/shard_map/ppermute | solution.py:324
  18.6 0.0 collective-permute-start.7
  18.6 0.8 %collective-permute-start.5 = (bf16[520,128]{1,0:T(8,128)(2,1)S(1)}, bf16[520,128]{1,0:T(8,128)(2,1)S(1)}, u32[]{:S(2)}, u32[]{:S(2)}) collective-permute-start(bf16[520,128]{1,0:T(8,128)(2,1)S(1)} %transform.1.refs_0_), channel_id=1, source_target_pairs={{0,8},{4,12},{8,0},{12,4},{16,24},{20,28},{24,16},{28,20},{1,9},{5... | collective-permute-start | bytes 399368 | tf_op jit(solution)/shard_map/ppermute | solution.py:324
  19.4 0.0 collective-permute-start.4
  19.4 3.9 %collective-permute-done.9.refs_6_ = bf16[520,128]{1,0:T(8,128)(2,1)S(1)} collective-permute-done((bf16[520,128]{1,0:T(8,128)(2,1)S(1)}, bf16[520,128]{1,0:T(8,128)(2,1)S(1)}, u32[]{:S(2)}, u32[]{:S(2)}) %collective-permute-start.9) | collective-permute-done | bytes 133152 | tf_op jit(solution)/shard_map/ppermute | solution.py:324
  23.3 0.0 collective-permute-start.10
  23.3 6.3 %collective-permute-done.7.refs_4_ = bf16[520,128]{1,0:T(8,128)(2,1)S(1)} collective-permute-done((bf16[520,128]{1,0:T(8,128)(2,1)S(1)}, bf16[520,128]{1,0:T(8,128)(2,1)S(1)}, u32[]{:S(2)}, u32[]{:S(2)}) %collective-permute-start.7) | collective-permute-done | bytes 133152 | tf_op jit(solution)/shard_map/ppermute | solution.py:324
  29.6 0.0 collective-permute-start.8
  29.6 0.0 collective-permute-done.5.refs_2_
  29.6 0.5 %collective-permute-start.6 = (bf16[520,128]{1,0:T(8,128)(2,1)S(1)}, bf16[520,128]{1,0:T(8,128)(2,1)S(1)}, u32[]{:S(2)}, u32[]{:S(2)}) collective-permute-start(bf16[520,128]{1,0:T(8,128)(2,1)S(1)} %collective-permute-done.5.refs_2_), channel_id=1, source_target_pairs={{0,4},{4,0},{8,12},{12,8},{16,20},{20,16},{24,28},{28,24},{1,5},{5... | collective-permute-start | bytes 399368 | tf_op jit(solution)/shard_map/ppermute | solution.py:324
  30.1 0.0 collective-permute-done.4.refs_1_
  30.1 0.0 collective-permute-done.10.refs_7_
  30.1 0.8 %collective-permute-done.8.refs_5_ = bf16[520,128]{1,0:T(8,128)(2,1)S(1)} collective-permute-done((bf16[520,128]{1,0:T(8,128)(2,1)S(1)}, bf16[520,128]{1,0:T(8,128)(2,1)S(1)}, u32[]{:S(2)}, u32[]{:S(2)}) %collective-permute-start.8) | collective-permute-done | bytes 133152 | tf_op jit(solution)/shard_map/ppermute | solution.py:324
  30.9 0.2 collective-permute-done.6.refs_3_
  31.1 0.8 %contract.1 = f32[16,16]{1,0:T(8,128)S(1)} custom-call(bf16[520,128]{1,0:T(8,128)(2,1)S(1)} %transform.1.refs_0_, bf16[520,128]{1,0:T(8,128)(2,1)S(1)} %collective-permute-done.4.refs_1_, bf16[520,128]{1,0:T(8,128)(2,1)S(1)} %collective-permute-done.5.refs_2_, bf16[520,128]{1,0:T(8,128)(2,1)S(1)} %collective-permute-done.6.refs_3_, ...), custom_call_target="tpu_custom_call" | custom-call | tf_op jit(solution)/shard_map/contract/pallas_call | solution.py:392
  32.0 2.9 %collective-permute-start.13 = (f32[16,16]{1,0:T(8,128)S(1)}, f32[16,16]{1,0:T(8,128)S(1)}, u32[]{:S(2)}, u32[]{:S(2)}) collective-permute-start(f32[16,16]{1,0:T(8,128)S(1)} %contract.1), channel_id=1, source_target_pairs={{0,3},{1,2},{2,1},{3,0},{4,7},{5,6},{6,5},{7,4},{8,11},{9,10},{10,... | collective-permute-start | bytes 3080 | tf_op jit(solution)/shard_map/ppermute | solution.py:324
  34.8 0.1 collective-permute-start.12
  35.0 0.5 %collective-permute-start.11 = (f32[16,16]{1,0:T(8,128)S(1)}, f32[16,16]{1,0:T(8,128)S(1)}, u32[]{:S(2)}, u32[]{:S(2)}) collective-permute-start(f32[16,16]{1,0:T(8,128)S(1)} %contract.1), channel_id=1, source_target_pairs={{0,1},{1,0},{2,3},{3,2},{4,5},{5,4},{6,7},{7,6},{8,9},{9,8},{10,11... | collective-permute-start | bytes 3080 | tf_op jit(solution)/shard_map/ppermute | solution.py:324
  35.5 1.1 %collective-permute-done.13 = f32[16,16]{1,0:T(8,128)S(1)} collective-permute-done((f32[16,16]{1,0:T(8,128)S(1)}, f32[16,16]{1,0:T(8,128)S(1)}, u32[]{:S(2)}, u32[]{:S(2)}) %collective-permute-start.13) | collective-permute-done | bytes 1056 | tf_op jit(solution)/shard_map/ppermute | solution.py:324
  36.6 1.9 %collective-permute-done.12 = f32[16,16]{1,0:T(8,128)S(1)} collective-permute-done((f32[16,16]{1,0:T(8,128)S(1)}, f32[16,16]{1,0:T(8,128)S(1)}, u32[]{:S(2)}, u32[]{:S(2)}) %collective-permute-start.12) | collective-permute-done | bytes 1056 | tf_op jit(solution)/shard_map/ppermute | solution.py:324
  38.5 0.1 collective-permute-done.11
  38.6 0.6 %add_add_fusion = f32[16,16]{1,0:T(8,128)} fusion(f32[16,16]{1,0:T(8,128)S(1)} %collective-permute-done.12, f32[16,16]{1,0:T(8,128)S(1)} %collective-permute-done.13, f32[16,16]{1,0:T(8,128)S(1)} %contract.1, f32[16,16]{1,0:T(8,128)S(1)} %collective-permute-done.11), kind=kLoop, calls=%fused_computation | loop fusion | flops 768 | bytes 5120 | tf_op jit(solution)/shard_map/add | solution.py:402
Async XLA Ops:
  1.4 8.8 %collective-permute-start.2 = (bf16[592,128]{1,0:T(8,128)(2,1)S(1)}, bf16[592,128]{1,0:T(8,128)(2,1)S(1)}, u32[]{:S(2)}, u32[]{:S(2)}) collective-permute-start(bf16[592,128]{1,0:T(8,128)(2,1)S(1)} %get-tuple-element.12), channel_id=1, source_target_pairs={{0,3},{1,2},{2,1},{3,0},{4,7},{5,6},{6,5},{7,4},{8,11},{9,10},{10,... | collective-permute-start | bytes 454664 | tf_op jit(solution)/shard_map/ppermute | solution.py:324
  5.4 8.5 %collective-permute-start = (bf16[784,128]{1,0:T(8,128)(2,1)S(1)}, bf16[784,128]{1,0:T(8,128)(2,1)S(1)}, u32[]{:S(2)}, u32[]{:S(2)}) collective-permute-start(bf16[784,128]{1,0:T(8,128)(2,1)S(1)} %get-tuple-element.10), channel_id=1, source_target_pairs={{0,1},{1,0},{2,3},{3,2},{4,5},{5,4},{6,7},{7,6},{8,9},{9,8},{10,11... | collective-permute-start | bytes 602120 | tf_op jit(solution)/shard_map/ppermute | solution.py:324
  5.9 8.0 %collective-permute-start.1 = (bf16[784,128]{1,0:T(8,128)(2,1)S(1)}, bf16[784,128]{1,0:T(8,128)(2,1)S(1)}, u32[]{:S(2)}, u32[]{:S(2)}) collective-permute-start(bf16[784,128]{1,0:T(8,128)(2,1)S(1)} %get-tuple-element.11), channel_id=1, source_target_pairs={{0,2},{1,3},{2,0},{3,1},{4,6},{5,7},{6,4},{7,5},{8,10},{9,11},{10,... | collective-permute-start | bytes 602120 | tf_op jit(solution)/shard_map/ppermute | solution.py:324
  10.2 3.7 %collective-permute-start.3 = (bf16[592,128]{1,0:T(8,128)(2,1)S(1)}, bf16[592,128]{1,0:T(8,128)(2,1)S(1)}, u32[]{:S(2)}, u32[]{:S(2)}) collective-permute-start(bf16[592,128]{1,0:T(8,128)(2,1)S(1)} %collective-permute-done.2.refs_2_), channel_id=1, source_target_pairs={{0,4},{4,0},{8,12},{12,8},{16,20},{20,16},{24,28},{28,24},{1,5},{5... | collective-permute-start | bytes 454664 | tf_op jit(solution)/shard_map/ppermute | solution.py:324
  15.0 8.3 %collective-permute-start.9 = (bf16[520,128]{1,0:T(8,128)(2,1)S(1)}, bf16[520,128]{1,0:T(8,128)(2,1)S(1)}, u32[]{:S(2)}, u32[]{:S(2)}) collective-permute-start(bf16[520,128]{1,0:T(8,128)(2,1)S(1)} %transform.1.refs_0_), channel_id=1, source_target_pairs={{0,24},{4,28},{8,16},{12,20},{16,8},{20,12},{24,0},{28,4},{1,25},{... | collective-permute-start | bytes 399368 | tf_op jit(solution)/shard_map/ppermute | solution.py:324
  18.6 11.0 %collective-permute-start.7 = (bf16[520,128]{1,0:T(8,128)(2,1)S(1)}, bf16[520,128]{1,0:T(8,128)(2,1)S(1)}, u32[]{:S(2)}, u32[]{:S(2)}) collective-permute-start(bf16[520,128]{1,0:T(8,128)(2,1)S(1)} %transform.1.refs_0_), channel_id=1, source_target_pairs={{0,16},{4,20},{8,24},{12,28},{16,0},{20,4},{24,8},{28,12},{1,17},{... | collective-permute-start | bytes 399368 | tf_op jit(solution)/shard_map/ppermute | solution.py:324
  18.6 11.0 %collective-permute-start.5 = (bf16[520,128]{1,0:T(8,128)(2,1)S(1)}, bf16[520,128]{1,0:T(8,128)(2,1)S(1)}, u32[]{:S(2)}, u32[]{:S(2)}) collective-permute-start(bf16[520,128]{1,0:T(8,128)(2,1)S(1)} %transform.1.refs_0_), channel_id=1, source_target_pairs={{0,8},{4,12},{8,0},{12,4},{16,24},{20,28},{24,16},{28,20},{1,9},{5... | collective-permute-start | bytes 399368 | tf_op jit(solution)/shard_map/ppermute | solution.py:324
  19.4 10.7 %collective-permute-start.4 = (bf16[520,128]{1,0:T(8,128)(2,1)S(1)}, bf16[520,128]{1,0:T(8,128)(2,1)S(1)}, u32[]{:S(2)}, u32[]{:S(2)}) collective-permute-start(bf16[520,128]{1,0:T(8,128)(2,1)S(1)} %transform.1.refs_0_), channel_id=1, source_target_pairs={{0,4},{4,0},{8,12},{12,8},{16,20},{20,16},{24,28},{28,24},{1,5},{5... | collective-permute-start | bytes 399368 | tf_op jit(solution)/shard_map/ppermute | solution.py:324
  23.3 6.8 %collective-permute-start.10 = (bf16[520,128]{1,0:T(8,128)(2,1)S(1)}, bf16[520,128]{1,0:T(8,128)(2,1)S(1)}, u32[]{:S(2)}, u32[]{:S(2)}) collective-permute-start(bf16[520,128]{1,0:T(8,128)(2,1)S(1)} %collective-permute-done.9.refs_6_), channel_id=1, source_target_pairs={{0,4},{4,0},{8,12},{12,8},{16,20},{20,16},{24,28},{28,24},{1,5},{5... | collective-permute-start | bytes 399368 | tf_op jit(solution)/shard_map/ppermute | solution.py:324
  29.6 1.4 %collective-permute-start.8 = (bf16[520,128]{1,0:T(8,128)(2,1)S(1)}, bf16[520,128]{1,0:T(8,128)(2,1)S(1)}, u32[]{:S(2)}, u32[]{:S(2)}) collective-permute-start(bf16[520,128]{1,0:T(8,128)(2,1)S(1)} %collective-permute-done.7.refs_4_), channel_id=1, source_target_pairs={{0,4},{4,0},{8,12},{12,8},{16,20},{20,16},{24,28},{28,24},{1,5},{5... | collective-permute-start | bytes 399368 | tf_op jit(solution)/shard_map/ppermute | solution.py:324
  29.6 1.5 %collective-permute-start.6 = (bf16[520,128]{1,0:T(8,128)(2,1)S(1)}, bf16[520,128]{1,0:T(8,128)(2,1)S(1)}, u32[]{:S(2)}, u32[]{:S(2)}) collective-permute-start(bf16[520,128]{1,0:T(8,128)(2,1)S(1)} %collective-permute-done.5.refs_2_), channel_id=1, source_target_pairs={{0,4},{4,0},{8,12},{12,8},{16,20},{20,16},{24,28},{28,24},{1,5},{5... | collective-permute-start | bytes 399368 | tf_op jit(solution)/shard_map/ppermute | solution.py:324
  32.0 4.6 %collective-permute-start.13 = (f32[16,16]{1,0:T(8,128)S(1)}, f32[16,16]{1,0:T(8,128)S(1)}, u32[]{:S(2)}, u32[]{:S(2)}) collective-permute-start(f32[16,16]{1,0:T(8,128)S(1)} %contract.1), channel_id=1, source_target_pairs={{0,3},{1,2},{2,1},{3,0},{4,7},{5,6},{6,5},{7,4},{8,11},{9,10},{10,... | collective-permute-start | bytes 3080 | tf_op jit(solution)/shard_map/ppermute | solution.py:324
  34.8 3.7 %collective-permute-start.12 = (f32[16,16]{1,0:T(8,128)S(1)}, f32[16,16]{1,0:T(8,128)S(1)}, u32[]{:S(2)}, u32[]{:S(2)}) collective-permute-start(f32[16,16]{1,0:T(8,128)S(1)} %contract.1), channel_id=1, source_target_pairs={{0,2},{1,3},{2,0},{3,1},{4,6},{5,7},{6,4},{7,5},{8,10},{9,11},{10,... | collective-permute-start | bytes 3080 | tf_op jit(solution)/shard_map/ppermute | solution.py:324
  35.0 3.7 %collective-permute-start.11 = (f32[16,16]{1,0:T(8,128)S(1)}, f32[16,16]{1,0:T(8,128)S(1)}, u32[]{:S(2)}, u32[]{:S(2)}) collective-permute-start(f32[16,16]{1,0:T(8,128)S(1)} %contract.1), channel_id=1, source_target_pairs={{0,1},{1,0},{2,3},{3,2},{4,5},{5,4},{6,7},{7,6},{8,9},{9,8},{10,11... | collective-permute-start | bytes 3080 | tf_op jit(solution)/shard_map/ppermute | solution.py:324

commit v6 on v5

--- a/solution.py
+++ b/solution.py
@@ -324,6 +324,31 @@
     return lax.ppermute(value, axis, [(i, i ^ k) for i in range(size)])
 
 
+def along(value, targets):
+    pairs = []
+    for source, target in enumerate(targets):
+        for core in range(2):
+            other = 2 * source + 1 - core if target == source else 2 * target + core
+            pairs.append((2 * source + core, other))
+    return lax.ppermute(value, "ri", pairs)
+
+
+def spread_along(value, ri):
+    if ri != 8:
+        sources = [value] + [exchange(value, "ri", ri, k) for k in range(2, ri, 2)]
+        forwards = [exchange(x, "ri", ri, 1) for x in sources]
+        return [x for pair in zip(sources, forwards) for x in pair]
+    chip = lax.shift_right_logical(lax.axis_index("ri"), jnp.int32(1))
+    inner = (chip == 1) | (chip == 2)
+    middle = along(value, (0, 2, 1, 3))
+    near = along(value, (1, 0, 3, 2))
+    far = along(value, (3, 1, 2, 0))
+    relayed, middle = lax.optimization_barrier((jnp.where(inner, middle, value), middle))
+    last = along(relayed, (2, 0, 3, 1))
+    across, other = jnp.where(inner, middle, far), jnp.where(inner, far, middle)
+    return [value, other] + [x for y in (near, last, across) for x in (y, exchange(y, "ri", ri, 1))]
+
+
 def shards(ri, ao, three_center, slab_tensor, occ_green, virt_green, pattern, atom_sizes):
     block = occ_green.shape[0]
     total = occ_green.shape[1]
@@ -382,19 +407,13 @@
         compiler_params=room((sum(sizes), block), (4 * block, total), (2, total, total), (ao, block, 2 * total), (4, block, total)),
         name="transform",
     )(*pays, own, screen, staged)
-    sources = [weighted]
-    for k in range(2, ri, 2):
-        sources.append(exchange(weighted, "ri", ri, k))
-    arrived = []
-    for value in sources:
-        arrived.append(value)
-        arrived.append(exchange(value, "ri", ri, 1))
+    arrived = spread_along(weighted, ri)
     part = pl.pallas_call(
         lambda *refs: contract_kernel(ri, ao, block, *refs),
         out_shape=jax.ShapeDtypeStruct((ri_rows, 2 * ri), jnp.float32),
-        in_specs=[vmem] * (ri + 1),
+        in_specs=[vmem] * (len(arrived) + 1),
         out_specs=vmem,
-        compiler_params=room((half * ri, block), (2 * ri_rows, block, total)),
+        compiler_params=room((half * len(arrived), block), (2 * ri_rows, block, total)),
         name="contract",
     )(*arrived, staged)
     parts = [part] + [exchange(part, "ao", ao, k) for k in range(1, ao)]

time: 39.4 us -> 38.3 us (0.972)
  waiting for transfers between devices: 19.9 us -> 15 us
  starting transfers between devices: 13.1 us -> 16.7 us
    ppermute x14 -> x10, waiting for transfers between devices: 19.9 us -> 10.1 us  [exchange(): return lax.ppermute(value, axis, [(i, i ^ k) for i in range(size)])]
    ppermute x0 -> x4, starting transfers between devices: none -> 8.52 us  [along(): return lax.ppermute(value, 'ri', pairs)]
    ppermute x0 -> x4, waiting for transfers between devices: none -> 4.94 us  [along(): return lax.ppermute(value, 'ri', pairs)]
    ppermute x14 -> x10, starting transfers between devices: 13.1 us -> 8.22 us  [exchange(): return lax.ppermute(value, axis, [(i, i ^ k) for i in range(size)])]
  transfers between devices with their start and end apart: 14 -> 14, of which waited for: 9 -> 8; matrix products, arithmetic and copies ran while one was open for 0% -> 0% of each run, Pallas kernels for 6% -> 6%
where the time goes in v6:
time: 38.3 us; the launch traced here: 38.1 us
  starting transfers between devices  16.7 us (44%)
  waiting for transfers between devices  15 us (39%)
  Pallas kernels  5.56 us (15%)
  other arithmetic  0.7 us (2%)
    ppermute x10, waiting for transfers between devices, exchange(): return lax.ppermute(value, axis, [(i, i ^ k) for i in range(size)])  10.1 us
    ppermute x4, starting transfers between devices, along(): return lax.ppermute(value, 'ri', pairs)  8.52 us
    ppermute x10, starting transfers between devices, exchange(): return lax.ppermute(value, axis, [(i, i ^ k) for i in range(size)])  8.22 us
    ppermute x4, waiting for transfers between devices, along(): return lax.ppermute(value, 'ri', pairs)  4.94 us
    pallas_call x1, Pallas kernels, shards(): pl.pallas_call(stage_kernel, out_shape=jax.ShapeDtypeStruct((ao, groups *...  2.25 us
    pallas_call x1, Pallas kernels, shards(): pl.pallas_call(prep_kernel, out_shape=[jax.ShapeDtypeStruct((4, block, to...  1.39 us
    pallas_call x1, Pallas kernels, shards(): pl.pallas_call(lambda *refs: transform_kernel(ao, block, *refs), out_shap...  1.06 us
    pallas_call x1, Pallas kernels, shards(): pl.pallas_call(lambda *refs: contract_kernel(ri, ao, block, *refs), out_s...  0.86 us
  transfers between devices with their start and end apart: 14, of which 8 were waited for; matrix products, arithmetic and copies ran while one was open for 0% of the time, Pallas kernels for 6%

profile of v6, /device:TPU:0, one launch (start us, length us, event | category | flops | bytes accessed | tf_op | source)
XLA Modules:
  0.0 38.1 jit_solution(9364953699305474056)
XLA Ops:
  0.0 1.4 %prep.1 = (bf16[4,128,512]{2,1,0:T(8,128)(2,1)S(1)}, bf16[128,512]{1,0:T(8,128)(2,1)S(1)}, bf16[784,128]{1,0:T(8,128)(2,1)S(1)}, bf16[784,128]{1,0:T(8,128)(2,1)S(1)}, bf16[592,128]{1,0:T(8,128)(2,1)S(1)}) custom-call(s32[1,32]{1,0:T(1,128)} %bitcast.1, s32[32,32]{1,0:T(8,128)} %refs_1_.1, bf16[2,128,512]{2,1,0:T(8,128)(2,1)} %refs_2_.1, ...), custom_call_target="tpu_custom_call" | custom-call | tf_op jit(solution)/shard_map/prep/pallas_call | solution.py:366
  1.4 4.0 %collective-permute-start.2 = (bf16[592,128]{1,0:T(8,128)(2,1)S(1)}, bf16[592,128]{1,0:T(8,128)(2,1)S(1)}, u32[]{:S(2)}, u32[]{:S(2)}) collective-permute-start(bf16[592,128]{1,0:T(8,128)(2,1)S(1)} %get-tuple-element.14), channel_id=1, source_target_pairs={{0,3},{1,2},{2,1},{3,0},{4,7},{5,6},{6,5},{7,4},{8,11},{9,10},{10,... | collective-permute-start | bytes 454664 | tf_op jit(solution)/shard_map/ppermute | solution.py:324
  5.4 0.5 %collective-permute-start = (bf16[784,128]{1,0:T(8,128)(2,1)S(1)}, bf16[784,128]{1,0:T(8,128)(2,1)S(1)}, u32[]{:S(2)}, u32[]{:S(2)}) collective-permute-start(bf16[784,128]{1,0:T(8,128)(2,1)S(1)} %get-tuple-element.12), channel_id=1, source_target_pairs={{0,1},{1,0},{2,3},{3,2},{4,5},{5,4},{6,7},{7,6},{8,9},{9,8},{10,11... | collective-permute-start | bytes 602120 | tf_op jit(solution)/shard_map/ppermute | solution.py:324
  5.9 0.1 collective-permute-start.1
  6.0 4.1 %collective-permute-done.2.refs_2_ = bf16[592,128]{1,0:T(8,128)(2,1)S(1)} collective-permute-done((bf16[592,128]{1,0:T(8,128)(2,1)S(1)}, bf16[592,128]{1,0:T(8,128)(2,1)S(1)}, u32[]{:S(2)}, u32[]{:S(2)}) %collective-permute-start.2) | collective-permute-done | bytes 151584 | tf_op jit(solution)/shard_map/ppermute | solution.py:324
  10.2 0.0 collective-permute-start.3
  10.2 2.2 %stage.1.refs_6_.refs_8_ = bf16[4,1024,256]{2,1,0:T(8,128)(2,1)S(1)} custom-call(bf16[16,128,512]{2,1,0:T(8,128)(2,1)} %tensor_hbm.1, bf16[128,512]{1,0:T(8,128)(2,1)S(1)} %get-tuple-element.16._.refs_5_), custom_call_target="tpu_custom_call" | custom-call | bytes 8388608 | tf_op jit(solution)/shard_map/stage/pallas_call | solution.py:383
  12.4 1.5 %collective-permute-done.refs_0_ = bf16[784,128]{1,0:T(8,128)(2,1)S(1)} collective-permute-done((bf16[784,128]{1,0:T(8,128)(2,1)S(1)}, bf16[784,128]{1,0:T(8,128)(2,1)S(1)}, u32[]{:S(2)}, u32[]{:S(2)}) %collective-permute-start) | collective-permute-done | bytes 200736 | tf_op jit(solution)/shard_map/ppermute | solution.py:324
  13.9 0.0 collective-permute-done.1.refs_1_
  13.9 0.0 collective-permute-done.3.refs_3_
  13.9 1.1 %transform.1.refs_0_ = bf16[520,128]{1,0:T(8,128)(2,1)S(1)} custom-call(bf16[784,128]{1,0:T(8,128)(2,1)S(1)} %collective-permute-done.refs_0_, bf16[784,128]{1,0:T(8,128)(2,1)S(1)} %collective-permute-done.1.refs_1_, bf16[592,128]{1,0:T(8,128)(2,1)S(1)} %collective-permute-done.2.refs_2_, bf16[592,128]{1,0:T(8,128)(2,1)S(1)} %collective-permute-done.3.refs_3_, ...), custom_call_target="tpu_custom_call" | custom-call | tf_op jit(solution)/shard_map/transform/pallas_call | solution.py:397
  15.0 0.1 collective-permute-start.5
  15.1 3.6 %collective-permute-start.4 = (bf16[520,128]{1,0:T(8,128)(2,1)S(1)}, bf16[520,128]{1,0:T(8,128)(2,1)S(1)}, u32[]{:S(2)}, u32[]{:S(2)}) collective-permute-start(bf16[520,128]{1,0:T(8,128)(2,1)S(1)} %transform.1.refs_0_), channel_id=1, source_target_pairs={{0,24},{4,28},{8,12},{12,8},{16,20},{20,16},{24,0},{28,4},{1,25},{... | collective-permute-start | bytes 399368 | tf_op jit(solution)/shard_map/ppermute | solution.py:333
  18.7 0.0 collective-permute-start.6
  18.7 0.0 collective-permute-done.5
  18.8 4.8 %collective-permute-start.8 = (bf16[520,128]{1,0:T(8,128)(2,1)S(1)}, bf16[520,128]{1,0:T(8,128)(2,1)S(1)}, u32[]{:S(2)}, u32[]{:S(2)}) collective-permute-start(bf16[520,128]{1,0:T(8,128)(2,1)S(1)} %broadcast_select_fusion.2), channel_id=1, source_target_pairs={{0,16},{4,20},{8,0},{12,4},{16,24},{20,28},{24,8},{28,12},{1,17},{... | collective-permute-start | bytes 399368 | tf_op jit(solution)/shard_map/ppermute | solution.py:333
  23.6 0.0 collective-permute-done.4
  23.6 0.1 broadcast_select_fusion
  23.6 0.1 collective-permute-start.10
  23.7 2.2 %collective-permute-done.6.refs_2_ = bf16[520,128]{1,0:T(8,128)(2,1)S(1)} collective-permute-done((bf16[520,128]{1,0:T(8,128)(2,1)S(1)}, bf16[520,128]{1,0:T(8,128)(2,1)S(1)}, u32[]{:S(2)}, u32[]{:S(2)}) %collective-permute-start.6) | collective-permute-done | bytes 133152 | tf_op jit(solution)/shard_map/ppermute | solution.py:333
  25.9 0.0 collective-permute-start.7
  25.9 2.8 %collective-permute-done.8.refs_4_ = bf16[520,128]{1,0:T(8,128)(2,1)S(1)} collective-permute-done((bf16[520,128]{1,0:T(8,128)(2,1)S(1)}, bf16[520,128]{1,0:T(8,128)(2,1)S(1)}, u32[]{:S(2)}, u32[]{:S(2)}) %collective-permute-start.8) | collective-permute-done | bytes 133152 | tf_op jit(solution)/shard_map/ppermute | solution.py:333
  28.6 0.0 collective-permute-start.9
  28.6 0.0 collective-permute-done.7.refs_3_
  28.6 0.0 collective-permute-done.10.refs_7_
  28.7 1.3 %collective-permute-done.9.refs_5_ = bf16[520,128]{1,0:T(8,128)(2,1)S(1)} collective-permute-done((bf16[520,128]{1,0:T(8,128)(2,1)S(1)}, bf16[520,128]{1,0:T(8,128)(2,1)S(1)}, u32[]{:S(2)}, u32[]{:S(2)}) %collective-permute-start.9) | collective-permute-done | bytes 133152 | tf_op jit(solution)/shard_map/ppermute | solution.py:324
  30.0 0.9 %contract.1 = f32[16,16]{1,0:T(8,128)S(1)} custom-call(bf16[520,128]{1,0:T(8,128)(2,1)S(1)} %transform.1.refs_0_, bf16[520,128]{1,0:T(8,128)(2,1)S(1)} %get-tuple-element.20.refs_1_, bf16[520,128]{1,0:T(8,128)(2,1)S(1)} %collective-permute-done.6.refs_2_, bf16[520,128]{1,0:T(8,128)(2,1)S(1)} %collective-permute-done.7.refs_3_, ...), custom_call_target="tpu_custom_call" | custom-call | tf_op jit(solution)/shard_map/contract/pallas_call | solution.py:411
  30.9 1.5 %collective-permute-start.12 = (f32[16,16]{1,0:T(8,128)S(1)}, f32[16,16]{1,0:T(8,128)S(1)}, u32[]{:S(2)}, u32[]{:S(2)}) collective-permute-start(f32[16,16]{1,0:T(8,128)S(1)} %contract.1), channel_id=1, source_target_pairs={{0,2},{1,3},{2,0},{3,1},{4,6},{5,7},{6,4},{7,5},{8,10},{9,11},{10,... | collective-permute-start | bytes 3080 | tf_op jit(solution)/shard_map/ppermute | solution.py:324
  32.3 1.5 %collective-permute-start.13 = (f32[16,16]{1,0:T(8,128)S(1)}, f32[16,16]{1,0:T(8,128)S(1)}, u32[]{:S(2)}, u32[]{:S(2)}) collective-permute-start(f32[16,16]{1,0:T(8,128)S(1)} %contract.1), channel_id=1, source_target_pairs={{0,3},{1,2},{2,1},{3,0},{4,7},{5,6},{6,5},{7,4},{8,11},{9,10},{10,... | collective-permute-start | bytes 3080 | tf_op jit(solution)/shard_map/ppermute | solution.py:324
  33.8 0.5 %collective-permute-start.11 = (f32[16,16]{1,0:T(8,128)S(1)}, f32[16,16]{1,0:T(8,128)S(1)}, u32[]{:S(2)}, u32[]{:S(2)}) collective-permute-start(f32[16,16]{1,0:T(8,128)S(1)} %contract.1), channel_id=1, source_target_pairs={{0,1},{1,0},{2,3},{3,2},{4,5},{5,4},{6,7},{7,6},{8,9},{9,8},{10,11... | collective-permute-start | bytes 3080 | tf_op jit(solution)/shard_map/ppermute | solution.py:324
  34.4 0.2 collective-permute-done.12
  34.5 2.3 %collective-permute-done.13 = f32[16,16]{1,0:T(8,128)S(1)} collective-permute-done((f32[16,16]{1,0:T(8,128)S(1)}, f32[16,16]{1,0:T(8,128)S(1)}, u32[]{:S(2)}, u32[]{:S(2)}) %collective-permute-start.13) | collective-permute-done | bytes 1056 | tf_op jit(solution)/shard_map/ppermute | solution.py:324
  36.9 0.6 %collective-permute-done.11 = f32[16,16]{1,0:T(8,128)S(1)} collective-permute-done((f32[16,16]{1,0:T(8,128)S(1)}, f32[16,16]{1,0:T(8,128)S(1)}, u32[]{:S(2)}, u32[]{:S(2)}) %collective-permute-start.11) | collective-permute-done | bytes 1056 | tf_op jit(solution)/shard_map/ppermute | solution.py:324
  37.5 0.6 %add_add_fusion = f32[16,16]{1,0:T(8,128)} fusion(f32[16,16]{1,0:T(8,128)S(1)} %collective-permute-done.12, f32[16,16]{1,0:T(8,128)S(1)} %collective-permute-done.13, f32[16,16]{1,0:T(8,128)S(1)} %contract.1, f32[16,16]{1,0:T(8,128)S(1)} %collective-permute-done.11), kind=kLoop, calls=%fused_computation.3 | loop fusion | flops 768 | bytes 5120 | tf_op jit(solution)/shard_map/add | solution.py:421
  (1 shorter events, 0.0 us)
Async XLA Ops:
  1.4 8.8 %collective-permute-start.2 = (bf16[592,128]{1,0:T(8,128)(2,1)S(1)}, bf16[592,128]{1,0:T(8,128)(2,1)S(1)}, u32[]{:S(2)}, u32[]{:S(2)}) collective-permute-start(bf16[592,128]{1,0:T(8,128)(2,1)S(1)} %get-tuple-element.14), channel_id=1, source_target_pairs={{0,3},{1,2},{2,1},{3,0},{4,7},{5,6},{6,5},{7,4},{8,11},{9,10},{10,... | collective-permute-start | bytes 454664 | tf_op jit(solution)/shard_map/ppermute | solution.py:324
  5.4 8.5 %collective-permute-start = (bf16[784,128]{1,0:T(8,128)(2,1)S(1)}, bf16[784,128]{1,0:T(8,128)(2,1)S(1)}, u32[]{:S(2)}, u32[]{:S(2)}) collective-permute-start(bf16[784,128]{1,0:T(8,128)(2,1)S(1)} %get-tuple-element.12), channel_id=1, source_target_pairs={{0,1},{1,0},{2,3},{3,2},{4,5},{5,4},{6,7},{7,6},{8,9},{9,8},{10,11... | collective-permute-start | bytes 602120 | tf_op jit(solution)/shard_map/ppermute | solution.py:324
  5.9 8.0 %collective-permute-start.1 = (bf16[784,128]{1,0:T(8,128)(2,1)S(1)}, bf16[784,128]{1,0:T(8,128)(2,1)S(1)}, u32[]{:S(2)}, u32[]{:S(2)}) collective-permute-start(bf16[784,128]{1,0:T(8,128)(2,1)S(1)} %get-tuple-element.13), channel_id=1, source_target_pairs={{0,2},{1,3},{2,0},{3,1},{4,6},{5,7},{6,4},{7,5},{8,10},{9,11},{10,... | collective-permute-start | bytes 602120 | tf_op jit(solution)/shard_map/ppermute | solution.py:324
  10.2 3.7 %collective-permute-start.3 = (bf16[592,128]{1,0:T(8,128)(2,1)S(1)}, bf16[592,128]{1,0:T(8,128)(2,1)S(1)}, u32[]{:S(2)}, u32[]{:S(2)}) collective-permute-start(bf16[592,128]{1,0:T(8,128)(2,1)S(1)} %collective-permute-done.2.refs_2_), channel_id=1, source_target_pairs={{0,4},{4,0},{8,12},{12,8},{16,20},{20,16},{24,28},{28,24},{1,5},{5... | collective-permute-start | bytes 454664 | tf_op jit(solution)/shard_map/ppermute | solution.py:324
  15.0 3.7 %collective-permute-start.5 = (bf16[520,128]{1,0:T(8,128)(2,1)S(1)}, bf16[520,128]{1,0:T(8,128)(2,1)S(1)}, u32[]{:S(2)}, u32[]{:S(2)}) collective-permute-start(bf16[520,128]{1,0:T(8,128)(2,1)S(1)} %transform.1.refs_0_), channel_id=1, source_target_pairs={{0,4},{4,0},{8,16},{12,20},{16,8},{20,12},{24,28},{28,24},{1,5},{5... | collective-permute-start | bytes 399368 | tf_op jit(solution)/shard_map/ppermute | solution.py:333
  15.1 8.5 %collective-permute-start.4 = (bf16[520,128]{1,0:T(8,128)(2,1)S(1)}, bf16[520,128]{1,0:T(8,128)(2,1)S(1)}, u32[]{:S(2)}, u32[]{:S(2)}) collective-permute-start(bf16[520,128]{1,0:T(8,128)(2,1)S(1)} %transform.1.refs_0_), channel_id=1, source_target_pairs={{0,24},{4,28},{8,12},{12,8},{16,20},{20,16},{24,0},{28,4},{1,25},{... | collective-permute-start | bytes 399368 | tf_op jit(solution)/shard_map/ppermute | solution.py:333
  18.7 7.2 %collective-permute-start.6 = (bf16[520,128]{1,0:T(8,128)(2,1)S(1)}, bf16[520,128]{1,0:T(8,128)(2,1)S(1)}, u32[]{:S(2)}, u32[]{:S(2)}) collective-permute-start(bf16[520,128]{1,0:T(8,128)(2,1)S(1)} %transform.1.refs_0_), channel_id=1, source_target_pairs={{0,8},{4,12},{8,0},{12,4},{16,24},{20,28},{24,16},{28,20},{1,9},{5... | collective-permute-start | bytes 399368 | tf_op jit(solution)/shard_map/ppermute | solution.py:333
  18.8 9.9 %collective-permute-start.8 = (bf16[520,128]{1,0:T(8,128)(2,1)S(1)}, bf16[520,128]{1,0:T(8,128)(2,1)S(1)}, u32[]{:S(2)}, u32[]{:S(2)}) collective-permute-start(bf16[520,128]{1,0:T(8,128)(2,1)S(1)} %broadcast_select_fusion.2), channel_id=1, source_target_pairs={{0,16},{4,20},{8,0},{12,4},{16,24},{20,28},{24,8},{28,12},{1,17},{... | collective-permute-start | bytes 399368 | tf_op jit(solution)/shard_map/ppermute | solution.py:333
  23.6 5.0 %collective-permute-start.10 = (bf16[520,128]{1,0:T(8,128)(2,1)S(1)}, bf16[520,128]{1,0:T(8,128)(2,1)S(1)}, u32[]{:S(2)}, u32[]{:S(2)}) collective-permute-start(bf16[520,128]{1,0:T(8,128)(2,1)S(1)} %get-tuple-element.19.refs_6_), channel_id=1, source_target_pairs={{0,4},{4,0},{8,12},{12,8},{16,20},{20,16},{24,28},{28,24},{1,5},{5... | collective-permute-start | bytes 399368 | tf_op jit(solution)/shard_map/ppermute | solution.py:324
  25.9 2.8 %collective-permute-start.7 = (bf16[520,128]{1,0:T(8,128)(2,1)S(1)}, bf16[520,128]{1,0:T(8,128)(2,1)S(1)}, u32[]{:S(2)}, u32[]{:S(2)}) collective-permute-start(bf16[520,128]{1,0:T(8,128)(2,1)S(1)} %collective-permute-done.6.refs_2_), channel_id=1, source_target_pairs={{0,4},{4,0},{8,12},{12,8},{16,20},{20,16},{24,28},{28,24},{1,5},{5... | collective-permute-start | bytes 399368 | tf_op jit(solution)/shard_map/ppermute | solution.py:324
  28.6 1.4 %collective-permute-start.9 = (bf16[520,128]{1,0:T(8,128)(2,1)S(1)}, bf16[520,128]{1,0:T(8,128)(2,1)S(1)}, u32[]{:S(2)}, u32[]{:S(2)}) collective-permute-start(bf16[520,128]{1,0:T(8,128)(2,1)S(1)} %collective-permute-done.8.refs_4_), channel_id=1, source_target_pairs={{0,4},{4,0},{8,12},{12,8},{16,20},{20,16},{24,28},{28,24},{1,5},{5... | collective-permute-start | bytes 399368 | tf_op jit(solution)/shard_map/ppermute | solution.py:324
  30.9 3.7 %collective-permute-start.12 = (f32[16,16]{1,0:T(8,128)S(1)}, f32[16,16]{1,0:T(8,128)S(1)}, u32[]{:S(2)}, u32[]{:S(2)}) collective-permute-start(f32[16,16]{1,0:T(8,128)S(1)} %contract.1), channel_id=1, source_target_pairs={{0,2},{1,3},{2,0},{3,1},{4,6},{5,7},{6,4},{7,5},{8,10},{9,11},{10,... | collective-permute-start | bytes 3080 | tf_op jit(solution)/shard_map/ppermute | solution.py:324
  32.3 4.5 %collective-permute-start.13 = (f32[16,16]{1,0:T(8,128)S(1)}, f32[16,16]{1,0:T(8,128)S(1)}, u32[]{:S(2)}, u32[]{:S(2)}) collective-permute-start(f32[16,16]{1,0:T(8,128)S(1)} %contract.1), channel_id=1, source_target_pairs={{0,3},{1,2},{2,1},{3,0},{4,7},{5,6},{6,5},{7,4},{8,11},{9,10},{10,... | collective-permute-start | bytes 3080 | tf_op jit(solution)/shard_map/ppermute | solution.py:324
  33.8 3.7 %collective-permute-start.11 = (f32[16,16]{1,0:T(8,128)S(1)}, f32[16,16]{1,0:T(8,128)S(1)}, u32[]{:S(2)}, u32[]{:S(2)}) collective-permute-start(f32[16,16]{1,0:T(8,128)S(1)} %contract.1), channel_id=1, source_target_pairs={{0,1},{1,0},{2,3},{3,2},{4,5},{5,4},{6,7},{7,6},{8,9},{9,8},{10,11... | collective-permute-start | bytes 3080 | tf_op jit(solution)/shard_map/ppermute | solution.py:324

commit v7 on v6

--- a/solution.py
+++ b/solution.py
@@ -48,8 +48,7 @@
 
 
 def prep_kernel(*refs):
-    hbm, outs, copied, mask_ref, sems = refs[:5], refs[5:-7], refs[-7:-2], refs[-2], refs[-1]
-    own_ref, screen_ref, pay_refs = outs[0], outs[1], outs[2:]
+    hbm, mask_ref, pay_refs, copied, sems = refs[:5], refs[5], refs[6:-6], refs[-6:-1], refs[-1]
     copies = []
     for i, (src, dst) in enumerate(zip(hbm, copied)):
         parts = [(src, dst)] if i < 2 else [(src.at[x], dst.at[x]) for x in pieces(src.shape)]
@@ -90,37 +89,40 @@
     below, on = tri_masks(block)
     for copy in copies[2:]:
         copy.wait()
-    slab_blocks, green_blocks = [], []
-    for k in range(ao):
+    even = (lax.axis_index("ri") & 1) == 0
+    rows, size = block // 2, (ao - 1) * block
+
+    def put(place, k, whole):
+        for m in range(1, ao):
+            if m == k:
+                continue
+            value, step = whole, block
+            if place == 1 and shared(m, ao):
+                value, step = jnp.where(even, whole[:rows], whole[rows:]), rows
+            at = place * size + ((ao - 2) if k == 0 else k - 1 - (k > m)) * step
+            pay_refs[m - 1][at : at + step, :] = value
+
+    tails = []
+    for k in range(1, ao + 1):
+        k %= ao
         screen = block_at(mask_ref, a ^ k, block)
-        span = slice(k * block, (k + 1) * block)
-        screen_ref[:, span] = screen
         cols = pl.ds(pl.multiple_of((a ^ k) * block, block), block)
-        slabs = [slab_ref[q, :, cols] * screen for q in range(2)]
-        greens = [occ_ref[:, cols], virt_ref[:, cols]]
-        own_ref[0, :, span], own_ref[1, :, span] = slabs
-        own_ref[2, :, span], own_ref[3, :, span] = greens
-        if k == 0:
-            folded = [fold_diagonal(x.astype(f32), y.astype(f32), below, on) for x, y in (slabs, greens)]
-        else:
-            first = which(a, k) == 0
-            slab_blocks.append(jnp.where(first, *slabs))
-            green_blocks.append(jnp.where(first, *greens))
-    slab_blocks.append(folded[0][0].astype(bf16))
-    green_blocks.append(folded[1][0].astype(bf16))
+        for place in range(2):
+            if place == 0:
+                pair = [slab_ref[q, :, cols] * screen for q in range(2)]
+            else:
+                pair = [occ_ref[:, cols], virt_ref[:, cols]]
+            if k:
+                value = jnp.where(which(a, k) == 0, *pair)
+            else:
+                value, diagonal = fold_diagonal(*(x.astype(f32) for x in pair), below, on)
+                value = value.astype(bf16)
+                tails.append(diagonal)
+            put(place, k, value)
     upper = lax.broadcasted_iota(jnp.int32, (2 * TAIL, block), 0) < TAIL
-    tail = jnp.where(upper, folded[0][1], folded[1][1]).astype(bf16)
-
-    even = (lax.axis_index("ri") & 1) == 0
-    rows = block // 2
-    for k in range(1, ao):
-        parts = green_blocks[: k - 1] + green_blocks[k:]
-        if shared(k, ao):
-            parts = [jnp.where(even, x[:rows], x[rows:]) for x in parts]
-        at = 0
-        for part in slab_blocks[: k - 1] + slab_blocks[k:] + parts + [tail]:
-            pay_refs[k - 1][at : at + part.shape[0], :] = part
-            at += part.shape[0]
+    tail = jnp.where(upper, *tails).astype(bf16)
+    for ref in pay_refs:
+        ref[ref.shape[0] - 2 * TAIL :, :] = tail
 
 
 def reader(ref, base, m, ao, block):
@@ -197,13 +199,13 @@
     def own(first):
         return lambda q, k: own_ref[first + q, :, k * block : (k + 1) * block]
 
-    unfold(greens, diagonals[1], own(2), a, ao, block, put_green)
     unfold(slabs, diagonals[0], own(0), a, ao, block, put_slab)
-    both = jnp.concatenate([green_ref[0, :, total:], green_ref[0, :, :total]], axis=0)
+    both = own_ref[2:4].reshape(2 * block, total)
     for q in range(2):
         left = jnp.dot(both, slab_ref[q], preferred_element_type=f32).astype(bf16)
         left_ref[q, :, :total] = left[:block]
         left_ref[q, :, total:] = left[block:]
+    unfold(greens, diagonals[1], own(2), a, ao, block, put_green)
     last = (((1,), (1,)), ((), ()))
     below, on = tri_masks(block)
 
@@ -230,12 +232,27 @@
     out_ref[at + block :, :] = jnp.broadcast_to(diagonal, (TAIL, block)).astype(bf16)
 
 
-def stage_kernel(tensor_hbm, _, out_ref, tensor_ref, rows_ref, sem):
+def stage_kernel(tensor_hbm, slab_hbm, occ_hbm, virt_hbm, mask_ref, out_ref, own_ref, screen_ref, *scratch):
+    tensor_ref, slab_ref, occ_ref, virt_ref, rows_ref, sems = scratch
     ri_rows, block, _ = tensor_ref.shape
     a = lax.axis_index("ao")
-    copy = pltpu.make_async_copy(tensor_hbm, tensor_ref, sem)
-    copy.start()
-    copy.wait()
+    sources = (slab_hbm, occ_hbm, virt_hbm, tensor_hbm)
+    targets = (slab_ref, occ_ref, virt_ref, tensor_ref)
+    copies = [pltpu.make_async_copy(x, y, sems.at[i]) for i, (x, y) in enumerate(zip(sources, targets))]
+    for copy in copies:
+        copy.start()
+    for copy in copies[:3]:
+        copy.wait()
+    for k in range(out_ref.shape[0]):
+        cols = pl.ds(pl.multiple_of((a ^ k) * block, block), block)
+        span = slice(k * block, (k + 1) * block)
+        screen = mask_ref[:, cols]
+        screen_ref[:, span] = screen
+        for q in range(2):
+            own_ref[q, :, span] = slab_ref[q, :, cols] * screen
+        own_ref[2, :, span] = occ_ref[:, cols]
+        own_ref[3, :, span] = virt_ref[:, cols]
+    copies[3].wait()
     for k in range(out_ref.shape[0]):
         cols = pl.ds(pl.multiple_of((a ^ k) * block, block), block)
         for g in range(block // TILE):
@@ -285,19 +302,20 @@
         return jnp.where(same, values, 0.0).reshape(count, TILE, width).sum(axis=1)
 
     traces = [trace(sums[:half]), trace(sums[half:])]
-    for k in range(1, ao):
-        start = (k - 1) * block
+    first = max(1, ao // 2)
+    while first >= 1 and ao > 1:
+        lefts = [
+            spread(pays, lambda pay, rows, at=(k - 1) * block: pay[at + rows.start : at + rows.stop, :])
+            for k in range(first, 2 * first)
+        ]
+        rights = tensor_ref[first : 2 * first].reshape(first * groups * block, width)
         part = trace(
-            lax.dot_general(
-                spread(pays, lambda pay, rows: pay[start + rows.start : start + rows.stop, :]),
-                tensor_ref[k],
-                plain,
-                preferred_element_type=f32,
-            )
+            lax.dot_general(jnp.concatenate(lefts, axis=1), rights, plain, preferred_element_type=f32)
         )
-        to_first = which(a, k) == 0
+        to_first = which(a, first) == 0
         traces[0] = traces[0] + jnp.where(to_first, part, 0.0)
         traces[1] = traces[1] + jnp.where(to_first, 0.0, part)
+        first //= 2
     traces = jnp.concatenate(traces, axis=0)
     pick = (
         lax.shift_right_logical(lax.broadcasted_iota(jnp.int32, (ri_rows, width), 1), jnp.int32(4))
@@ -365,35 +383,37 @@
     sizes = [size + (size // 2 if shared(k, ao) else size) + 2 * TAIL for k in range(1, ao)]
     prepared = pl.pallas_call(
         prep_kernel,
-        out_shape=[jax.ShapeDtypeStruct((4, block, total), bf16), jax.ShapeDtypeStruct((block, total), bf16)]
+        out_shape=[jax.ShapeDtypeStruct((block, total), bf16)]
         + [jax.ShapeDtypeStruct((rows, block), bf16) for rows in sizes],
         in_specs=[pl.BlockSpec(memory_space=pltpu.HBM)] * 5,
-        out_specs=[vmem] * (2 + len(sizes)),
+        out_specs=[vmem] * (1 + len(sizes)),
         scratch_shapes=[pltpu.VMEM(x.shape, x.dtype) for x in inputs]
-        + [pltpu.VMEM((block, total), bf16), pltpu.SemaphoreType.DMA((2 + sum(len(pieces(x.shape)) for x in inputs[2:]),))],
+        + [pltpu.SemaphoreType.DMA((2 + sum(len(pieces(x.shape)) for x in inputs[2:]),))],
         compiler_params=room((sum(sizes), block), (5 * block, total), (2 * block, 2 * total)),
         name="prep",
     )(*inputs)
-    own, screen, *pays = prepared
+    mask, *pays = prepared
     arrived = []
     for k, pay in enumerate(pays, 1):
         arrived.append(exchange(pay, "ao", ao, k))
     pays = arrived + [exchange(x, "ri", ri, 1) for k, x in enumerate(arrived, 1) if shared(k, ao)]
     groups = block // TILE
-    staged = pl.pallas_call(
+    rows = ri_rows * TILE
+    staged, own, screen = pl.pallas_call(
         stage_kernel,
-        out_shape=jax.ShapeDtypeStruct((ao, groups * block, ri_rows * TILE), bf16),
-        in_specs=[pl.BlockSpec(memory_space=pltpu.HBM)] * 2,
-        out_specs=vmem,
-        scratch_shapes=[
-            pltpu.VMEM(three_center.shape, bf16),
-            pltpu.VMEM((ri_rows * TILE, block), bf16),
-            pltpu.SemaphoreType.DMA,
+        out_shape=[
+            jax.ShapeDtypeStruct((ao, groups * block, rows), bf16),
+            jax.ShapeDtypeStruct((4, block, total), bf16),
+            jax.ShapeDtypeStruct((block, total), bf16),
         ],
-        compiler_params=room((2 * ri_rows, block, total)),
+        in_specs=[pl.BlockSpec(memory_space=pltpu.HBM)] * 4 + [vmem],
+        out_specs=[vmem] * 3,
+        scratch_shapes=[pltpu.VMEM(x.shape, bf16) for x in (three_center, *inputs[2:])]
+        + [pltpu.VMEM((rows, block), bf16), pltpu.SemaphoreType.DMA((4,))],
+        compiler_params=room((2 * ri_rows, block, total), (8 * block, total)),
         cost_estimate=pl.CostEstimate(flops=0, transcendentals=0, bytes_accessed=8 * ri_rows * block * total),
         name="stage",
-    )(pltpu.with_memory_space_constraint(three_center, pltpu.HBM), screen)
+    )(pltpu.with_memory_space_constraint(three_center, pltpu.HBM), *inputs[2:], mask)
     weighted = pl.pallas_call(
         lambda *refs: transform_kernel(ao, block, *refs),
         out_shape=jax.ShapeDtypeStruct((half, block), bf16),

time: 38.3 us -> 38.2 us (level)
  waiting for transfers between devices: 15 us -> 12.6 us
  starting transfers between devices: 16.7 us -> 18.9 us
    ppermute x4, waiting for transfers between devices: 4.94 us -> 2.82 us  [along(): return lax.ppermute(value, 'ri', pairs)]
    ppermute x4, starting transfers between devices: 8.52 us -> 10.4 us  [along(): return lax.ppermute(value, 'ri', pairs)]
  transfers between devices with their start and end apart: 14 -> 14, of which waited for: 8 -> 8; matrix products, arithmetic and copies ran while one was open for 0% -> 0% of each run, Pallas kernels for 6% -> 7%
where the time goes in v7:
time: 38.2 us; the launch traced here: 38 us
  starting transfers between devices  18.9 us (49%)
  waiting for transfers between devices  12.6 us (33%)
  Pallas kernels  5.7 us (15%)
  other arithmetic  0.7 us (2%)
    ppermute x4, starting transfers between devices, along(): return lax.ppermute(value, 'ri', pairs)  10.4 us
    ppermute x10, waiting for transfers between devices, exchange(): return lax.ppermute(value, axis, [(i, i ^ k) for i in range(size)])  9.81 us
    ppermute x10, starting transfers between devices, exchange(): return lax.ppermute(value, axis, [(i, i ^ k) for i in range(size)])  8.45 us
    ppermute x4, waiting for transfers between devices, along(): return lax.ppermute(value, 'ri', pairs)  2.82 us
    pallas_call x1, Pallas kernels, shards(): pl.pallas_call(stage_kernel, out_shape=[jax.ShapeDtypeStruct((ao, groups...  2.51 us
    pallas_call x1, Pallas kernels, shards(): pl.pallas_call(prep_kernel, out_shape=[jax.ShapeDtypeStruct((block, total...  1.3 us
    pallas_call x1, Pallas kernels, shards(): pl.pallas_call(lambda *refs: transform_kernel(ao, block, *refs), out_shap...  1.04 us
    pallas_call x1, Pallas kernels, shards(): pl.pallas_call(lambda *refs: contract_kernel(ri, ao, block, *refs), out_s...  0.86 us
  transfers between devices with their start and end apart: 14, of which 8 were waited for; matrix products, arithmetic and copies ran while one was open for 0% of the time, Pallas kernels for 7%

profile of v7, /device:TPU:0, one launch (start us, length us, event | category | flops | bytes accessed | tf_op | source)
XLA Modules:
  0.0 38.0 jit_solution(1468019267524002599)
XLA Ops:
  0.0 1.3 %prep.1 = (bf16[128,512]{1,0:T(8,128)(2,1)S(1)}, bf16[784,128]{1,0:T(8,128)(2,1)S(1)}, bf16[784,128]{1,0:T(8,128)(2,1)S(1)}, bf16[592,128]{1,0:T(8,128)(2,1)S(1)}) custom-call(s32[1,32]{1,0:T(1,128)} %bitcast.1, s32[32,32]{1,0:T(8,128)} %refs_1_.1, bf16[2,128,512]{2,1,0:T(8,128)(2,1)} %slab_hbm.1, bf16[128,512]{1,0:T(8,128)(2,1)} %occ_hbm.1, ...), custom_call_target="tpu_custom_call" | custom-call | tf_op jit(solution)/shard_map/prep/pallas_call | solution.py:384
  1.3 4.0 %collective-permute-start.2 = (bf16[592,128]{1,0:T(8,128)(2,1)S(1)}, bf16[592,128]{1,0:T(8,128)(2,1)S(1)}, u32[]{:S(2)}, u32[]{:S(2)}) collective-permute-start(bf16[592,128]{1,0:T(8,128)(2,1)S(1)} %get-tuple-element.16), channel_id=1, source_target_pairs={{0,3},{1,2},{2,1},{3,0},{4,7},{5,6},{6,5},{7,4},{8,11},{9,10},{10,... | collective-permute-start | bytes 454664 | tf_op jit(solution)/shard_map/ppermute | solution.py:342
  5.3 0.5 %collective-permute-start = (bf16[784,128]{1,0:T(8,128)(2,1)S(1)}, bf16[784,128]{1,0:T(8,128)(2,1)S(1)}, u32[]{:S(2)}, u32[]{:S(2)}) collective-permute-start(bf16[784,128]{1,0:T(8,128)(2,1)S(1)} %get-tuple-element.14), channel_id=1, source_target_pairs={{0,1},{1,0},{2,3},{3,2},{4,5},{5,4},{6,7},{7,6},{8,9},{9,8},{10,11... | collective-permute-start | bytes 602120 | tf_op jit(solution)/shard_map/ppermute | solution.py:342
  5.8 0.1 collective-permute-start.1
  5.9 4.1 %collective-permute-done.2.refs_2_ = bf16[592,128]{1,0:T(8,128)(2,1)S(1)} collective-permute-done((bf16[592,128]{1,0:T(8,128)(2,1)S(1)}, bf16[592,128]{1,0:T(8,128)(2,1)S(1)}, u32[]{:S(2)}, u32[]{:S(2)}) %collective-permute-start.2) | collective-permute-done | bytes 151584 | tf_op jit(solution)/shard_map/ppermute | solution.py:342
  10.1 0.0 collective-permute-start.3
  10.1 2.5 %stage.1 = (bf16[4,1024,256]{2,1,0:T(8,128)(2,1)S(1)}, bf16[4,128,512]{2,1,0:T(8,128)(2,1)S(1)}, bf16[128,512]{1,0:T(8,128)(2,1)S(1)}) custom-call(bf16[16,128,512]{2,1,0:T(8,128)(2,1)} %tensor_hbm.1, bf16[2,128,512]{2,1,0:T(8,128)(2,1)} %slab_hbm.1, bf16[128,512]{1,0:T(8,128)(2,1)} %occ_hbm.1, bf16[128,512]{1,0:T(8,128)(2,1)} %virt_hbm.1, ...), custom_call_target="tpu_custom_call" | custom-call | bytes 8388608 | tf_op jit(solution)/shard_map/stage/pallas_call | solution.py:402
  12.6 1.2 %collective-permute-done.refs_0_ = bf16[784,128]{1,0:T(8,128)(2,1)S(1)} collective-permute-done((bf16[784,128]{1,0:T(8,128)(2,1)S(1)}, bf16[784,128]{1,0:T(8,128)(2,1)S(1)}, u32[]{:S(2)}, u32[]{:S(2)}) %collective-permute-start) | collective-permute-done | bytes 200736 | tf_op jit(solution)/shard_map/ppermute | solution.py:342
  13.8 0.0 collective-permute-done.1.refs_1_
  13.8 0.0 collective-permute-done.3.refs_3_
  13.8 1.0 %transform.1.refs_0_ = bf16[520,128]{1,0:T(8,128)(2,1)S(1)} custom-call(bf16[784,128]{1,0:T(8,128)(2,1)S(1)} %collective-permute-done.refs_0_, bf16[784,128]{1,0:T(8,128)(2,1)S(1)} %collective-permute-done.1.refs_1_, bf16[592,128]{1,0:T(8,128)(2,1)S(1)} %collective-permute-done.2.refs_2_, bf16[592,128]{1,0:T(8,128)(2,1)S(1)} %collective-permute-done.3.refs_3_, ...), custom_call_target="tpu_custom_call" | custom-call | tf_op jit(solution)/shard_map/transform/pallas_call | solution.py:417
  14.9 0.1 collective-permute-start.5
  14.9 3.6 %collective-permute-start.4 = (bf16[520,128]{1,0:T(8,128)(2,1)S(1)}, bf16[520,128]{1,0:T(8,128)(2,1)S(1)}, u32[]{:S(2)}, u32[]{:S(2)}) collective-permute-start(bf16[520,128]{1,0:T(8,128)(2,1)S(1)} %transform.1.refs_0_), channel_id=1, source_target_pairs={{0,24},{4,28},{8,12},{12,8},{16,20},{20,16},{24,0},{28,4},{1,25},{... | collective-permute-start | bytes 399368 | tf_op jit(solution)/shard_map/ppermute | solution.py:351
  18.6 0.0 collective-permute-start.6
  18.6 0.0 collective-permute-done.5
  18.6 6.7 %collective-permute-start.8 = (bf16[520,128]{1,0:T(8,128)(2,1)S(1)}, bf16[520,128]{1,0:T(8,128)(2,1)S(1)}, u32[]{:S(2)}, u32[]{:S(2)}) collective-permute-start(bf16[520,128]{1,0:T(8,128)(2,1)S(1)} %broadcast_select_fusion.2), channel_id=1, source_target_pairs={{0,16},{4,20},{8,0},{12,4},{16,24},{20,28},{24,8},{28,12},{1,17},{... | collective-permute-start | bytes 399368 | tf_op jit(solution)/shard_map/ppermute | solution.py:351
  25.3 0.0 collective-permute-done.4
  25.3 0.1 broadcast_select_fusion
  25.4 0.1 collective-permute-start.10
  25.5 0.3 collective-permute-done.6.refs_2_
  25.8 0.2 collective-permute-start.7
  26.0 2.5 %collective-permute-done.8.refs_4_ = bf16[520,128]{1,0:T(8,128)(2,1)S(1)} collective-permute-done((bf16[520,128]{1,0:T(8,128)(2,1)S(1)}, bf16[520,128]{1,0:T(8,128)(2,1)S(1)}, u32[]{:S(2)}, u32[]{:S(2)}) %collective-permute-start.8) | collective-permute-done | bytes 133152 | tf_op jit(solution)/shard_map/ppermute | solution.py:351
  28.5 0.0 collective-permute-start.9
  28.5 0.0 collective-permute-done.7.refs_3_
  28.5 0.0 collective-permute-done.10.refs_7_
  28.5 1.3 %collective-permute-done.9.refs_5_ = bf16[520,128]{1,0:T(8,128)(2,1)S(1)} collective-permute-done((bf16[520,128]{1,0:T(8,128)(2,1)S(1)}, bf16[520,128]{1,0:T(8,128)(2,1)S(1)}, u32[]{:S(2)}, u32[]{:S(2)}) %collective-permute-start.9) | collective-permute-done | bytes 133152 | tf_op jit(solution)/shard_map/ppermute | solution.py:342
  29.9 0.9 %contract.1 = f32[16,16]{1,0:T(8,128)S(1)} custom-call(bf16[520,128]{1,0:T(8,128)(2,1)S(1)} %transform.1.refs_0_, bf16[520,128]{1,0:T(8,128)(2,1)S(1)} %get-tuple-element.24.refs_1_, bf16[520,128]{1,0:T(8,128)(2,1)S(1)} %collective-permute-done.6.refs_2_, bf16[520,128]{1,0:T(8,128)(2,1)S(1)} %collective-permute-done.7.refs_3_, ...), custom_call_target="tpu_custom_call" | custom-call | tf_op jit(solution)/shard_map/contract/pallas_call | solution.py:431
  30.7 1.5 %collective-permute-start.12 = (f32[16,16]{1,0:T(8,128)S(1)}, f32[16,16]{1,0:T(8,128)S(1)}, u32[]{:S(2)}, u32[]{:S(2)}) collective-permute-start(f32[16,16]{1,0:T(8,128)S(1)} %contract.1), channel_id=1, source_target_pairs={{0,2},{1,3},{2,0},{3,1},{4,6},{5,7},{6,4},{7,5},{8,10},{9,11},{10,... | collective-permute-start | bytes 3080 | tf_op jit(solution)/shard_map/ppermute | solution.py:342
  32.2 1.5 %collective-permute-start.13 = (f32[16,16]{1,0:T(8,128)S(1)}, f32[16,16]{1,0:T(8,128)S(1)}, u32[]{:S(2)}, u32[]{:S(2)}) collective-permute-start(f32[16,16]{1,0:T(8,128)S(1)} %contract.1), channel_id=1, source_target_pairs={{0,3},{1,2},{2,1},{3,0},{4,7},{5,6},{6,5},{7,4},{8,11},{9,10},{10,... | collective-permute-start | bytes 3080 | tf_op jit(solution)/shard_map/ppermute | solution.py:342
  33.7 0.5 %collective-permute-start.11 = (f32[16,16]{1,0:T(8,128)S(1)}, f32[16,16]{1,0:T(8,128)S(1)}, u32[]{:S(2)}, u32[]{:S(2)}) collective-permute-start(f32[16,16]{1,0:T(8,128)S(1)} %contract.1), channel_id=1, source_target_pairs={{0,1},{1,0},{2,3},{3,2},{4,5},{5,4},{6,7},{7,6},{8,9},{9,8},{10,11... | collective-permute-start | bytes 3080 | tf_op jit(solution)/shard_map/ppermute | solution.py:342
  34.2 0.2 collective-permute-done.12
  34.4 2.3 %collective-permute-done.13 = f32[16,16]{1,0:T(8,128)S(1)} collective-permute-done((f32[16,16]{1,0:T(8,128)S(1)}, f32[16,16]{1,0:T(8,128)S(1)}, u32[]{:S(2)}, u32[]{:S(2)}) %collective-permute-start.13) | collective-permute-done | bytes 1056 | tf_op jit(solution)/shard_map/ppermute | solution.py:342
  36.7 0.6 %collective-permute-done.11 = f32[16,16]{1,0:T(8,128)S(1)} collective-permute-done((f32[16,16]{1,0:T(8,128)S(1)}, f32[16,16]{1,0:T(8,128)S(1)}, u32[]{:S(2)}, u32[]{:S(2)}) %collective-permute-start.11) | collective-permute-done | bytes 1056 | tf_op jit(solution)/shard_map/ppermute | solution.py:342
  37.4 0.6 %add_add_fusion = f32[16,16]{1,0:T(8,128)} fusion(f32[16,16]{1,0:T(8,128)S(1)} %collective-permute-done.12, f32[16,16]{1,0:T(8,128)S(1)} %collective-permute-done.13, f32[16,16]{1,0:T(8,128)S(1)} %contract.1, f32[16,16]{1,0:T(8,128)S(1)} %collective-permute-done.11), kind=kLoop, calls=%fused_computation.3 | loop fusion | flops 768 | bytes 5120 | tf_op jit(solution)/shard_map/add | solution.py:441
  (1 shorter events, 0.0 us)
Async XLA Ops:
  1.3 8.8 %collective-permute-start.2 = (bf16[592,128]{1,0:T(8,128)(2,1)S(1)}, bf16[592,128]{1,0:T(8,128)(2,1)S(1)}, u32[]{:S(2)}, u32[]{:S(2)}) collective-permute-start(bf16[592,128]{1,0:T(8,128)(2,1)S(1)} %get-tuple-element.16), channel_id=1, source_target_pairs={{0,3},{1,2},{2,1},{3,0},{4,7},{5,6},{6,5},{7,4},{8,11},{9,10},{10,... | collective-permute-start | bytes 454664 | tf_op jit(solution)/shard_map/ppermute | solution.py:342
  5.3 8.5 %collective-permute-start = (bf16[784,128]{1,0:T(8,128)(2,1)S(1)}, bf16[784,128]{1,0:T(8,128)(2,1)S(1)}, u32[]{:S(2)}, u32[]{:S(2)}) collective-permute-start(bf16[784,128]{1,0:T(8,128)(2,1)S(1)} %get-tuple-element.14), channel_id=1, source_target_pairs={{0,1},{1,0},{2,3},{3,2},{4,5},{5,4},{6,7},{7,6},{8,9},{9,8},{10,11... | collective-permute-start | bytes 602120 | tf_op jit(solution)/shard_map/ppermute | solution.py:342
  5.8 8.0 %collective-permute-start.1 = (bf16[784,128]{1,0:T(8,128)(2,1)S(1)}, bf16[784,128]{1,0:T(8,128)(2,1)S(1)}, u32[]{:S(2)}, u32[]{:S(2)}) collective-permute-start(bf16[784,128]{1,0:T(8,128)(2,1)S(1)} %get-tuple-element.15), channel_id=1, source_target_pairs={{0,2},{1,3},{2,0},{3,1},{4,6},{5,7},{6,4},{7,5},{8,10},{9,11},{10,... | collective-permute-start | bytes 602120 | tf_op jit(solution)/shard_map/ppermute | solution.py:342
  10.1 3.7 %collective-permute-start.3 = (bf16[592,128]{1,0:T(8,128)(2,1)S(1)}, bf16[592,128]{1,0:T(8,128)(2,1)S(1)}, u32[]{:S(2)}, u32[]{:S(2)}) collective-permute-start(bf16[592,128]{1,0:T(8,128)(2,1)S(1)} %collective-permute-done.2.refs_2_), channel_id=1, source_target_pairs={{0,4},{4,0},{8,12},{12,8},{16,20},{20,16},{24,28},{28,24},{1,5},{5... | collective-permute-start | bytes 454664 | tf_op jit(solution)/shard_map/ppermute | solution.py:342
  14.9 3.7 %collective-permute-start.5 = (bf16[520,128]{1,0:T(8,128)(2,1)S(1)}, bf16[520,128]{1,0:T(8,128)(2,1)S(1)}, u32[]{:S(2)}, u32[]{:S(2)}) collective-permute-start(bf16[520,128]{1,0:T(8,128)(2,1)S(1)} %transform.1.refs_0_), channel_id=1, source_target_pairs={{0,4},{4,0},{8,16},{12,20},{16,8},{20,12},{24,28},{28,24},{1,5},{5... | collective-permute-start | bytes 399368 | tf_op jit(solution)/shard_map/ppermute | solution.py:351
  14.9 10.4 %collective-permute-start.4 = (bf16[520,128]{1,0:T(8,128)(2,1)S(1)}, bf16[520,128]{1,0:T(8,128)(2,1)S(1)}, u32[]{:S(2)}, u32[]{:S(2)}) collective-permute-start(bf16[520,128]{1,0:T(8,128)(2,1)S(1)} %transform.1.refs_0_), channel_id=1, source_target_pairs={{0,24},{4,28},{8,12},{12,8},{16,20},{20,16},{24,0},{28,4},{1,25},{... | collective-permute-start | bytes 399368 | tf_op jit(solution)/shard_map/ppermute | solution.py:351
  18.6 7.2 %collective-permute-start.6 = (bf16[520,128]{1,0:T(8,128)(2,1)S(1)}, bf16[520,128]{1,0:T(8,128)(2,1)S(1)}, u32[]{:S(2)}, u32[]{:S(2)}) collective-permute-start(bf16[520,128]{1,0:T(8,128)(2,1)S(1)} %transform.1.refs_0_), channel_id=1, source_target_pairs={{0,8},{4,12},{8,0},{12,4},{16,24},{20,28},{24,16},{28,20},{1,9},{5... | collective-permute-start | bytes 399368 | tf_op jit(solution)/shard_map/ppermute | solution.py:351
  18.6 9.9 %collective-permute-start.8 = (bf16[520,128]{1,0:T(8,128)(2,1)S(1)}, bf16[520,128]{1,0:T(8,128)(2,1)S(1)}, u32[]{:S(2)}, u32[]{:S(2)}) collective-permute-start(bf16[520,128]{1,0:T(8,128)(2,1)S(1)} %broadcast_select_fusion.2), channel_id=1, source_target_pairs={{0,16},{4,20},{8,0},{12,4},{16,24},{20,28},{24,8},{28,12},{1,17},{... | collective-permute-start | bytes 399368 | tf_op jit(solution)/shard_map/ppermute | solution.py:351
  25.4 3.1 %collective-permute-start.10 = (bf16[520,128]{1,0:T(8,128)(2,1)S(1)}, bf16[520,128]{1,0:T(8,128)(2,1)S(1)}, u32[]{:S(2)}, u32[]{:S(2)}) collective-permute-start(bf16[520,128]{1,0:T(8,128)(2,1)S(1)} %get-tuple-element.23.refs_6_), channel_id=1, source_target_pairs={{0,4},{4,0},{8,12},{12,8},{16,20},{20,16},{24,28},{28,24},{1,5},{5... | collective-permute-start | bytes 399368 | tf_op jit(solution)/shard_map/ppermute | solution.py:342
  25.8 2.8 %collective-permute-start.7 = (bf16[520,128]{1,0:T(8,128)(2,1)S(1)}, bf16[520,128]{1,0:T(8,128)(2,1)S(1)}, u32[]{:S(2)}, u32[]{:S(2)}) collective-permute-start(bf16[520,128]{1,0:T(8,128)(2,1)S(1)} %collective-permute-done.6.refs_2_), channel_id=1, source_target_pairs={{0,4},{4,0},{8,12},{12,8},{16,20},{20,16},{24,28},{28,24},{1,5},{5... | collective-permute-start | bytes 399368 | tf_op jit(solution)/shard_map/ppermute | solution.py:342
  28.5 1.4 %collective-permute-start.9 = (bf16[520,128]{1,0:T(8,128)(2,1)S(1)}, bf16[520,128]{1,0:T(8,128)(2,1)S(1)}, u32[]{:S(2)}, u32[]{:S(2)}) collective-permute-start(bf16[520,128]{1,0:T(8,128)(2,1)S(1)} %collective-permute-done.8.refs_4_), channel_id=1, source_target_pairs={{0,4},{4,0},{8,12},{12,8},{16,20},{20,16},{24,28},{28,24},{1,5},{5... | collective-permute-start | bytes 399368 | tf_op jit(solution)/shard_map/ppermute | solution.py:342
  30.7 3.7 %collective-permute-start.12 = (f32[16,16]{1,0:T(8,128)S(1)}, f32[16,16]{1,0:T(8,128)S(1)}, u32[]{:S(2)}, u32[]{:S(2)}) collective-permute-start(f32[16,16]{1,0:T(8,128)S(1)} %contract.1), channel_id=1, source_target_pairs={{0,2},{1,3},{2,0},{3,1},{4,6},{5,7},{6,4},{7,5},{8,10},{9,11},{10,... | collective-permute-start | bytes 3080 | tf_op jit(solution)/shard_map/ppermute | solution.py:342
  32.2 4.5 %collective-permute-start.13 = (f32[16,16]{1,0:T(8,128)S(1)}, f32[16,16]{1,0:T(8,128)S(1)}, u32[]{:S(2)}, u32[]{:S(2)}) collective-permute-start(f32[16,16]{1,0:T(8,128)S(1)} %contract.1), channel_id=1, source_target_pairs={{0,3},{1,2},{2,1},{3,0},{4,7},{5,6},{6,5},{7,4},{8,11},{9,10},{10,... | collective-permute-start | bytes 3080 | tf_op jit(solution)/shard_map/ppermute | solution.py:342
  33.7 3.7 %collective-permute-start.11 = (f32[16,16]{1,0:T(8,128)S(1)}, f32[16,16]{1,0:T(8,128)S(1)}, u32[]{:S(2)}, u32[]{:S(2)}) collective-permute-start(f32[16,16]{1,0:T(8,128)S(1)} %contract.1), channel_id=1, source_target_pairs={{0,1},{1,0},{2,3},{3,2},{4,5},{5,4},{6,7},{7,6},{8,9},{9,8},{10,11... | collective-permute-start | bytes 3080 | tf_op jit(solution)/shard_map/ppermute | solution.py:342

commit v8 on v7

--- a/solution.py
+++ b/solution.py
@@ -41,18 +41,11 @@
     return ref[:, pl.ds(pl.multiple_of(index * block, block), block)]
 
 
-def pieces(shape):
-    half = shape[-2] // 2
-    halves = [pl.ds(0, half), pl.ds(half, half)]
-    return halves if len(shape) == 2 else [(i, x) for i in range(shape[0]) for x in halves]
-
-
 def prep_kernel(*refs):
     hbm, mask_ref, pay_refs, copied, sems = refs[:5], refs[5], refs[6:-6], refs[-6:-1], refs[-1]
     copies = []
     for i, (src, dst) in enumerate(zip(hbm, copied)):
-        parts = [(src, dst)] if i < 2 else [(src.at[x], dst.at[x]) for x in pieces(src.shape)]
-        copies += [pltpu.make_async_copy(x, y, sems.at[len(copies) + n]) for n, (x, y) in enumerate(parts)]
+        copies.append(pltpu.make_async_copy(src, dst, sems.at[i]))
     for copy in copies:
         copy.start()
     sizes_ref, pattern_ref, slab_ref, occ_ref, virt_ref = copied
@@ -317,18 +310,32 @@
         traces[1] = traces[1] + jnp.where(to_first, 0.0, part)
         first //= 2
     traces = jnp.concatenate(traces, axis=0)
+
+    def parts(values):
+        out, rest = [], values
+        for _ in range(3):
+            out.append(rest.astype(bf16))
+            rest = rest - out[-1].astype(f32)
+        return jnp.concatenate(out, axis=0)
+
+    wide = 3 * 2 * count
+    target = lax.broadcasted_iota(jnp.int32, (2 * count, wide), 0)
+    source = lax.broadcasted_iota(jnp.int32, (2 * count, wide), 1)
+    source = jnp.where(source >= 4 * count, source - 4 * count, source)
+    source = jnp.where(source >= 2 * count, source - 2 * count, source)
+    second = source >= count
+    place = ((jnp.where(second, source - count, source) ^ r) * 2 + second.astype(jnp.int32)) == target
+    placed = jnp.dot(place.astype(f32).astype(bf16), parts(traces), preferred_element_type=f32)
     pick = (
         lax.shift_right_logical(lax.broadcasted_iota(jnp.int32, (ri_rows, width), 1), jnp.int32(4))
         == lax.broadcasted_iota(jnp.int32, (ri_rows, width), 0)
-    ).astype(f32)
-    by_source = lax.dot_general(
-        pick, traces, last, precision=lax.Precision.HIGHEST, preferred_element_type=f32
-    )
-    source = lax.broadcasted_iota(jnp.int32, (2 * count, 2 * count), 0)
-    target = lax.broadcasted_iota(jnp.int32, (2 * count, 2 * count), 1)
-    place = ((jnp.where(source < count, source, source - count) ^ r) * 2 + (source >= count).astype(jnp.int32)) == target
-    ordered = jnp.dot(
-        by_source, place.astype(f32), precision=lax.Precision.HIGHEST, preferred_element_type=f32
+    ).astype(f32).astype(bf16)
+    split = parts(placed)
+    ordered = sum(
+        lax.dot_general(
+            pick, split[n * 2 * count : (n + 1) * 2 * count], last, preferred_element_type=f32
+        )
+        for n in range(3)
     )
     out_ref[...] = ordered * (1.0 / (ao * block))
 
@@ -388,7 +395,7 @@
         in_specs=[pl.BlockSpec(memory_space=pltpu.HBM)] * 5,
         out_specs=[vmem] * (1 + len(sizes)),
         scratch_shapes=[pltpu.VMEM(x.shape, x.dtype) for x in inputs]
-        + [pltpu.SemaphoreType.DMA((2 + sum(len(pieces(x.shape)) for x in inputs[2:]),))],
+        + [pltpu.SemaphoreType.DMA((len(inputs),))],
         compiler_params=room((sum(sizes), block), (5 * block, total), (2 * block, 2 * total)),
         name="prep",
     )(*inputs)

time: 38.2 us -> 38 us (level)
  no operation moved by 1% of the time
where the time goes in v8:
time: 38 us; the launch traced here: 37.9 us
  starting transfers between devices  18.9 us (50%)
  waiting for transfers between devices  12.6 us (33%)
  Pallas kernels  5.6 us (15%)
  other arithmetic  0.7 us (2%)
    ppermute x4, starting transfers between devices, along(): return lax.ppermute(value, 'ri', pairs)  10.4 us
    ppermute x10, waiting for transfers between devices, exchange(): return lax.ppermute(value, axis, [(i, i ^ k) for i in range(size)])  9.81 us
    ppermute x10, starting transfers between devices, exchange(): return lax.ppermute(value, axis, [(i, i ^ k) for i in range(size)])  8.45 us
    ppermute x4, waiting for transfers between devices, along(): return lax.ppermute(value, 'ri', pairs)  2.8 us
    pallas_call x1, Pallas kernels, shards(): pl.pallas_call(stage_kernel, out_shape=[jax.ShapeDtypeStruct((ao, groups...  2.51 us
    pallas_call x1, Pallas kernels, shards(): pl.pallas_call(prep_kernel, out_shape=[jax.ShapeDtypeStruct((block, total...  1.24 us
    pallas_call x1, Pallas kernels, shards(): pl.pallas_call(lambda *refs: transform_kernel(ao, block, *refs), out_shap...  1.04 us
    pallas_call x1, Pallas kernels, shards(): pl.pallas_call(lambda *refs: contract_kernel(ri, ao, block, *refs), out_s...  0.81 us
  transfers between devices with their start and end apart: 14, of which 8 were waited for; matrix products, arithmetic and copies ran while one was open for 0% of the time, Pallas kernels for 7%

profile of v8, /device:TPU:0, one launch (start us, length us, event | category | flops | bytes accessed | tf_op | source)
XLA Modules:
  0.0 37.9 jit_solution(15563262227354744078)
XLA Ops:
  0.0 1.2 %prep.1 = (bf16[128,512]{1,0:T(8,128)(2,1)S(1)}, bf16[784,128]{1,0:T(8,128)(2,1)S(1)}, bf16[784,128]{1,0:T(8,128)(2,1)S(1)}, bf16[592,128]{1,0:T(8,128)(2,1)S(1)}) custom-call(s32[1,32]{1,0:T(1,128)} %bitcast.1, s32[32,32]{1,0:T(8,128)} %refs_1_.1, bf16[2,128,512]{2,1,0:T(8,128)(2,1)} %slab_hbm.1, bf16[128,512]{1,0:T(8,128)(2,1)} %occ_hbm.1, ...), custom_call_target="tpu_custom_call" | custom-call | tf_op jit(solution)/shard_map/prep/pallas_call | solution.py:391
  1.3 4.0 %collective-permute-start.2 = (bf16[592,128]{1,0:T(8,128)(2,1)S(1)}, bf16[592,128]{1,0:T(8,128)(2,1)S(1)}, u32[]{:S(2)}, u32[]{:S(2)}) collective-permute-start(bf16[592,128]{1,0:T(8,128)(2,1)S(1)} %get-tuple-element.16), channel_id=1, source_target_pairs={{0,3},{1,2},{2,1},{3,0},{4,7},{5,6},{6,5},{7,4},{8,11},{9,10},{10,... | collective-permute-start | bytes 454664 | tf_op jit(solution)/shard_map/ppermute | solution.py:349
  5.2 0.5 %collective-permute-start = (bf16[784,128]{1,0:T(8,128)(2,1)S(1)}, bf16[784,128]{1,0:T(8,128)(2,1)S(1)}, u32[]{:S(2)}, u32[]{:S(2)}) collective-permute-start(bf16[784,128]{1,0:T(8,128)(2,1)S(1)} %get-tuple-element.14), channel_id=1, source_target_pairs={{0,1},{1,0},{2,3},{3,2},{4,5},{5,4},{6,7},{7,6},{8,9},{9,8},{10,11... | collective-permute-start | bytes 602120 | tf_op jit(solution)/shard_map/ppermute | solution.py:349
  5.8 0.1 collective-permute-start.1
  5.9 4.1 %collective-permute-done.2.refs_2_ = bf16[592,128]{1,0:T(8,128)(2,1)S(1)} collective-permute-done((bf16[592,128]{1,0:T(8,128)(2,1)S(1)}, bf16[592,128]{1,0:T(8,128)(2,1)S(1)}, u32[]{:S(2)}, u32[]{:S(2)}) %collective-permute-start.2) | collective-permute-done | bytes 151584 | tf_op jit(solution)/shard_map/ppermute | solution.py:349
  10.0 0.0 collective-permute-start.3
  10.0 2.5 %stage.1 = (bf16[4,1024,256]{2,1,0:T(8,128)(2,1)S(1)}, bf16[4,128,512]{2,1,0:T(8,128)(2,1)S(1)}, bf16[128,512]{1,0:T(8,128)(2,1)S(1)}) custom-call(bf16[16,128,512]{2,1,0:T(8,128)(2,1)} %tensor_hbm.1, bf16[2,128,512]{2,1,0:T(8,128)(2,1)} %slab_hbm.1, bf16[128,512]{1,0:T(8,128)(2,1)} %occ_hbm.1, bf16[128,512]{1,0:T(8,128)(2,1)} %virt_hbm.1, ...), custom_call_target="tpu_custom_call" | custom-call | bytes 8388608 | tf_op jit(solution)/shard_map/stage/pallas_call | solution.py:409
  12.5 1.2 %collective-permute-done.refs_0_ = bf16[784,128]{1,0:T(8,128)(2,1)S(1)} collective-permute-done((bf16[784,128]{1,0:T(8,128)(2,1)S(1)}, bf16[784,128]{1,0:T(8,128)(2,1)S(1)}, u32[]{:S(2)}, u32[]{:S(2)}) %collective-permute-start) | collective-permute-done | bytes 200736 | tf_op jit(solution)/shard_map/ppermute | solution.py:349
  13.8 0.0 collective-permute-done.1.refs_1_
  13.8 0.0 collective-permute-done.3.refs_3_
  13.8 1.0 %transform.1.refs_0_ = bf16[520,128]{1,0:T(8,128)(2,1)S(1)} custom-call(bf16[784,128]{1,0:T(8,128)(2,1)S(1)} %collective-permute-done.refs_0_, bf16[784,128]{1,0:T(8,128)(2,1)S(1)} %collective-permute-done.1.refs_1_, bf16[592,128]{1,0:T(8,128)(2,1)S(1)} %collective-permute-done.2.refs_2_, bf16[592,128]{1,0:T(8,128)(2,1)S(1)} %collective-permute-done.3.refs_3_, ...), custom_call_target="tpu_custom_call" | custom-call | tf_op jit(solution)/shard_map/transform/pallas_call | solution.py:424
  14.8 0.1 collective-permute-start.5
  14.9 3.7 %collective-permute-start.4 = (bf16[520,128]{1,0:T(8,128)(2,1)S(1)}, bf16[520,128]{1,0:T(8,128)(2,1)S(1)}, u32[]{:S(2)}, u32[]{:S(2)}) collective-permute-start(bf16[520,128]{1,0:T(8,128)(2,1)S(1)} %transform.1.refs_0_), channel_id=1, source_target_pairs={{0,24},{4,28},{8,12},{12,8},{16,20},{20,16},{24,0},{28,4},{1,25},{... | collective-permute-start | bytes 399368 | tf_op jit(solution)/shard_map/ppermute | solution.py:358
  18.5 0.0 collective-permute-start.6
  18.5 0.0 collective-permute-done.5
  18.6 6.7 %collective-permute-start.8 = (bf16[520,128]{1,0:T(8,128)(2,1)S(1)}, bf16[520,128]{1,0:T(8,128)(2,1)S(1)}, u32[]{:S(2)}, u32[]{:S(2)}) collective-permute-start(bf16[520,128]{1,0:T(8,128)(2,1)S(1)} %broadcast_select_fusion.2), channel_id=1, source_target_pairs={{0,16},{4,20},{8,0},{12,4},{16,24},{20,28},{24,8},{28,12},{1,17},{... | collective-permute-start | bytes 399368 | tf_op jit(solution)/shard_map/ppermute | solution.py:358
  25.3 0.0 collective-permute-done.4
  25.3 0.1 broadcast_select_fusion
  25.4 0.1 collective-permute-start.10
  25.4 0.3 collective-permute-done.6.refs_2_
  25.7 0.2 collective-permute-start.7
  25.9 2.5 %collective-permute-done.8.refs_4_ = bf16[520,128]{1,0:T(8,128)(2,1)S(1)} collective-permute-done((bf16[520,128]{1,0:T(8,128)(2,1)S(1)}, bf16[520,128]{1,0:T(8,128)(2,1)S(1)}, u32[]{:S(2)}, u32[]{:S(2)}) %collective-permute-start.8) | collective-permute-done | bytes 133152 | tf_op jit(solution)/shard_map/ppermute | solution.py:358
  28.5 0.0 collective-permute-start.9
  28.5 0.0 collective-permute-done.7.refs_3_
  28.5 0.0 collective-permute-done.10.refs_7_
  28.5 1.3 %collective-permute-done.9.refs_5_ = bf16[520,128]{1,0:T(8,128)(2,1)S(1)} collective-permute-done((bf16[520,128]{1,0:T(8,128)(2,1)S(1)}, bf16[520,128]{1,0:T(8,128)(2,1)S(1)}, u32[]{:S(2)}, u32[]{:S(2)}) %collective-permute-start.9) | collective-permute-done | bytes 133152 | tf_op jit(solution)/shard_map/ppermute | solution.py:349
  29.8 0.8 %contract.1 = f32[16,16]{1,0:T(8,128)S(1)} custom-call(bf16[520,128]{1,0:T(8,128)(2,1)S(1)} %transform.1.refs_0_, bf16[520,128]{1,0:T(8,128)(2,1)S(1)} %get-tuple-element.24.refs_1_, bf16[520,128]{1,0:T(8,128)(2,1)S(1)} %collective-permute-done.6.refs_2_, bf16[520,128]{1,0:T(8,128)(2,1)S(1)} %collective-permute-done.7.refs_3_, ...), custom_call_target="tpu_custom_call" | custom-call | tf_op jit(solution)/shard_map/contract/pallas_call | solution.py:438
  30.6 1.5 %collective-permute-start.12 = (f32[16,16]{1,0:T(8,128)S(1)}, f32[16,16]{1,0:T(8,128)S(1)}, u32[]{:S(2)}, u32[]{:S(2)}) collective-permute-start(f32[16,16]{1,0:T(8,128)S(1)} %contract.1), channel_id=1, source_target_pairs={{0,2},{1,3},{2,0},{3,1},{4,6},{5,7},{6,4},{7,5},{8,10},{9,11},{10,... | collective-permute-start | bytes 3080 | tf_op jit(solution)/shard_map/ppermute | solution.py:349
  32.1 1.5 %collective-permute-start.13 = (f32[16,16]{1,0:T(8,128)S(1)}, f32[16,16]{1,0:T(8,128)S(1)}, u32[]{:S(2)}, u32[]{:S(2)}) collective-permute-start(f32[16,16]{1,0:T(8,128)S(1)} %contract.1), channel_id=1, source_target_pairs={{0,3},{1,2},{2,1},{3,0},{4,7},{5,6},{6,5},{7,4},{8,11},{9,10},{10,... | collective-permute-start | bytes 3080 | tf_op jit(solution)/shard_map/ppermute | solution.py:349
  33.6 0.5 %collective-permute-start.11 = (f32[16,16]{1,0:T(8,128)S(1)}, f32[16,16]{1,0:T(8,128)S(1)}, u32[]{:S(2)}, u32[]{:S(2)}) collective-permute-start(f32[16,16]{1,0:T(8,128)S(1)} %contract.1), channel_id=1, source_target_pairs={{0,1},{1,0},{2,3},{3,2},{4,5},{5,4},{6,7},{7,6},{8,9},{9,8},{10,11... | collective-permute-start | bytes 3080 | tf_op jit(solution)/shard_map/ppermute | solution.py:349
  34.1 0.2 collective-permute-done.12
  34.3 2.4 %collective-permute-done.13 = f32[16,16]{1,0:T(8,128)S(1)} collective-permute-done((f32[16,16]{1,0:T(8,128)S(1)}, f32[16,16]{1,0:T(8,128)S(1)}, u32[]{:S(2)}, u32[]{:S(2)}) %collective-permute-start.13) | collective-permute-done | bytes 1056 | tf_op jit(solution)/shard_map/ppermute | solution.py:349
  36.7 0.6 %collective-permute-done.11 = f32[16,16]{1,0:T(8,128)S(1)} collective-permute-done((f32[16,16]{1,0:T(8,128)S(1)}, f32[16,16]{1,0:T(8,128)S(1)}, u32[]{:S(2)}, u32[]{:S(2)}) %collective-permute-start.11) | collective-permute-done | bytes 1056 | tf_op jit(solution)/shard_map/ppermute | solution.py:349
  37.2 0.6 %add_add_fusion = f32[16,16]{1,0:T(8,128)} fusion(f32[16,16]{1,0:T(8,128)S(1)} %collective-permute-done.12, f32[16,16]{1,0:T(8,128)S(1)} %collective-permute-done.13, f32[16,16]{1,0:T(8,128)S(1)} %contract.1, f32[16,16]{1,0:T(8,128)S(1)} %collective-permute-done.11), kind=kLoop, calls=%fused_computation.3 | loop fusion | flops 768 | bytes 5120 | tf_op jit(solution)/shard_map/add | solution.py:448
  (1 shorter events, 0.0 us)
Async XLA Ops:
  1.3 8.8 %collective-permute-start.2 = (bf16[592,128]{1,0:T(8,128)(2,1)S(1)}, bf16[592,128]{1,0:T(8,128)(2,1)S(1)}, u32[]{:S(2)}, u32[]{:S(2)}) collective-permute-start(bf16[592,128]{1,0:T(8,128)(2,1)S(1)} %get-tuple-element.16), channel_id=1, source_target_pairs={{0,3},{1,2},{2,1},{3,0},{4,7},{5,6},{6,5},{7,4},{8,11},{9,10},{10,... | collective-permute-start | bytes 454664 | tf_op jit(solution)/shard_map/ppermute | solution.py:349
  5.2 8.5 %collective-permute-start = (bf16[784,128]{1,0:T(8,128)(2,1)S(1)}, bf16[784,128]{1,0:T(8,128)(2,1)S(1)}, u32[]{:S(2)}, u32[]{:S(2)}) collective-permute-start(bf16[784,128]{1,0:T(8,128)(2,1)S(1)} %get-tuple-element.14), channel_id=1, source_target_pairs={{0,1},{1,0},{2,3},{3,2},{4,5},{5,4},{6,7},{7,6},{8,9},{9,8},{10,11... | collective-permute-start | bytes 602120 | tf_op jit(solution)/shard_map/ppermute | solution.py:349
  5.8 8.0 %collective-permute-start.1 = (bf16[784,128]{1,0:T(8,128)(2,1)S(1)}, bf16[784,128]{1,0:T(8,128)(2,1)S(1)}, u32[]{:S(2)}, u32[]{:S(2)}) collective-permute-start(bf16[784,128]{1,0:T(8,128)(2,1)S(1)} %get-tuple-element.15), channel_id=1, source_target_pairs={{0,2},{1,3},{2,0},{3,1},{4,6},{5,7},{6,4},{7,5},{8,10},{9,11},{10,... | collective-permute-start | bytes 602120 | tf_op jit(solution)/shard_map/ppermute | solution.py:349
  10.0 3.7 %collective-permute-start.3 = (bf16[592,128]{1,0:T(8,128)(2,1)S(1)}, bf16[592,128]{1,0:T(8,128)(2,1)S(1)}, u32[]{:S(2)}, u32[]{:S(2)}) collective-permute-start(bf16[592,128]{1,0:T(8,128)(2,1)S(1)} %collective-permute-done.2.refs_2_), channel_id=1, source_target_pairs={{0,4},{4,0},{8,12},{12,8},{16,20},{20,16},{24,28},{28,24},{1,5},{5... | collective-permute-start | bytes 454664 | tf_op jit(solution)/shard_map/ppermute | solution.py:349
  14.8 3.7 %collective-permute-start.5 = (bf16[520,128]{1,0:T(8,128)(2,1)S(1)}, bf16[520,128]{1,0:T(8,128)(2,1)S(1)}, u32[]{:S(2)}, u32[]{:S(2)}) collective-permute-start(bf16[520,128]{1,0:T(8,128)(2,1)S(1)} %transform.1.refs_0_), channel_id=1, source_target_pairs={{0,4},{4,0},{8,16},{12,20},{16,8},{20,12},{24,28},{28,24},{1,5},{5... | collective-permute-start | bytes 399368 | tf_op jit(solution)/shard_map/ppermute | solution.py:358
  14.9 10.4 %collective-permute-start.4 = (bf16[520,128]{1,0:T(8,128)(2,1)S(1)}, bf16[520,128]{1,0:T(8,128)(2,1)S(1)}, u32[]{:S(2)}, u32[]{:S(2)}) collective-permute-start(bf16[520,128]{1,0:T(8,128)(2,1)S(1)} %transform.1.refs_0_), channel_id=1, source_target_pairs={{0,24},{4,28},{8,12},{12,8},{16,20},{20,16},{24,0},{28,4},{1,25},{... | collective-permute-start | bytes 399368 | tf_op jit(solution)/shard_map/ppermute | solution.py:358
  18.5 7.2 %collective-permute-start.6 = (bf16[520,128]{1,0:T(8,128)(2,1)S(1)}, bf16[520,128]{1,0:T(8,128)(2,1)S(1)}, u32[]{:S(2)}, u32[]{:S(2)}) collective-permute-start(bf16[520,128]{1,0:T(8,128)(2,1)S(1)} %transform.1.refs_0_), channel_id=1, source_target_pairs={{0,8},{4,12},{8,0},{12,4},{16,24},{20,28},{24,16},{28,20},{1,9},{5... | collective-permute-start | bytes 399368 | tf_op jit(solution)/shard_map/ppermute | solution.py:358
  18.6 9.9 %collective-permute-start.8 = (bf16[520,128]{1,0:T(8,128)(2,1)S(1)}, bf16[520,128]{1,0:T(8,128)(2,1)S(1)}, u32[]{:S(2)}, u32[]{:S(2)}) collective-permute-start(bf16[520,128]{1,0:T(8,128)(2,1)S(1)} %broadcast_select_fusion.2), channel_id=1, source_target_pairs={{0,16},{4,20},{8,0},{12,4},{16,24},{20,28},{24,8},{28,12},{1,17},{... | collective-permute-start | bytes 399368 | tf_op jit(solution)/shard_map/ppermute | solution.py:358
  25.4 3.1 %collective-permute-start.10 = (bf16[520,128]{1,0:T(8,128)(2,1)S(1)}, bf16[520,128]{1,0:T(8,128)(2,1)S(1)}, u32[]{:S(2)}, u32[]{:S(2)}) collective-permute-start(bf16[520,128]{1,0:T(8,128)(2,1)S(1)} %get-tuple-element.23.refs_6_), channel_id=1, source_target_pairs={{0,4},{4,0},{8,12},{12,8},{16,20},{20,16},{24,28},{28,24},{1,5},{5... | collective-permute-start | bytes 399368 | tf_op jit(solution)/shard_map/ppermute | solution.py:349
  25.7 2.8 %collective-permute-start.7 = (bf16[520,128]{1,0:T(8,128)(2,1)S(1)}, bf16[520,128]{1,0:T(8,128)(2,1)S(1)}, u32[]{:S(2)}, u32[]{:S(2)}) collective-permute-start(bf16[520,128]{1,0:T(8,128)(2,1)S(1)} %collective-permute-done.6.refs_2_), channel_id=1, source_target_pairs={{0,4},{4,0},{8,12},{12,8},{16,20},{20,16},{24,28},{28,24},{1,5},{5... | collective-permute-start | bytes 399368 | tf_op jit(solution)/shard_map/ppermute | solution.py:349
  28.5 1.4 %collective-permute-start.9 = (bf16[520,128]{1,0:T(8,128)(2,1)S(1)}, bf16[520,128]{1,0:T(8,128)(2,1)S(1)}, u32[]{:S(2)}, u32[]{:S(2)}) collective-permute-start(bf16[520,128]{1,0:T(8,128)(2,1)S(1)} %collective-permute-done.8.refs_4_), channel_id=1, source_target_pairs={{0,4},{4,0},{8,12},{12,8},{16,20},{20,16},{24,28},{28,24},{1,5},{5... | collective-permute-start | bytes 399368 | tf_op jit(solution)/shard_map/ppermute | solution.py:349
  30.6 3.7 %collective-permute-start.12 = (f32[16,16]{1,0:T(8,128)S(1)}, f32[16,16]{1,0:T(8,128)S(1)}, u32[]{:S(2)}, u32[]{:S(2)}) collective-permute-start(f32[16,16]{1,0:T(8,128)S(1)} %contract.1), channel_id=1, source_target_pairs={{0,2},{1,3},{2,0},{3,1},{4,6},{5,7},{6,4},{7,5},{8,10},{9,11},{10,... | collective-permute-start | bytes 3080 | tf_op jit(solution)/shard_map/ppermute | solution.py:349
  32.1 4.5 %collective-permute-start.13 = (f32[16,16]{1,0:T(8,128)S(1)}, f32[16,16]{1,0:T(8,128)S(1)}, u32[]{:S(2)}, u32[]{:S(2)}) collective-permute-start(f32[16,16]{1,0:T(8,128)S(1)} %contract.1), channel_id=1, source_target_pairs={{0,3},{1,2},{2,1},{3,0},{4,7},{5,6},{6,5},{7,4},{8,11},{9,10},{10,... | collective-permute-start | bytes 3080 | tf_op jit(solution)/shard_map/ppermute | solution.py:349
  33.6 3.7 %collective-permute-start.11 = (f32[16,16]{1,0:T(8,128)S(1)}, f32[16,16]{1,0:T(8,128)S(1)}, u32[]{:S(2)}, u32[]{:S(2)}) collective-permute-start(f32[16,16]{1,0:T(8,128)S(1)} %contract.1), channel_id=1, source_target_pairs={{0,1},{1,0},{2,3},{3,2},{4,5},{5,4},{6,7},{7,6},{8,9},{9,8},{10,11... | collective-permute-start | bytes 3080 | tf_op jit(solution)/shard_map/ppermute | solution.py:349

commit v9 on v8

--- a/solution.py
+++ b/solution.py
@@ -21,6 +21,10 @@
     return ao == 4 and k == 3
 
 
+def crosses(k, ao):
+    return ao == 4 and k in (1, 2)
+
+
 def which(a, k):
     return lax.shift_right_logical(a, jnp.int32(top_bit(k))) & 1
 
@@ -41,11 +45,18 @@
     return ref[:, pl.ds(pl.multiple_of(index * block, block), block)]
 
 
+def pieces(shape):
+    half = shape[-2] // 2
+    halves = [pl.ds(0, half), pl.ds(half, half)]
+    return halves if len(shape) == 2 else [(i, x) for i in range(shape[0]) for x in halves]
+
+
 def prep_kernel(*refs):
     hbm, mask_ref, pay_refs, copied, sems = refs[:5], refs[5], refs[6:-6], refs[-6:-1], refs[-1]
     copies = []
     for i, (src, dst) in enumerate(zip(hbm, copied)):
-        copies.append(pltpu.make_async_copy(src, dst, sems.at[i]))
+        parts = [(src, dst)] if i < 2 else [(src.at[x], dst.at[x]) for x in pieces(src.shape)]
+        copies += [pltpu.make_async_copy(x, y, sems.at[len(copies) + n]) for n, (x, y) in enumerate(parts)]
     for copy in copies:
         copy.start()
     sizes_ref, pattern_ref, slab_ref, occ_ref, virt_ref = copied
@@ -87,7 +98,7 @@
 
     def put(place, k, whole):
         for m in range(1, ao):
-            if m == k:
+            if m == k or crosses(m, ao) and crosses(k, ao):
                 continue
             value, step = whole, block
             if place == 1 and shared(m, ao):
@@ -95,7 +106,7 @@
             at = place * size + ((ao - 2) if k == 0 else k - 1 - (k > m)) * step
             pay_refs[m - 1][at : at + step, :] = value
 
-    tails = []
+    tails, held = [], {}
     for k in range(1, ao + 1):
         k %= ao
         screen = block_at(mask_ref, a ^ k, block)
@@ -112,6 +123,13 @@
                 value = value.astype(bf16)
                 tails.append(diagonal)
             put(place, k, value)
+            if crosses(k, ao):
+                held[place, k] = value
+    if held:
+        for place in range(2):
+            one, two = held[place, 1], held[place, 2]
+            pay_refs[0][place * size : place * size + block, :] = jnp.where(even, two, one)
+            pay_refs[1][place * size : place * size + block, :] = jnp.where(even, one, two)
     upper = lax.broadcasted_iota(jnp.int32, (2 * TAIL, block), 0) < TAIL
     tail = jnp.where(upper, *tails).astype(bf16)
     for ref in pay_refs:
@@ -124,6 +142,10 @@
         return ref[at : at + block, :]
 
     return read
+
+
+def either(chosen, first, second):
+    return lambda k: jnp.where(chosen, first(k), second(k))
 
 
 def halves_reader(mine, other, even, base, m, ao, block):
@@ -174,13 +196,22 @@
     slabs, greens, diagonals = [None], [None], ([None], [None])
     for m, x in enumerate(pays, 1):
         tail = x[x.shape[0] - 2 * TAIL :, :].astype(f32)
+        if crosses(m, ao):
+            other = pays[2 - m]
+            tail = jnp.where(even, tail, other[other.shape[0] - 2 * TAIL :, :].astype(f32))
+            reads = [
+                either(even, reader(x, base, m, ao, block), reader(other, base, m, ao, block)) for base in (0, size)
+            ]
+        elif shared(m, ao):
+            reads = [
+                reader(x, 0, m, ao, block), halves_reader(x, others.pop(0), even, size, m, ao, block)
+            ]
+        else:
+            reads = [reader(x, base, m, ao, block) for base in (0, size)]
+        slabs.append(reads[0])
+        greens.append(reads[1])
         for rows, at in zip(diagonals, (0, TAIL)):
             rows.append(tail[at : at + 1])
-        slabs.append(reader(x, 0, m, ao, block))
-        if shared(m, ao):
-            greens.append(halves_reader(x, others.pop(0), even, size, m, ao, block))
-        else:
-            greens.append(reader(x, size, m, ao, block))
 
     def put_slab(matrix, row, col, value):
         slab_ref[matrix, row * block : (row + 1) * block, col * block : (col + 1) * block] = value
@@ -349,6 +380,11 @@
     return lax.ppermute(value, axis, [(i, i ^ k) for i in range(size)])
 
 
+def crossed(value, ri, ao, k, j):
+    pairs = [(r * ao + a, r * ao + (a ^ (j if r % 2 else k))) for r in range(ri) for a in range(ao)]
+    return lax.ppermute(value, ("ri", "ao"), pairs)
+
+
 def along(value, targets):
     pairs = []
     for source, target in enumerate(targets):
@@ -395,14 +431,14 @@
         in_specs=[pl.BlockSpec(memory_space=pltpu.HBM)] * 5,
         out_specs=[vmem] * (1 + len(sizes)),
         scratch_shapes=[pltpu.VMEM(x.shape, x.dtype) for x in inputs]
-        + [pltpu.SemaphoreType.DMA((len(inputs),))],
+        + [pltpu.SemaphoreType.DMA((2 + sum(len(pieces(x.shape)) for x in inputs[2:]),))],
         compiler_params=room((sum(sizes), block), (5 * block, total), (2 * block, 2 * total)),
         name="prep",
     )(*inputs)
     mask, *pays = prepared
     arrived = []
     for k, pay in enumerate(pays, 1):
-        arrived.append(exchange(pay, "ao", ao, k))
+        arrived.append(crossed(pay, ri, ao, k, 3 - k) if crosses(k, ao) else exchange(pay, "ao", ao, k))
     pays = arrived + [exchange(x, "ri", ri, 1) for k, x in enumerate(arrived, 1) if shared(k, ao)]
     groups = block // TILE
     rows = ri_rows * TILE

time: 38 us -> 38.2 us (level)
  waiting for transfers between devices: 12.6 us -> 14.7 us
  starting transfers between devices: 18.9 us -> 16.8 us
    ppermute x4, waiting for transfers between devices: 2.8 us -> 4.87 us  [along(): return lax.ppermute(value, 'ri', pairs)]
    ppermute x4, starting transfers between devices: 10.4 us -> 8.61 us  [along(): return lax.ppermute(value, 'ri', pairs)]
    ppermute x0 -> x2, waiting for transfers between devices: none -> 1.47 us  [crossed(): return lax.ppermute(value, ('ri', 'ao'), pairs)]
    ppermute x10 -> x8, waiting for transfers between devices: 9.81 us -> 8.36 us  [exchange(): return lax.ppermute(value, axis, [(i, i ^ k) for i in range(size)])]
    ppermute x10 -> x8, starting transfers between devices: 8.45 us -> 7.57 us  [exchange(): return lax.ppermute(value, axis, [(i, i ^ k) for i in range(size)])]
    ppermute x0 -> x2, starting transfers between devices: none -> 0.64 us  [crossed(): return lax.ppermute(value, ('ri', 'ao'), pairs)]
where the time goes in v9:
time: 38.2 us; the launch traced here: 38 us
  starting transfers between devices  16.8 us (44%)
  waiting for transfers between devices  14.7 us (38%)
  Pallas kernels  5.66 us (15%)
  other arithmetic  0.7 us (2%)
    ppermute x4, starting transfers between devices, along(): return lax.ppermute(value, 'ri', pairs)  8.61 us
    ppermute x8, waiting for transfers between devices, exchange(): return lax.ppermute(value, axis, [(i, i ^ k) for i in range(size)])  8.36 us
    ppermute x8, starting transfers between devices, exchange(): return lax.ppermute(value, axis, [(i, i ^ k) for i in range(size)])  7.57 us
    ppermute x4, waiting for transfers between devices, along(): return lax.ppermute(value, 'ri', pairs)  4.87 us
    pallas_call x1, Pallas kernels, shards(): pl.pallas_call(stage_kernel, out_shape=[jax.ShapeDtypeStruct((ao, groups...  2.51 us
    ppermute x2, waiting for transfers between devices, crossed(): return lax.ppermute(value, ('ri', 'ao'), pairs)  1.47 us
    pallas_call x1, Pallas kernels, shards(): pl.pallas_call(prep_kernel, out_shape=[jax.ShapeDtypeStruct((block, total...  1.31 us
    pallas_call x1, Pallas kernels, shards(): pl.pallas_call(lambda *refs: transform_kernel(ao, block, *refs), out_shap...  1.04 us
  transfers between devices with their start and end apart: 14, of which 8 were waited for; matrix products, arithmetic and copies ran while one was open for 0% of the time, Pallas kernels for 7%

profile of v9, /device:TPU:0, one launch (start us, length us, event | category | flops | bytes accessed | tf_op | source)
XLA Modules:
  0.0 38.0 jit_solution(250772995320170398)
XLA Ops:
  0.0 1.3 %prep.1 = (bf16[128,512]{1,0:T(8,128)(2,1)S(1)}, bf16[784,128]{1,0:T(8,128)(2,1)S(1)}, bf16[784,128]{1,0:T(8,128)(2,1)S(1)}, bf16[592,128]{1,0:T(8,128)(2,1)S(1)}) custom-call(s32[1,32]{1,0:T(1,128)} %bitcast.1, s32[32,32]{1,0:T(8,128)} %refs_1_.1, bf16[2,128,512]{2,1,0:T(8,128)(2,1)} %slab_hbm.1, bf16[128,512]{1,0:T(8,128)(2,1)} %occ_hbm.1, ...), custom_call_target="tpu_custom_call" | custom-call | tf_op jit(solution)/shard_map/prep/pallas_call | solution.py:427
  1.3 4.0 %collective-permute-start.2 = (bf16[592,128]{1,0:T(8,128)(2,1)S(1)}, bf16[592,128]{1,0:T(8,128)(2,1)S(1)}, u32[]{:S(2)}, u32[]{:S(2)}) collective-permute-start(bf16[592,128]{1,0:T(8,128)(2,1)S(1)} %get-tuple-element.16), channel_id=1, source_target_pairs={{0,3},{1,2},{2,1},{3,0},{4,7},{5,6},{6,5},{7,4},{8,11},{9,10},{10,... | collective-permute-start | bytes 454664 | tf_op jit(solution)/shard_map/ppermute | solution.py:380
  5.3 0.5 %collective-permute-start = (bf16[784,128]{1,0:T(8,128)(2,1)S(1)}, bf16[784,128]{1,0:T(8,128)(2,1)S(1)}, u32[]{:S(2)}, u32[]{:S(2)}) collective-permute-start(bf16[784,128]{1,0:T(8,128)(2,1)S(1)} %get-tuple-element.14), channel_id=1, source_target_pairs={{0,1},{1,0},{2,3},{3,2},{4,6},{5,7},{6,4},{7,5},{8,9},{9,8},{10,11... | collective-permute-start | bytes 602120 | tf_op jit(solution)/shard_map/ppermute | solution.py:385
  5.8 0.1 collective-permute-start.1
  5.9 3.9 %collective-permute-done.2.refs_2_ = bf16[592,128]{1,0:T(8,128)(2,1)S(1)} collective-permute-done((bf16[592,128]{1,0:T(8,128)(2,1)S(1)}, bf16[592,128]{1,0:T(8,128)(2,1)S(1)}, u32[]{:S(2)}, u32[]{:S(2)}) %collective-permute-start.2) | collective-permute-done | bytes 151584 | tf_op jit(solution)/shard_map/ppermute | solution.py:380
  9.8 0.0 collective-permute-start.3
  9.8 2.5 %stage.1 = (bf16[4,1024,256]{2,1,0:T(8,128)(2,1)S(1)}, bf16[4,128,512]{2,1,0:T(8,128)(2,1)S(1)}, bf16[128,512]{1,0:T(8,128)(2,1)S(1)}) custom-call(bf16[16,128,512]{2,1,0:T(8,128)(2,1)} %tensor_hbm.1, bf16[2,128,512]{2,1,0:T(8,128)(2,1)} %slab_hbm.1, bf16[128,512]{1,0:T(8,128)(2,1)} %occ_hbm.1, bf16[128,512]{1,0:T(8,128)(2,1)} %virt_hbm.1, ...), custom_call_target="tpu_custom_call" | custom-call | bytes 8388608 | tf_op jit(solution)/shard_map/stage/pallas_call | solution.py:445
  12.4 1.5 %collective-permute-done.refs_0_ = bf16[784,128]{1,0:T(8,128)(2,1)S(1)} collective-permute-done((bf16[784,128]{1,0:T(8,128)(2,1)S(1)}, bf16[784,128]{1,0:T(8,128)(2,1)S(1)}, u32[]{:S(2)}, u32[]{:S(2)}) %collective-permute-start) | collective-permute-done | bytes 200736 | tf_op jit(solution)/shard_map/ppermute | solution.py:385
  13.8 0.0 collective-permute-done.1.refs_1_
  13.8 0.0 collective-permute-done.3.refs_3_
  13.8 1.0 %transform.1.refs_0_ = bf16[520,128]{1,0:T(8,128)(2,1)S(1)} custom-call(bf16[784,128]{1,0:T(8,128)(2,1)S(1)} %collective-permute-done.refs_0_, bf16[784,128]{1,0:T(8,128)(2,1)S(1)} %collective-permute-done.1.refs_1_, bf16[592,128]{1,0:T(8,128)(2,1)S(1)} %collective-permute-done.2.refs_2_, bf16[592,128]{1,0:T(8,128)(2,1)S(1)} %collective-permute-done.3.refs_3_, ...), custom_call_target="tpu_custom_call" | custom-call | tf_op jit(solution)/shard_map/transform/pallas_call | solution.py:460
  14.9 0.1 collective-permute-start.5
  15.0 3.7 %collective-permute-start.4 = (bf16[520,128]{1,0:T(8,128)(2,1)S(1)}, bf16[520,128]{1,0:T(8,128)(2,1)S(1)}, u32[]{:S(2)}, u32[]{:S(2)}) collective-permute-start(bf16[520,128]{1,0:T(8,128)(2,1)S(1)} %transform.1.refs_0_), channel_id=1, source_target_pairs={{0,24},{4,28},{8,12},{12,8},{16,20},{20,16},{24,0},{28,4},{1,25},{... | collective-permute-start | bytes 399368 | tf_op jit(solution)/shard_map/ppermute | solution.py:394
  18.6 0.0 collective-permute-start.6
  18.6 0.0 collective-permute-done.5
  18.7 4.9 %collective-permute-start.8 = (bf16[520,128]{1,0:T(8,128)(2,1)S(1)}, bf16[520,128]{1,0:T(8,128)(2,1)S(1)}, u32[]{:S(2)}, u32[]{:S(2)}) collective-permute-start(bf16[520,128]{1,0:T(8,128)(2,1)S(1)} %broadcast_select_fusion.2), channel_id=1, source_target_pairs={{0,16},{4,20},{8,0},{12,4},{16,24},{20,28},{24,8},{28,12},{1,17},{... | collective-permute-start | bytes 399368 | tf_op jit(solution)/shard_map/ppermute | solution.py:394
  23.6 0.0 collective-permute-done.4
  23.6 0.1 broadcast_select_fusion
  23.6 0.1 collective-permute-start.10
  23.7 2.1 %collective-permute-done.6.refs_2_ = bf16[520,128]{1,0:T(8,128)(2,1)S(1)} collective-permute-done((bf16[520,128]{1,0:T(8,128)(2,1)S(1)}, bf16[520,128]{1,0:T(8,128)(2,1)S(1)}, u32[]{:S(2)}, u32[]{:S(2)}) %collective-permute-start.6) | collective-permute-done | bytes 133152 | tf_op jit(solution)/shard_map/ppermute | solution.py:394
  25.8 0.0 collective-permute-start.7
  25.8 2.8 %collective-permute-done.8.refs_4_ = bf16[520,128]{1,0:T(8,128)(2,1)S(1)} collective-permute-done((bf16[520,128]{1,0:T(8,128)(2,1)S(1)}, bf16[520,128]{1,0:T(8,128)(2,1)S(1)}, u32[]{:S(2)}, u32[]{:S(2)}) %collective-permute-start.8) | collective-permute-done | bytes 133152 | tf_op jit(solution)/shard_map/ppermute | solution.py:394
  28.6 0.0 collective-permute-start.9
  28.6 0.0 collective-permute-done.7.refs_3_
  28.6 0.0 collective-permute-done.10.refs_7_
  28.6 1.3 %collective-permute-done.9.refs_5_ = bf16[520,128]{1,0:T(8,128)(2,1)S(1)} collective-permute-done((bf16[520,128]{1,0:T(8,128)(2,1)S(1)}, bf16[520,128]{1,0:T(8,128)(2,1)S(1)}, u32[]{:S(2)}, u32[]{:S(2)}) %collective-permute-start.9) | collective-permute-done | bytes 133152 | tf_op jit(solution)/shard_map/ppermute | solution.py:380
  29.9 0.8 %contract.1 = f32[16,16]{1,0:T(8,128)S(1)} custom-call(bf16[520,128]{1,0:T(8,128)(2,1)S(1)} %transform.1.refs_0_, bf16[520,128]{1,0:T(8,128)(2,1)S(1)} %get-tuple-element.24.refs_1_, bf16[520,128]{1,0:T(8,128)(2,1)S(1)} %collective-permute-done.6.refs_2_, bf16[520,128]{1,0:T(8,128)(2,1)S(1)} %collective-permute-done.7.refs_3_, ...), custom_call_target="tpu_custom_call" | custom-call | tf_op jit(solution)/shard_map/contract/pallas_call | solution.py:474
  30.7 1.4 %collective-permute-start.12 = (f32[16,16]{1,0:T(8,128)S(1)}, f32[16,16]{1,0:T(8,128)S(1)}, u32[]{:S(2)}, u32[]{:S(2)}) collective-permute-start(f32[16,16]{1,0:T(8,128)S(1)} %contract.1), channel_id=1, source_target_pairs={{0,2},{1,3},{2,0},{3,1},{4,6},{5,7},{6,4},{7,5},{8,10},{9,11},{10,... | collective-permute-start | bytes 3080 | tf_op jit(solution)/shard_map/ppermute | solution.py:380
  32.2 1.5 %collective-permute-start.13 = (f32[16,16]{1,0:T(8,128)S(1)}, f32[16,16]{1,0:T(8,128)S(1)}, u32[]{:S(2)}, u32[]{:S(2)}) collective-permute-start(f32[16,16]{1,0:T(8,128)S(1)} %contract.1), channel_id=1, source_target_pairs={{0,3},{1,2},{2,1},{3,0},{4,7},{5,6},{6,5},{7,4},{8,11},{9,10},{10,... | collective-permute-start | bytes 3080 | tf_op jit(solution)/shard_map/ppermute | solution.py:380
  33.7 0.5 %collective-permute-start.11 = (f32[16,16]{1,0:T(8,128)S(1)}, f32[16,16]{1,0:T(8,128)S(1)}, u32[]{:S(2)}, u32[]{:S(2)}) collective-permute-start(f32[16,16]{1,0:T(8,128)S(1)} %contract.1), channel_id=1, source_target_pairs={{0,1},{1,0},{2,3},{3,2},{4,5},{5,4},{6,7},{7,6},{8,9},{9,8},{10,11... | collective-permute-start | bytes 3080 | tf_op jit(solution)/shard_map/ppermute | solution.py:380
  34.2 0.2 collective-permute-done.12
  34.4 2.3 %collective-permute-done.13 = f32[16,16]{1,0:T(8,128)S(1)} collective-permute-done((f32[16,16]{1,0:T(8,128)S(1)}, f32[16,16]{1,0:T(8,128)S(1)}, u32[]{:S(2)}, u32[]{:S(2)}) %collective-permute-start.13) | collective-permute-done | bytes 1056 | tf_op jit(solution)/shard_map/ppermute | solution.py:380
  36.7 0.6 %collective-permute-done.11 = f32[16,16]{1,0:T(8,128)S(1)} collective-permute-done((f32[16,16]{1,0:T(8,128)S(1)}, f32[16,16]{1,0:T(8,128)S(1)}, u32[]{:S(2)}, u32[]{:S(2)}) %collective-permute-start.11) | collective-permute-done | bytes 1056 | tf_op jit(solution)/shard_map/ppermute | solution.py:380
  37.4 0.6 %add_add_fusion = f32[16,16]{1,0:T(8,128)} fusion(f32[16,16]{1,0:T(8,128)S(1)} %collective-permute-done.12, f32[16,16]{1,0:T(8,128)S(1)} %collective-permute-done.13, f32[16,16]{1,0:T(8,128)S(1)} %contract.1, f32[16,16]{1,0:T(8,128)S(1)} %collective-permute-done.11), kind=kLoop, calls=%fused_computation.3 | loop fusion | flops 768 | bytes 5120 | tf_op jit(solution)/shard_map/add | solution.py:484
  (1 shorter events, 0.0 us)
Async XLA Ops:
  1.3 8.5 %collective-permute-start.2 = (bf16[592,128]{1,0:T(8,128)(2,1)S(1)}, bf16[592,128]{1,0:T(8,128)(2,1)S(1)}, u32[]{:S(2)}, u32[]{:S(2)}) collective-permute-start(bf16[592,128]{1,0:T(8,128)(2,1)S(1)} %get-tuple-element.16), channel_id=1, source_target_pairs={{0,3},{1,2},{2,1},{3,0},{4,7},{5,6},{6,5},{7,4},{8,11},{9,10},{10,... | collective-permute-start | bytes 454664 | tf_op jit(solution)/shard_map/ppermute | solution.py:380
  5.3 8.5 %collective-permute-start = (bf16[784,128]{1,0:T(8,128)(2,1)S(1)}, bf16[784,128]{1,0:T(8,128)(2,1)S(1)}, u32[]{:S(2)}, u32[]{:S(2)}) collective-permute-start(bf16[784,128]{1,0:T(8,128)(2,1)S(1)} %get-tuple-element.14), channel_id=1, source_target_pairs={{0,1},{1,0},{2,3},{3,2},{4,6},{5,7},{6,4},{7,5},{8,9},{9,8},{10,11... | collective-permute-start | bytes 602120 | tf_op jit(solution)/shard_map/ppermute | solution.py:385
  5.8 8.0 %collective-permute-start.1 = (bf16[784,128]{1,0:T(8,128)(2,1)S(1)}, bf16[784,128]{1,0:T(8,128)(2,1)S(1)}, u32[]{:S(2)}, u32[]{:S(2)}) collective-permute-start(bf16[784,128]{1,0:T(8,128)(2,1)S(1)} %get-tuple-element.15), channel_id=1, source_target_pairs={{0,2},{1,3},{2,0},{3,1},{4,5},{5,4},{6,7},{7,6},{8,10},{9,11},{10,... | collective-permute-start | bytes 602120 | tf_op jit(solution)/shard_map/ppermute | solution.py:385
  9.8 4.0 %collective-permute-start.3 = (bf16[592,128]{1,0:T(8,128)(2,1)S(1)}, bf16[592,128]{1,0:T(8,128)(2,1)S(1)}, u32[]{:S(2)}, u32[]{:S(2)}) collective-permute-start(bf16[592,128]{1,0:T(8,128)(2,1)S(1)} %collective-permute-done.2.refs_2_), channel_id=1, source_target_pairs={{0,4},{4,0},{8,12},{12,8},{16,20},{20,16},{24,28},{28,24},{1,5},{5... | collective-permute-start | bytes 454664 | tf_op jit(solution)/shard_map/ppermute | solution.py:380
  14.9 3.8 %collective-permute-start.5 = (bf16[520,128]{1,0:T(8,128)(2,1)S(1)}, bf16[520,128]{1,0:T(8,128)(2,1)S(1)}, u32[]{:S(2)}, u32[]{:S(2)}) collective-permute-start(bf16[520,128]{1,0:T(8,128)(2,1)S(1)} %transform.1.refs_0_), channel_id=1, source_target_pairs={{0,4},{4,0},{8,16},{12,20},{16,8},{20,12},{24,28},{28,24},{1,5},{5... | collective-permute-start | bytes 399368 | tf_op jit(solution)/shard_map/ppermute | solution.py:394
  15.0 8.6 %collective-permute-start.4 = (bf16[520,128]{1,0:T(8,128)(2,1)S(1)}, bf16[520,128]{1,0:T(8,128)(2,1)S(1)}, u32[]{:S(2)}, u32[]{:S(2)}) collective-permute-start(bf16[520,128]{1,0:T(8,128)(2,1)S(1)} %transform.1.refs_0_), channel_id=1, source_target_pairs={{0,24},{4,28},{8,12},{12,8},{16,20},{20,16},{24,0},{28,4},{1,25},{... | collective-permute-start | bytes 399368 | tf_op jit(solution)/shard_map/ppermute | solution.py:394
  18.6 7.2 %collective-permute-start.6 = (bf16[520,128]{1,0:T(8,128)(2,1)S(1)}, bf16[520,128]{1,0:T(8,128)(2,1)S(1)}, u32[]{:S(2)}, u32[]{:S(2)}) collective-permute-start(bf16[520,128]{1,0:T(8,128)(2,1)S(1)} %transform.1.refs_0_), channel_id=1, source_target_pairs={{0,8},{4,12},{8,0},{12,4},{16,24},{20,28},{24,16},{28,20},{1,9},{5... | collective-permute-start | bytes 399368 | tf_op jit(solution)/shard_map/ppermute | solution.py:394
  18.7 9.9 %collective-permute-start.8 = (bf16[520,128]{1,0:T(8,128)(2,1)S(1)}, bf16[520,128]{1,0:T(8,128)(2,1)S(1)}, u32[]{:S(2)}, u32[]{:S(2)}) collective-permute-start(bf16[520,128]{1,0:T(8,128)(2,1)S(1)} %broadcast_select_fusion.2), channel_id=1, source_target_pairs={{0,16},{4,20},{8,0},{12,4},{16,24},{20,28},{24,8},{28,12},{1,17},{... | collective-permute-start | bytes 399368 | tf_op jit(solution)/shard_map/ppermute | solution.py:394
  23.6 5.0 %collective-permute-start.10 = (bf16[520,128]{1,0:T(8,128)(2,1)S(1)}, bf16[520,128]{1,0:T(8,128)(2,1)S(1)}, u32[]{:S(2)}, u32[]{:S(2)}) collective-permute-start(bf16[520,128]{1,0:T(8,128)(2,1)S(1)} %get-tuple-element.23.refs_6_), channel_id=1, source_target_pairs={{0,4},{4,0},{8,12},{12,8},{16,20},{20,16},{24,28},{28,24},{1,5},{5... | collective-permute-start | bytes 399368 | tf_op jit(solution)/shard_map/ppermute | solution.py:380
  25.8 2.8 %collective-permute-start.7 = (bf16[520,128]{1,0:T(8,128)(2,1)S(1)}, bf16[520,128]{1,0:T(8,128)(2,1)S(1)}, u32[]{:S(2)}, u32[]{:S(2)}) collective-permute-start(bf16[520,128]{1,0:T(8,128)(2,1)S(1)} %collective-permute-done.6.refs_2_), channel_id=1, source_target_pairs={{0,4},{4,0},{8,12},{12,8},{16,20},{20,16},{24,28},{28,24},{1,5},{5... | collective-permute-start | bytes 399368 | tf_op jit(solution)/shard_map/ppermute | solution.py:380
  28.6 1.4 %collective-permute-start.9 = (bf16[520,128]{1,0:T(8,128)(2,1)S(1)}, bf16[520,128]{1,0:T(8,128)(2,1)S(1)}, u32[]{:S(2)}, u32[]{:S(2)}) collective-permute-start(bf16[520,128]{1,0:T(8,128)(2,1)S(1)} %collective-permute-done.8.refs_4_), channel_id=1, source_target_pairs={{0,4},{4,0},{8,12},{12,8},{16,20},{20,16},{24,28},{28,24},{1,5},{5... | collective-permute-start | bytes 399368 | tf_op jit(solution)/shard_map/ppermute | solution.py:380
  30.7 3.7 %collective-permute-start.12 = (f32[16,16]{1,0:T(8,128)S(1)}, f32[16,16]{1,0:T(8,128)S(1)}, u32[]{:S(2)}, u32[]{:S(2)}) collective-permute-start(f32[16,16]{1,0:T(8,128)S(1)} %contract.1), channel_id=1, source_target_pairs={{0,2},{1,3},{2,0},{3,1},{4,6},{5,7},{6,4},{7,5},{8,10},{9,11},{10,... | collective-permute-start | bytes 3080 | tf_op jit(solution)/shard_map/ppermute | solution.py:380
  32.2 4.5 %collective-permute-start.13 = (f32[16,16]{1,0:T(8,128)S(1)}, f32[16,16]{1,0:T(8,128)S(1)}, u32[]{:S(2)}, u32[]{:S(2)}) collective-permute-start(f32[16,16]{1,0:T(8,128)S(1)} %contract.1), channel_id=1, source_target_pairs={{0,3},{1,2},{2,1},{3,0},{4,7},{5,6},{6,5},{7,4},{8,11},{9,10},{10,... | collective-permute-start | bytes 3080 | tf_op jit(solution)/shard_map/ppermute | solution.py:380
  33.7 3.7 %collective-permute-start.11 = (f32[16,16]{1,0:T(8,128)S(1)}, f32[16,16]{1,0:T(8,128)S(1)}, u32[]{:S(2)}, u32[]{:S(2)}) collective-permute-start(f32[16,16]{1,0:T(8,128)S(1)} %contract.1), channel_id=1, source_target_pairs={{0,1},{1,0},{2,3},{3,2},{4,5},{5,4},{6,7},{7,6},{8,9},{9,8},{10,11... | collective-permute-start | bytes 3080 | tf_op jit(solution)/shard_map/ppermute | solution.py:380
